TPU v7x, 32 devices: a whole 2x2x4 slice. The times are simulated.
32 devices in a mesh: seq: 2 (over x), fsdp: 16 (over z, y, core).
Axes of the slice: x: 2, y: 2, z: 4, core: 2. Of those that a mesh axis runs over, the one named last changes fastest.
Arguments:
- tokens: bfloat16 [16, 1024, 1024], P('fsdp', 'seq'), may hold values from -6 to 6
- cotangent: bfloat16 [16, 1024, 1024], P('fsdp', 'seq'), may hold values from -6 to 6
- ffn1_up: float32 [1024, 4096], P('fsdp'), may hold values from -0.1875 to 0.1875
- ffn1_down: float32 [4096, 1024], P('fsdp'), may hold values from -0.09375 to 0.09375
- qkv_weight: float32 [1024, 3072], P('fsdp'), may hold values from -0.1875 to 0.1875
- out_weight: float32 [1024, 1024], P('fsdp'), may hold values from -3 to 3
- conv_in: float32 [1024, 2048], P('fsdp'), may hold values from -0.1875 to 0.1875
- conv_out: float32 [1024, 1024], P('fsdp'), may hold values from -0.1875 to 0.1875
- ffn2_up: float32 [1024, 4096], P('fsdp'), may hold values from -0.1875 to 0.1875
- ffn2_down: float32 [4096, 1024], P('fsdp'), may hold values from -0.09375 to 0.09375
- norm_gains: float32 [6, 1024], replicated, may hold values from 0.5 to 1.5
- norm_biases: float32 [6, 1024], replicated, may hold values from -1 to 1
- hidden_biases: float32 [2, 4096], replicated, may hold values from -1.5 to 1.5
- model_biases: float32 [5, 1024], replicated, may hold values from -1.5 to 1.5
- dw_kernel: float32 [31, 1024], replicated, may hold values from -1 to 1
- rel_table: float32 [73, 64], replicated, may hold values from -6 to 6
Outputs:
- output: bfloat16 [16, 1024, 1024], P('fsdp', 'seq')
- input_grad: bfloat16 [16, 1024, 1024], P('fsdp', 'seq')
- ffn1_up_grad: float32 [1024, 4096], P('fsdp', 'seq')
- ffn1_down_grad: float32 [4096, 1024], P('fsdp', 'seq')
- qkv_grad: float32 [1024, 3072], P('fsdp', 'seq')
- out_grad: float32 [1024, 1024], P('fsdp', 'seq')
- conv_in_grad: float32 [1024, 2048], P('fsdp', 'seq')
- conv_out_grad: float32 [1024, 1024], P('fsdp', 'seq')
- ffn2_up_grad: float32 [1024, 4096], P('fsdp', 'seq')
- ffn2_down_grad: float32 [4096, 1024], P('fsdp', 'seq')
- gains_grad: float32 [6, 1024], replicated
- norm_biases_grad: float32 [3, 1024], replicated
- later_biases_grad: float32 [3, 1024], replicated
- hidden_biases_grad: float32 [2, 4096], replicated
- model_biases_grad: float32 [3, 1024], replicated
- output_biases_grad: float32 [2, 1024], replicated
- kernel_grad: float32 [31, 1024], replicated
- table_grad: float32 [73, 64], replicated
All inputs are finite; a program needn't handle non-finite values.
Results may differ from a plain program's by a relative error of at most 0.02.
Values may be sent and summed in bfloat16 or wider, within the bound.
A program may use at most 256 MiB of HBM per device.

v0:
```python
from functools import partial

import jax
import jax.numpy as jnp
from jax import lax
from jax.sharding import PartitionSpec as P

HEAD = 64
KERNEL = 31
LEFT = 64
RIGHT = 8
BUCKETS = 73


EPSILON = 1e-05


def passed_along(value, axis, by):
    length = lax.axis_size(axis)
    pairs = [(i, i + by) for i in range(length) if 0 <= i + by < length]
    return lax.ppermute(value, axis, pairs)


def layer_norm(values, norm_gain, norm_shift):
    center = values - jnp.mean(values, axis=-1, keepdims=True)
    spread = jnp.mean(center * center, axis=-1, keepdims=True)
    return center * lax.rsqrt(spread + EPSILON) * norm_gain + norm_shift


def product(former, latter):
    return jnp.dot(former, latter, preferred_element_type=jnp.float32)


def contract_rows(former, latter):
    return lax.dot_general(
        former, latter, (((0,), (0,)), ((), ())), preferred_element_type=jnp.float32
    )


def times_transposed(former, latter):
    return lax.dot_general(
        former, latter, (((1,), (1,)), ((), ())), preferred_element_type=jnp.float32
    )


def glu_function(gate_input):
    half_width = gate_input.shape[1] // 2
    return gate_input[:, :half_width] * jax.nn.sigmoid(gate_input[:, half_width:])


def conv_tail(mixed_rows, norm_gain, norm_shift):
    return jax.nn.silu(layer_norm(mixed_rows, norm_gain, norm_shift))


def depthwise(wide_rows, kernel_now):
    return lax.conv_general_dilated(
        wide_rows,
        kernel_now[:, None, :],
        (1,),
        "VALID",
        dimension_numbers=("NWC", "WIO", "NWC"),
        feature_group_count=wide_rows.shape[2],
        precision=lax.Precision.HIGHEST,
    )


def relative_grid(length):
    row_places = lax.broadcasted_iota(jnp.int32, (length, length), 0)
    col_places = lax.broadcasted_iota(jnp.int32, (length, length), 1)
    return col_places - row_places


def spread_band(position, length):
    row_width = length + BUCKETS
    padded = jnp.pad(position, ((0, 0), (0, row_width + 1 - BUCKETS)))
    skewed = padded.reshape(length * (row_width + 1))[: length * row_width].reshape(
        length, row_width
    )
    band_part = skewed[:, LEFT : LEFT + length]
    relative = relative_grid(length)
    return jnp.where(
        relative <= -LEFT,
        position[:, 0:1],
        jnp.where(relative >= RIGHT, position[:, BUCKETS - 1 : BUCKETS], band_part),
    )


def collect_band(score_wide, length):
    row_width = length + BUCKETS
    relative = relative_grid(length)
    inside = jnp.where((relative > -LEFT) & (relative < RIGHT), score_wide, 0.0)
    first_bucket = jnp.sum(jnp.where(relative <= -LEFT, score_wide, 0.0), axis=1, keepdims=True)
    last_bucket = jnp.sum(jnp.where(relative >= RIGHT, score_wide, 0.0), axis=1, keepdims=True)
    widened = jnp.pad(inside, ((0, 0), (LEFT, RIGHT + 1)))
    flat_rows = jnp.pad(widened.reshape(length * row_width), (0, length))
    unskewed = flat_rows.reshape(length, row_width + 1)[:, 1 : BUCKETS - 1]
    return jnp.concatenate([first_bucket, unskewed, last_bucket], axis=1)


def feed_forward(values, norm_gain, norm_shift, weight_up, bias_up, weight_down, bias_down):
    normed = layer_norm(values, norm_gain, norm_shift).astype(jnp.bfloat16)
    hidden = product(normed, weight_up) + bias_up
    active = jax.nn.silu(hidden).astype(jnp.bfloat16)
    branch = product(active, weight_down) + bias_down
    return (branch, (normed, hidden, active))


def feed_backward(residual_grad, values, kept_parts, norm_gain, norm_shift, weight_up, weight_down):
    normed, hidden, active = kept_parts
    branch_grad = (0.5 * residual_grad).astype(jnp.bfloat16)
    down_grad = contract_rows(active, branch_grad)
    down_bias_grad = jnp.sum(branch_grad.astype(jnp.float32), axis=0)
    active_grad = times_transposed(branch_grad, weight_down)
    silu_pull = jax.vjp(jax.nn.silu, hidden)[1]
    hidden_grad = silu_pull(active_grad)[0].astype(jnp.bfloat16)
    up_grad = contract_rows(normed, hidden_grad)
    up_bias_grad = jnp.sum(hidden_grad.astype(jnp.float32), axis=0)
    normed_grad = times_transposed(hidden_grad, weight_up)
    norm_pull = jax.vjp(layer_norm, values, norm_gain, norm_shift)[1]
    values_grad, gain_grad, shift_grad = norm_pull(normed_grad)
    return (
        residual_grad + values_grad,
        up_grad,
        up_bias_grad,
        down_grad,
        down_bias_grad,
        gain_grad,
        shift_grad,
    )


def split_heads(array, clip_count, length, head_count):
    shaped = array.reshape(clip_count, length, head_count, HEAD).transpose(0, 2, 1, 3)
    return shaped.reshape(clip_count * head_count, length, HEAD)


def merge_heads(array, clip_count, length, head_count):
    shaped = array.reshape(clip_count, head_count, length, HEAD).transpose(0, 2, 1, 3)
    return shaped.reshape(clip_count, length, head_count * HEAD)


def body(
    tokens,
    cotangent,
    ffn1_up,
    ffn1_down,
    qkv_weight,
    out_weight,
    conv_in,
    conv_out,
    ffn2_up,
    ffn2_down,
    norm_gains,
    norm_biases,
    hidden_biases,
    model_biases,
    dw_kernel,
    rel_table,
):
    clip_count, segment, model_width = tokens.shape
    row_count = clip_count * segment
    groups = lax.axis_size("seq")
    length = segment * groups
    head_count = model_width // groups // HEAD
    rim_width = KERNEL - 1
    score_scale = HEAD ** (-0.5)
    up_one, down_one, qkv_full, out_full, conv_first, conv_second, up_two, down_two = (
        lax.all_gather(ffn1_up.astype(jnp.bfloat16), "fsdp", axis=0, tiled=True),
        lax.all_gather(ffn1_down.astype(jnp.bfloat16), "fsdp", axis=0, tiled=True),
        lax.all_gather(qkv_weight.astype(jnp.bfloat16), "fsdp", axis=0, tiled=True),
        lax.all_gather(out_weight.astype(jnp.bfloat16), "fsdp", axis=0, tiled=True),
        lax.all_gather(conv_in.astype(jnp.bfloat16), "fsdp", axis=0, tiled=True),
        lax.all_gather(conv_out.astype(jnp.bfloat16), "fsdp", axis=0, tiled=True),
        lax.all_gather(ffn2_up.astype(jnp.bfloat16), "fsdp", axis=0, tiled=True),
        lax.all_gather(ffn2_down.astype(jnp.bfloat16), "fsdp", axis=0, tiled=True),
    )
    input_rows = tokens.reshape(row_count, model_width).astype(jnp.float32)
    branch_one, kept_one = feed_forward(
        input_rows,
        norm_gains[0],
        norm_biases[0],
        up_one,
        hidden_biases[0],
        down_one,
        model_biases[0],
    )
    after_one = input_rows + 0.5 * branch_one
    normed_attn = layer_norm(after_one, norm_gains[1], norm_biases[1]).astype(jnp.bfloat16)
    projected = product(normed_attn, qkv_full)
    queries = (
        (projected[:, :model_width] + model_biases[1])
        .astype(jnp.bfloat16)
        .reshape(clip_count, segment, model_width)
    )
    keys_seq = (
        projected[:, model_width : 2 * model_width]
        .astype(jnp.bfloat16)
        .reshape(clip_count, segment, model_width)
    )
    values_seq = (
        (projected[:, 2 * model_width :] + model_biases[2])
        .astype(jnp.bfloat16)
        .reshape(clip_count, segment, model_width)
    )
    query_heads, key_heads, value_heads = (
        lax.all_to_all(queries, "seq", split_axis=2, concat_axis=1, tiled=True),
        lax.all_to_all(keys_seq, "seq", split_axis=2, concat_axis=1, tiled=True),
        lax.all_to_all(values_seq, "seq", split_axis=2, concat_axis=1, tiled=True),
    )
    query_items = split_heads(query_heads, clip_count, length, head_count)
    key_items = split_heads(key_heads, clip_count, length, head_count)
    value_items = split_heads(value_heads, clip_count, length, head_count)
    rel_low = rel_table.astype(jnp.bfloat16)
    rel_wide = rel_low.astype(jnp.float32)

    def head_scores(query_head, key_head):
        direct = times_transposed(query_head, key_head)
        position = times_transposed(query_head, rel_low)
        return (direct + spread_band(position, length)) * score_scale

    def attend(operands):
        query_head, key_head, value_head = operands
        scores = head_scores(query_head, key_head)
        highest = jnp.max(scores, axis=-1, keepdims=True)
        weights_exp = jnp.exp(scores - highest)
        row_total = jnp.sum(weights_exp, axis=-1, keepdims=True)
        weights_soft = (weights_exp / row_total).astype(jnp.bfloat16)
        head_out = product(weights_soft, value_head).astype(jnp.bfloat16)
        return (head_out, highest[:, 0] + jnp.log(row_total[:, 0]))

    head_outputs, log_totals = lax.map(attend, (query_items, key_items, value_items))
    merged = merge_heads(head_outputs, clip_count, length, head_count)
    attn_seq = lax.all_to_all(merged, "seq", split_axis=1, concat_axis=2, tiled=True)
    attn_rows = attn_seq.reshape(row_count, model_width)
    after_two = after_one + product(attn_rows, out_full) + model_biases[3]
    normed_conv = layer_norm(after_two, norm_gains[2], norm_biases[2]).astype(jnp.bfloat16)
    gate_input = product(normed_conv, conv_first)
    glu_out = (
        glu_function(gate_input).astype(jnp.bfloat16).reshape(clip_count, segment, model_width)
    )
    glu_before = passed_along(glu_out[:, segment - rim_width :], "seq", 1)
    glu_wide = jnp.concatenate([glu_before, glu_out], axis=1).astype(jnp.float32)
    mixed_rows, kernel_pull = jax.vjp(partial(depthwise, glu_wide), dw_kernel)
    mixed_flat = mixed_rows.reshape(row_count, model_width)
    swished = conv_tail(mixed_flat, norm_gains[3], norm_biases[3]).astype(jnp.bfloat16)
    after_three = after_two + product(swished, conv_second)
    branch_two, kept_two = feed_forward(
        after_three,
        norm_gains[4],
        norm_biases[4],
        up_two,
        hidden_biases[1],
        down_two,
        model_biases[4],
    )
    after_four = after_three + 0.5 * branch_two
    final_rows, final_pull = jax.vjp(layer_norm, after_four, norm_gains[5], norm_biases[5])
    output = final_rows.astype(jnp.bfloat16).reshape(clip_count, segment, model_width)
    grad_four, gain_five, shift_five = final_pull(
        cotangent.reshape(row_count, model_width).astype(jnp.float32)
    )
    grad_three, up_two_grad, up_two_bias, down_two_grad, down_two_bias, gain_four, shift_four = (
        feed_backward(
            grad_four, after_three, kept_two, norm_gains[4], norm_biases[4], up_two, down_two
        )
    )
    conv_grad = grad_three.astype(jnp.bfloat16)
    conv_second_grad = contract_rows(swished, conv_grad)
    swished_grad = times_transposed(conv_grad, conv_second)
    tail_pull = jax.vjp(conv_tail, mixed_flat, norm_gains[3], norm_biases[3])[1]
    mixed_grad, gain_three, shift_three = tail_pull(swished_grad)
    mixed_low = mixed_grad.astype(jnp.bfloat16).reshape(clip_count, segment, model_width)
    mixed_after = passed_along(mixed_low[:, 0:rim_width], "seq", -1)
    mixed_wide = jnp.concatenate([mixed_low, mixed_after], axis=1).astype(jnp.float32)
    glu_grad = depthwise(mixed_wide, dw_kernel[::-1])
    kernel_grad = kernel_pull(mixed_low.astype(jnp.float32))[0]
    glu_pull = jax.vjp(glu_function, gate_input)[1]
    gate_grad = glu_pull(glu_grad.reshape(row_count, model_width))[0].astype(jnp.bfloat16)
    conv_first_grad = contract_rows(normed_conv, gate_grad)
    conv_norm_pull = jax.vjp(layer_norm, after_two, norm_gains[2], norm_biases[2])[1]
    values_grad, gain_two, shift_two = conv_norm_pull(times_transposed(gate_grad, conv_first))
    grad_two = grad_three + values_grad
    attn_grad = grad_two.astype(jnp.bfloat16)
    out_grad = contract_rows(attn_rows, attn_grad)
    out_bias_grad = jnp.sum(attn_grad.astype(jnp.float32), axis=0)
    merged_grad = (
        times_transposed(attn_grad, out_full)
        .astype(jnp.bfloat16)
        .reshape(clip_count, segment, model_width)
    )
    merged_heads = lax.all_to_all(merged_grad, "seq", split_axis=2, concat_axis=1, tiled=True)
    grad_items = split_heads(merged_heads, clip_count, length, head_count)

    def attend_back(operands):
        query_head, key_head, value_head, out_head, log_total = operands
        scores = head_scores(query_head, key_head)
        weights_soft = jnp.exp(scores - log_total[:, None])
        weights_low = weights_soft.astype(jnp.bfloat16)
        value_part = contract_rows(weights_low, out_head)
        weights_grad = times_transposed(out_head, value_head)
        delta_rows = jnp.sum(weights_soft * weights_grad, axis=-1, keepdims=True)
        score_grad = (weights_soft * (weights_grad - delta_rows)).astype(jnp.bfloat16)
        bucket_grad = collect_band(score_grad.astype(jnp.float32), length) * score_scale
        query_part = product(score_grad, key_head) * score_scale
        query_part = query_part + jnp.dot(bucket_grad, rel_wide, precision=lax.Precision.HIGHEST)
        key_part = contract_rows(score_grad, query_head) * score_scale
        table_part = jnp.dot(
            bucket_grad.T, query_head.astype(jnp.float32), precision=lax.Precision.HIGHEST
        )
        return (
            query_part.astype(jnp.bfloat16),
            key_part.astype(jnp.bfloat16),
            value_part.astype(jnp.bfloat16),
            table_part,
        )

    query_back, key_back, value_back, table_parts = lax.map(
        attend_back, (query_items, key_items, value_items, grad_items, log_totals)
    )
    table_grad = jnp.sum(table_parts, axis=0)
    query_seq_grad, key_seq_grad, value_seq_grad = (
        lax.all_to_all(
            merge_heads(query_back, clip_count, length, head_count),
            "seq",
            split_axis=1,
            concat_axis=2,
            tiled=True,
        ),
        lax.all_to_all(
            merge_heads(key_back, clip_count, length, head_count),
            "seq",
            split_axis=1,
            concat_axis=2,
            tiled=True,
        ),
        lax.all_to_all(
            merge_heads(value_back, clip_count, length, head_count),
            "seq",
            split_axis=1,
            concat_axis=2,
            tiled=True,
        ),
    )
    projected_grad = jnp.concatenate(
        [query_seq_grad, key_seq_grad, value_seq_grad], axis=-1
    ).reshape(row_count, 3 * model_width)
    qkv_grad = contract_rows(normed_attn, projected_grad)
    query_bias_grad = jnp.sum(query_seq_grad.astype(jnp.float32), axis=(0, 1))
    value_bias_grad = jnp.sum(value_seq_grad.astype(jnp.float32), axis=(0, 1))
    attn_norm_pull = jax.vjp(layer_norm, after_one, norm_gains[1], norm_biases[1])[1]
    values_grad, gain_one, shift_one = attn_norm_pull(times_transposed(projected_grad, qkv_full))
    grad_one = grad_two + values_grad
    grad_zero, up_one_grad, up_one_bias, down_one_grad, down_one_bias, gain_zero, shift_zero = (
        feed_backward(
            grad_one, input_rows, kept_one, norm_gains[0], norm_biases[0], up_one, down_one
        )
    )
    input_grad = grad_zero.astype(jnp.bfloat16).reshape(clip_count, segment, model_width)
    partial_sums = (
        lax.psum_scatter(
            up_one_grad.astype(jnp.bfloat16), "seq", scatter_dimension=1, tiled=True
        ).astype(jnp.float32),
        lax.psum_scatter(
            down_one_grad.astype(jnp.bfloat16), "seq", scatter_dimension=1, tiled=True
        ).astype(jnp.float32),
        lax.psum_scatter(
            qkv_grad.astype(jnp.bfloat16), "seq", scatter_dimension=1, tiled=True
        ).astype(jnp.float32),
        lax.psum_scatter(
            out_grad.astype(jnp.bfloat16), "seq", scatter_dimension=1, tiled=True
        ).astype(jnp.float32),
        lax.psum_scatter(
            conv_first_grad.astype(jnp.bfloat16), "seq", scatter_dimension=1, tiled=True
        ).astype(jnp.float32),
        lax.psum_scatter(
            conv_second_grad.astype(jnp.bfloat16), "seq", scatter_dimension=1, tiled=True
        ).astype(jnp.float32),
        lax.psum_scatter(
            up_two_grad.astype(jnp.bfloat16), "seq", scatter_dimension=1, tiled=True
        ).astype(jnp.float32),
        lax.psum_scatter(
            down_two_grad.astype(jnp.bfloat16), "seq", scatter_dimension=1, tiled=True
        ).astype(jnp.float32),
    )
    reduced = (
        lax.psum_scatter(
            partial_sums[0].astype(jnp.bfloat16), "fsdp", scatter_dimension=0, tiled=True
        ).astype(jnp.float32),
        lax.psum_scatter(
            partial_sums[1].astype(jnp.bfloat16), "fsdp", scatter_dimension=0, tiled=True
        ).astype(jnp.float32),
        lax.psum_scatter(
            partial_sums[2].astype(jnp.bfloat16), "fsdp", scatter_dimension=0, tiled=True
        ).astype(jnp.float32),
        lax.psum_scatter(
            partial_sums[3].astype(jnp.bfloat16), "fsdp", scatter_dimension=0, tiled=True
        ).astype(jnp.float32),
        lax.psum_scatter(
            partial_sums[4].astype(jnp.bfloat16), "fsdp", scatter_dimension=0, tiled=True
        ).astype(jnp.float32),
        lax.psum_scatter(
            partial_sums[5].astype(jnp.bfloat16), "fsdp", scatter_dimension=0, tiled=True
        ).astype(jnp.float32),
        lax.psum_scatter(
            partial_sums[6].astype(jnp.bfloat16), "fsdp", scatter_dimension=0, tiled=True
        ).astype(jnp.float32),
        lax.psum_scatter(
            partial_sums[7].astype(jnp.bfloat16), "fsdp", scatter_dimension=0, tiled=True
        ).astype(jnp.float32),
    )
    gains_stack = jnp.stack([gain_zero, gain_one, gain_two, gain_three, gain_four, gain_five])
    shifts_stack = jnp.stack(
        [shift_zero, shift_one, shift_two, shift_three, shift_four, shift_five]
    )
    hidden_stack = jnp.stack([up_one_bias, up_two_bias])
    model_stack = jnp.stack(
        [down_one_bias, query_bias_grad, value_bias_grad, out_bias_grad, down_two_bias]
    )
    gains_sum, shifts_sum, hidden_sum, model_sum, kernel_sum, table_sum = lax.psum(
        (gains_stack, shifts_stack, hidden_stack, model_stack, kernel_grad, table_grad),
        ("seq", "fsdp"),
    )
    return (
        output,
        input_grad,
        reduced[0],
        reduced[1],
        reduced[2],
        reduced[3],
        reduced[4],
        reduced[5],
        reduced[6],
        reduced[7],
        gains_sum,
        shifts_sum[0:3],
        shifts_sum[3:6],
        hidden_sum,
        model_sum[0:3],
        model_sum[3:5],
        kernel_sum,
        table_sum,
    )


def solution(mesh):
    in_specs = (
        P("fsdp", "seq", None),
        P("fsdp", "seq", None),
        P("fsdp", None),
        P("fsdp", None),
        P("fsdp", None),
        P("fsdp", None),
        P("fsdp", None),
        P("fsdp", None),
        P("fsdp", None),
        P("fsdp", None),
        P(),
        P(),
        P(),
        P(),
        P(),
        P(),
    )
    out_specs = (
        P("fsdp", "seq", None),
        P("fsdp", "seq", None),
        P("fsdp", "seq"),
        P("fsdp", "seq"),
        P("fsdp", "seq"),
        P("fsdp", "seq"),
        P("fsdp", "seq"),
        P("fsdp", "seq"),
        P("fsdp", "seq"),
        P("fsdp", "seq"),
        P(),
        P(),
        P(),
        P(),
        P(),
        P(),
        P(),
        P(),
    )
    return jax.shard_map(body, mesh=mesh, in_specs=in_specs, out_specs=out_specs, check_vma=False)
```

profile of v0, /device:TPU:0, one launch (start us, length us, event | category | flops | bytes accessed | tf_op | source)
XLA Modules:
  0.0 2970.4 jit_solution(3702273306651622581)
XLA Ops:
  20.3 68.1 %all-gather.9.cloned.1.call-done = bf16[1024,4096]{1,0:T(8,128)(2,1)} async-done(((bf16[64,4096]{1,0:T(8,128)(2,1)}), bf16[1024,4096]{1,0:T(8,128)(2,1)}) %all-gather.9.cloned.1.call-update) | async-done | bytes 8388624 | tf_op jit(solution)/shard_map/all_gather | solution.py:168
  98.8 65.6 %all-gather.11.cloned.1.call-done = bf16[4096,1024]{1,0:T(8,128)(2,1)} async-done(((bf16[256,1024]{1,0:T(8,128)(2,1)}), bf16[4096,1024]{1,0:T(8,128)(2,1)}) %all-gather.11.cloned.1.call-update) | async-done | bytes 8388624 | tf_op jit(solution)/shard_map/all_gather | solution.py:169
  174.5 52.8 %all-gather.13.cloned.1.call-done = bf16[1024,3072]{1,0:T(8,128)(2,1)} async-done(((bf16[64,3072]{1,0:T(8,128)(2,1)}), bf16[1024,3072]{1,0:T(8,128)(2,1)}) %all-gather.13.cloned.1.call-update) | async-done | bytes 6291472 | tf_op jit(solution)/shard_map/all_gather | solution.py:170
  326.7 344.6 %while.32 = (s32[]{:T(128)}, bf16[8,1024,64]{1,2,0:T(8,128)(2,1)}, f32[8,1024]{1,0:T(8,128)}, bf16[8,1024,64]{2,1,0:T(8,128)(2,1)S(1)}, bf16[8,1024,64]{2,1,0:T(...) while((s32[]{:T(128)}, bf16[8,1024,64]{1,2,0:T(8,128)(2,1)}, ...), condition=%wide.region_7.8_spmd, body=%wide.region_4.7_spmd.sunk | while | flops 291699712 | bytes 84261000 | solution.py:231
  689.2 18.1 all_to_all.129
  745.5 11.9 fusion.177
  774.1 14.2 convert_reduce_fusion
  870.5 13.5 all-to-all-done.4
  890.3 683.5 %while.33 = (s32[]{:T(128)}, bf16[8,1024,64]{1,2,0:T(8,128)(2,1)}, bf16[8,1024,64]{1,2,0:T(8,128)(2,1)}, bf16[8,1024,64]{1,2,0:T(8,128)(2,1)}, f32[8,73,64]{1,2,...) while((s32[]{:T(128)}, bf16[8,1024,64]{1,2,0:T(8,128)(2,1)}, ...), condition=%wide.region_28.29_spmd, body=%wide.region_24.28_spmd.sunk | while | flops 825674752 | bytes 199772352 | solution.py:317
  1744.5 91.4 %reduce-scatter.41.cloned.1.call-done = bf16[1024,2048]{1,0:T(8,128)(2,1)} async-done(((bf16[1024,4096]{1,0:T(8,128)(2,1)}), bf16[1024,2048]{1,0:T(8,128)(2,1)}) %reduce-scatter.41.cloned.1.call-update) | async-done | bytes 4194320 | tf_op jit(solution)/shard_map/reduce_scatter | solution.py:378
  1836.0 101.5 %reduce-scatter.45.cloned.1.call-done = bf16[4096,512]{1,0:T(8,128)(2,1)} async-done(((bf16[4096,1024]{1,0:T(8,128)(2,1)}), bf16[4096,512]{1,0:T(8,128)(2,1)}) %reduce-scatter.45.cloned.1.call-update) | async-done | bytes 4194320 | tf_op jit(solution)/shard_map/reduce_scatter | solution.py:381
  1937.5 101.4 %reduce-scatter.21.cloned.1.call-done = bf16[4096,512]{1,0:T(8,128)(2,1)} async-done(((bf16[4096,1024]{1,0:T(8,128)(2,1)}), bf16[4096,512]{1,0:T(8,128)(2,1)}) %reduce-scatter.21.cloned.1.call-update) | async-done | bytes 4194320 | tf_op jit(solution)/shard_map/reduce_scatter | solution.py:363
  2038.9 101.5 %reduce-scatter.17.cloned.1.call-done = bf16[1024,2048]{1,0:T(8,128)(2,1)} async-done(((bf16[1024,4096]{1,0:T(8,128)(2,1)}), bf16[1024,2048]{1,0:T(8,128)(2,1)}) %reduce-scatter.17.cloned.1.call-update) | async-done | bytes 4194320 | tf_op jit(solution)/shard_map/reduce_scatter | solution.py:360
  2140.9 49.4 %fusion.93 = f32[31,1,1024]{2,1,0:T(1,128)S(1)} fusion(bf16[1,542,1024]{2,1,0:T(8,128)(2,1)} %copy-done.29, bf16[1,512,1024]{2,1,0:T(8,128)(2,1)} %copy-done.28), kind=kOutput, calls=%fused_computation.135 | convolution fusion | flops 32505856 | bytes 2285568 | tf_op jit(solution)/shard_map/transpose(jvp())/conv_general_dilated | solution.py:56
  2194.3 78.9 %all-reduce.12.cloned.1.call-done = (f32[6,1024]{1,0:T(8,128)}, f32[6,1024]{1,0:T(8,128)}, f32[2,4096]{1,0:T(2,128)}, f32[5,1024]{1,0:T(8,128)}, f32[73,64]{0,1:T(8,128)}) async-done(((f32[6,1024]{1,0:T(8,128)}, f32[6,1024]{1,0:T(8,128)}, f32[2,4096]{1,0:T(2,128)}, f32[5,1024]{1,0:T(8,128)}, f32[73,64]{0,1:T(8,128)}), (f32[6,1024]{1,0:T(8,128)}, f32[6,1024]{1,0:T(8,128)}, f32[2,4096]{1,0:T(2,128)}, ...) | async-done | bytes 121104 | tf_op jit(solution)/shard_map/psum | solution.py:419
  2277.4 58.3 %reduce-scatter.39.cloned.1.call-done = bf16[64,512]{1,0:T(8,128)(2,1)} async-done(((bf16[1024,512]{1,0:T(8,128)(2,1)}), bf16[64,512]{1,0:T(8,128)(2,1)}) %reduce-scatter.39.cloned.1.call-update) | async-done | bytes 65552 | tf_op jit(solution)/shard_map/reduce_scatter | solution.py:401
  2337.1 59.0 %reduce-scatter.31.cloned.1.call-done = bf16[64,512]{1,0:T(8,128)(2,1)} async-done(((bf16[1024,512]{1,0:T(8,128)(2,1)}), bf16[64,512]{1,0:T(8,128)(2,1)}) %reduce-scatter.31.cloned.1.call-update) | async-done | bytes 65552 | tf_op jit(solution)/shard_map/reduce_scatter | solution.py:395
  2397.6 62.7 %reduce-scatter.35.cloned.1.call-done = bf16[64,1024]{1,0:T(8,128)(2,1)} async-done(((bf16[1024,1024]{1,0:T(8,128)(2,1)}), bf16[64,1024]{1,0:T(8,128)(2,1)}) %reduce-scatter.35.cloned.1.call-update) | async-done | bytes 131088 | tf_op jit(solution)/shard_map/reduce_scatter | solution.py:398
  2462.0 67.9 %reduce-scatter.27.cloned.1.call-done = bf16[64,1536]{1,0:T(8,128)(2,1)} async-done(((bf16[1024,1536]{1,0:T(8,128)(2,1)}), bf16[64,1536]{1,0:T(8,128)(2,1)}) %reduce-scatter.27.cloned.1.call-update) | async-done | bytes 196624 | tf_op jit(solution)/shard_map/reduce_scatter | solution.py:392
  2531.6 74.1 %reduce-scatter.43.cloned.1.call-done = bf16[64,2048]{1,0:T(8,128)(2,1)} async-done(((bf16[1024,2048]{1,0:T(8,128)(2,1)}), bf16[64,2048]{1,0:T(8,128)(2,1)}) %reduce-scatter.43.cloned.1.call-update) | async-done | bytes 262160 | tf_op jit(solution)/shard_map/reduce_scatter | solution.py:404
  2607.4 73.4 %reduce-scatter.47.cloned.1.call-done = bf16[256,512]{1,0:T(8,128)(2,1)} async-done(((bf16[4096,512]{1,0:T(8,128)(2,1)}), bf16[256,512]{1,0:T(8,128)(2,1)}) %reduce-scatter.47.cloned.1.call-update) | async-done | bytes 262160 | tf_op jit(solution)/shard_map/reduce_scatter | solution.py:407
  2682.6 73.9 %reduce-scatter.23.cloned.1.call-done = bf16[256,512]{1,0:T(8,128)(2,1)} async-done(((bf16[4096,512]{1,0:T(8,128)(2,1)}), bf16[256,512]{1,0:T(8,128)(2,1)}) %reduce-scatter.23.cloned.1.call-update) | async-done | bytes 262160 | tf_op jit(solution)/shard_map/reduce_scatter | solution.py:389
  2758.3 73.4 %reduce-scatter.19.cloned.1.call-done = bf16[64,2048]{1,0:T(8,128)(2,1)} async-done(((bf16[1024,2048]{1,0:T(8,128)(2,1)}), bf16[64,2048]{1,0:T(8,128)(2,1)}) %reduce-scatter.19.cloned.1.call-update) | async-done | bytes 262160 | tf_op jit(solution)/shard_map/reduce_scatter | solution.py:386
  2833.5 126.7 %all-reduce.10.cloned.1.call-done = f32[31,1024]{1,0:T(8,128)} async-done(((f32[31,1024]{1,0:T(8,128)}), f32[31,1024]{1,0:T(8,128)}) %all-reduce.10.cloned.1.call-update) | async-done | bytes 126992 | tf_op jit(solution)/shard_map/psum | solution.py:419
  (922 shorter events, 1515.0 us)
Async XLA Ops:
  9.5 154.8 %all-gather.11.cloned.1.call-start = ((), (), s32[]{:S(2)}) async-start(), calls=%async_computation.25 | async-start | bytes 8912896 | tf_op jit(solution)/shard_map/all_gather | solution.py:169
  10.4 216.8 %all-gather.13.cloned.1.call-start = ((), (), s32[]{:S(2)}) async-start(), calls=%async_computation.26 | async-start | bytes 6684672 | tf_op jit(solution)/shard_map/all_gather | solution.py:170
  11.3 698.5 %all-gather.15.cloned.1.call-start = ((), (), s32[]{:S(2)}) async-start(), calls=%async_computation.27 | async-start | bytes 2228224 | tf_op jit(solution)/shard_map/all_gather | solution.py:171
  13.1 702.3 %all-gather.17.cloned.1.call-start = ((), (), s32[]{:S(2)}) async-start(), calls=%async_computation.28 | async-start | bytes 4456448 | tf_op jit(solution)/shard_map/all_gather | solution.py:172
  13.9 725.9 %all-gather.19.cloned.1.call-start = ((), (), s32[]{:S(2)}) async-start(), calls=%async_computation.29 | async-start | bytes 2228224 | tf_op jit(solution)/shard_map/all_gather | solution.py:173
  15.7 729.8 %all-gather.21.cloned.1.call-start = ((), (), s32[]{:S(2)}) async-start(), calls=%async_computation.30 | async-start | bytes 8912896 | tf_op jit(solution)/shard_map/all_gather | solution.py:174
  293.9 463.4 %all-gather.23.cloned.1.call-start = ((), (), s32[]{:S(2)}) async-start(), calls=%async_computation.31 | async-start | bytes 8912896 | tf_op jit(solution)/shard_map/all_gather | solution.py:175
  294.9 1447.0 %reduce-scatter.37.cloned.1.call-start = ((), (), s32[]{:S(2)}) async-start(), calls=%async_computation.42 | async-start | bytes 3145728 | tf_op jit(solution)/shard_map/reduce_scatter | solution.py:375
  808.2 934.3 %reduce-scatter.29.cloned.1.call-start = ((), (), s32[]{:S(2)}) async-start(), calls=%async_computation.38 | async-start | bytes 3145728 | tf_op jit(solution)/shard_map/reduce_scatter | solution.py:369
  863.6 879.6 %reduce-scatter.33.cloned.1.call-start = ((), (), s32[]{:S(2)}) async-start(), calls=%async_computation.40 | async-start | bytes 6291456 | tf_op jit(solution)/shard_map/reduce_scatter | solution.py:372
  1656.9 179.0 %reduce-scatter.41.cloned.1.call-start = ((), (), s32[]{:S(2)}) async-start(), calls=%async_computation.44 | async-start | bytes 12582912 | tf_op jit(solution)/shard_map/reduce_scatter | solution.py:378
  1668.3 269.1 %reduce-scatter.45.cloned.1.call-start = ((), (), s32[]{:S(2)}) async-start(), calls=%async_computation.46 | async-start | bytes 12582912 | tf_op jit(solution)/shard_map/reduce_scatter | solution.py:381
  1680.8 358.0 %reduce-scatter.21.cloned.1.call-start = ((), (), s32[]{:S(2)}) async-start(), calls=%async_computation.34 | async-start | bytes 12582912 | tf_op jit(solution)/shard_map/reduce_scatter | solution.py:363
  1706.3 434.1 %reduce-scatter.17.cloned.1.call-start = ((), (), s32[]{:S(2)}) async-start(), calls=%async_computation.32 | async-start | bytes 12582912 | tf_op jit(solution)/shard_map/reduce_scatter | solution.py:360
  1727.1 546.1 %all-reduce.12.cloned.1.call-start = ((), (), s32[]{:S(2)}) async-start(), calls=%async_computation.49 | async-start | bytes 327680 | tf_op jit(solution)/shard_map/psum | solution.py:419
  1741.8 593.8 %reduce-scatter.39.cloned.1.call-start = ((), (), s32[]{:S(2)}) async-start(), calls=%async_computation.43 | async-start | bytes 1114112 | tf_op jit(solution)/shard_map/reduce_scatter | solution.py:401
  1742.4 653.7 %reduce-scatter.31.cloned.1.call-start = ((), (), s32[]{:S(2)}) async-start(), calls=%async_computation.39 | async-start | bytes 1114112 | tf_op jit(solution)/shard_map/reduce_scatter | solution.py:395
  1743.1 717.2 %reduce-scatter.35.cloned.1.call-start = ((), (), s32[]{:S(2)}) async-start(), calls=%async_computation.41 | async-start | bytes 2228224 | tf_op jit(solution)/shard_map/reduce_scatter | solution.py:398
  1743.7 786.1 %reduce-scatter.27.cloned.1.call-start = ((), (), s32[]{:S(2)}) async-start(), calls=%async_computation.37 | async-start | bytes 3342336 | tf_op jit(solution)/shard_map/reduce_scatter | solution.py:392
  1744.5 861.2 %reduce-scatter.43.cloned.1.call-start = ((), (), s32[]{:S(2)}) async-start(), calls=%async_computation.45 | async-start | bytes 4456448 | tf_op jit(solution)/shard_map/reduce_scatter | solution.py:404
  1835.9 844.9 %reduce-scatter.47.cloned.1.call-start = ((), (), s32[]{:S(2)}) async-start(), calls=%async_computation.47 | async-start | bytes 4456448 | tf_op jit(solution)/shard_map/reduce_scatter | solution.py:407
  1937.4 819.0 %reduce-scatter.23.cloned.1.call-start = ((), (), s32[]{:S(2)}) async-start(), calls=%async_computation.35 | async-start | bytes 4456448 | tf_op jit(solution)/shard_map/reduce_scatter | solution.py:389
  2038.9 792.8 %reduce-scatter.19.cloned.1.call-start = ((), (), s32[]{:S(2)}) async-start(), calls=%async_computation.33 | async-start | bytes 4456448 | tf_op jit(solution)/shard_map/reduce_scatter | solution.py:386
  2140.4 819.8 %all-reduce.10.cloned.1.call-start = ((), (), s32[]{:S(2)}) async-start(), calls=%async_computation.48 | async-start | bytes 262144 | tf_op jit(solution)/shard_map/psum | solution.py:419
  (173 other events, 4053.0 us)
Sparse Core Ops, SparseCore 0:
  10.8 77.5 all-gather.8
  91.1 73.1 all-gather.10
  167.2 60.0 all-gather.12
  229.9 39.9 all-gather.14
  272.5 49.3 all-gather.16
  324.4 39.8 all-gather.18
  367.1 73.6 all-gather.20
  443.5 73.1 all-gather.22
  884.3 56.8 reduce-scatter.32
  1657.0 77.2 reduce-scatter.24
  1736.6 99.2 reduce-scatter.40
  1838.1 99.2 reduce-scatter.44
  1939.6 99.2 reduce-scatter.20
  2041.1 99.2 reduce-scatter.16
  2148.4 124.7 all-reduce.11
  2276.7 58.9 reduce-scatter.38
  2339.7 56.3 reduce-scatter.30
  2399.7 60.5 reduce-scatter.34
  2464.6 65.1 reduce-scatter.26
  2534.2 71.3 reduce-scatter.42
  2609.5 71.2 reduce-scatter.46
  2685.0 71.4 reduce-scatter.22
  2760.4 71.3 reduce-scatter.18
  2838.6 121.5 all-reduce.9
  (2 shorter events, 71.3 us)
where the time goes:
time: 2990 us; the launch traced here: 2970 us
  waiting for transfers between devices  1350 us (45%)
  local copies, waits for them, and re-layouts  970 us (32%)
  matrix products  421 us (14%)
  other arithmetic  155 us (5%)
  starting transfers between devices  32.9 us (1%)
    reshape x32, local copies, waits for them, and re-layouts, spread_band(): padded.reshape(length * (row_width + 1))[:length * row_width]  241 us
    psum x2, waiting for transfers between devices, body(): lax.psum((gains_stack, shifts_stack, hidden_stack, model_stack, kernel_gr...  206 us
    while x152, local copies, waits for them, and re-layouts  143 us
    dot_general x48, matrix products, times_transposed(): lax.dot_general(former, latter, (((1,), (1,)), ((), ())), preferred_eleme...  131 us
    dot_general x24, matrix products, product(): return jnp.dot(former, latter, preferred_element_type=jnp.float32)  103 us
    reduce_scatter x1, waiting for transfers between devices, body(): lax.psum_scatter(down_two_grad.astype(jnp.bfloat16), 'seq', scatter_dimen...  101 us
    reduce_scatter x1, waiting for transfers between devices, body(): lax.psum_scatter(up_one_grad.astype(jnp.bfloat16), 'seq', scatter_dimensi...  101 us
    reduce_scatter x1, waiting for transfers between devices, body(): lax.psum_scatter(down_one_grad.astype(jnp.bfloat16), 'seq', scatter_dimen...  101 us
  transfers between devices with their start and end apart: 35, of which 21 were waited for; matrix products, arithmetic and copies ran while one was open for 49% of the time, Pallas kernels for 0%

commit v1 on v0

--- a/solution.py
+++ b/solution.py
@@ -3,6 +3,8 @@
 import jax
 import jax.numpy as jnp
 from jax import lax
+from jax.experimental import pallas as pl
+from jax.experimental.pallas import tpu as pltpu
 from jax.sharding import PartitionSpec as P
 
 HEAD = 64
@@ -64,37 +66,195 @@
     )
 
 
-def relative_grid(length):
-    row_places = lax.broadcasted_iota(jnp.int32, (length, length), 0)
-    col_places = lax.broadcasted_iota(jnp.int32, (length, length), 1)
-    return col_places - row_places
-
-
-def spread_band(position, length):
-    row_width = length + BUCKETS
-    padded = jnp.pad(position, ((0, 0), (0, row_width + 1 - BUCKETS)))
-    skewed = padded.reshape(length * (row_width + 1))[: length * row_width].reshape(
-        length, row_width
-    )
-    band_part = skewed[:, LEFT : LEFT + length]
-    relative = relative_grid(length)
-    return jnp.where(
-        relative <= -LEFT,
-        position[:, 0:1],
-        jnp.where(relative >= RIGHT, position[:, BUCKETS - 1 : BUCKETS], band_part),
-    )
-
-
-def collect_band(score_wide, length):
-    row_width = length + BUCKETS
-    relative = relative_grid(length)
-    inside = jnp.where((relative > -LEFT) & (relative < RIGHT), score_wide, 0.0)
-    first_bucket = jnp.sum(jnp.where(relative <= -LEFT, score_wide, 0.0), axis=1, keepdims=True)
-    last_bucket = jnp.sum(jnp.where(relative >= RIGHT, score_wide, 0.0), axis=1, keepdims=True)
-    widened = jnp.pad(inside, ((0, 0), (LEFT, RIGHT + 1)))
-    flat_rows = jnp.pad(widened.reshape(length * row_width), (0, length))
-    unskewed = flat_rows.reshape(length, row_width + 1)[:, 1 : BUCKETS - 1]
-    return jnp.concatenate([first_bucket, unskewed, last_bucket], axis=1)
+PAIR = 2
+LANES = 128
+FWD_ROWS = 256
+BACK_ROWS = 256
+
+
+def nt(former, latter):
+    return lax.dot_general(former, latter, (((1,), (1,)), ((), ())), preferred_element_type=jnp.float32)
+
+
+def nn(former, latter):
+    return lax.dot_general(former, latter, (((1,), (0,)), ((), ())), preferred_element_type=jnp.float32)
+
+
+def window_of(start, rows, length):
+    low, high = start - LANES, start + rows + LANES
+    return max(low, 0), min(high, length), max(low, 0) - low
+
+
+def window_buckets(rows):
+    width = rows + 2 * LANES
+    places = lax.broadcasted_iota(jnp.int32, (rows, width), 1)
+    lines = lax.broadcasted_iota(jnp.int32, (rows, width), 0)
+    return places - lines - (LANES - LEFT)
+
+
+def biased_scores(scores, position, start, rows, length):
+    width = rows + 2 * LANES
+    low, high, skip = window_of(start, rows, length)
+    wide = jnp.concatenate([position, jnp.zeros((rows, width - LANES), jnp.float32)], axis=1)
+    band = pltpu.roll(wide, LANES - LEFT, 1, stride=1, stride_axis=0)
+    first, last = position[:, 0:1], position[:, BUCKETS - 1 : BUCKETS]
+    bucket = window_buckets(rows)
+    band = jnp.where(bucket <= 0, first, jnp.where(bucket >= BUCKETS - 1, last, band))
+    pieces = []
+    if low > 0:
+        pieces.append(scores[:, :low] + first)
+    pieces.append(scores[:, low:high] + band[:, skip : skip + high - low])
+    if high < length:
+        pieces.append(scores[:, high:] + last)
+    return pieces[0] if len(pieces) == 1 else jnp.concatenate(pieces, axis=1)
+
+
+def bucket_sums(score_grad, mirror, start, rows, length):
+    width = rows + 2 * LANES
+    low, high, skip = window_of(start, rows, length)
+    inner = score_grad[:, low:high]
+    pieces = []
+    if skip > 0:
+        pieces.append(jnp.zeros((rows, skip), jnp.float32))
+    pieces.append(inner)
+    if skip + high - low < width:
+        pieces.append(jnp.zeros((rows, width - skip - high + low), jnp.float32))
+    wide = pieces[0] if len(pieces) == 1 else jnp.concatenate(pieces, axis=1)
+    bucket = window_buckets(rows)
+    first = jnp.sum(jnp.where(bucket <= 0, wide, 0.0), axis=1, keepdims=True)
+    last = jnp.sum(jnp.where(bucket >= BUCKETS - 1, wide, 0.0), axis=1, keepdims=True)
+    if low > 0:
+        first = first + jnp.sum(score_grad[:, :low], axis=1, keepdims=True)
+    if high < length:
+        last = last + jnp.sum(score_grad[:, high:], axis=1, keepdims=True)
+    turned = nn(wide.astype(jnp.bfloat16), mirror)
+    band = pltpu.roll(turned, (LANES + LANES - LEFT) % width, 1, stride=1, stride_axis=0)[:, :LANES]
+    bucket = LANES - 1 - lax.broadcasted_iota(jnp.int32, (rows, LANES), 1)
+    return jnp.where(bucket == 0, first, jnp.where(bucket == BUCKETS - 1, last, jnp.where(bucket < BUCKETS, band, 0.0)))
+
+
+def mirror_of(width):
+    lines = lax.broadcasted_iota(jnp.int32, (width, width), 0)
+    places = lax.broadcasted_iota(jnp.int32, (width, width), 1)
+    return jnp.where(lines + places == width - 1, 1.0, 0.0).astype(jnp.bfloat16)
+
+
+def attend_kernel(q_ref, k_ref, v_ref, rel_ref, out_ref, log_ref):
+    length = q_ref.shape[1]
+    rows = min(FWD_ROWS, length)
+    scale = HEAD ** (-0.5)
+    rel = rel_ref[...]
+    for start in range(0, length, rows):
+        outs, logs = [], []
+        for h in range(PAIR):
+            lanes = slice(h * HEAD, (h + 1) * HEAD)
+            query = q_ref[0, start : start + rows, lanes] * scale
+            scores = nt(query, k_ref[0, :, lanes])
+            scores = biased_scores(scores, nt(query, rel), start, rows, length)
+            highest = jnp.max(scores, axis=1, keepdims=True)
+            weights = jnp.exp(scores - highest)
+            total = jnp.sum(weights, axis=1, keepdims=True)
+            outs.append(nn(weights.astype(jnp.bfloat16), v_ref[0, :, lanes]) / total)
+            logs.append(highest + jnp.log(total))
+        out_ref[0, start : start + rows, :] = jnp.concatenate(outs, axis=1).astype(jnp.bfloat16)
+        log_ref[0, 0, start : start + rows, :] = jnp.concatenate(logs, axis=1)
+
+
+def attend_back_kernel(q_ref, k_ref, v_ref, do_ref, log_ref, rel_ref, back_ref, mirror_ref, dq_ref, dk_ref, dv_ref, table_ref, dkt, dvt):
+    length = q_ref.shape[1]
+    rows = min(BACK_ROWS, length)
+    scale = HEAD ** (-0.5)
+    rel = rel_ref[...]
+    q_turned = (jnp.transpose(q_ref[0].astype(jnp.float32)) * scale).astype(jnp.bfloat16)
+    do_turned = jnp.transpose(do_ref[0].astype(jnp.float32)).astype(jnp.bfloat16)
+    back = back_ref[...]
+    table = jnp.zeros((HEAD, LANES), jnp.float32)
+    for start in range(0, length, rows):
+        span = slice(start, start + rows)
+        parts = []
+        for h in range(PAIR):
+            lanes = slice(h * HEAD, (h + 1) * HEAD)
+            query = q_ref[0, span, lanes] * scale
+            scores = nt(query, k_ref[0, :, lanes])
+            scores = biased_scores(scores, nt(query, rel), start, rows, length)
+            weights = jnp.exp(scores - log_ref[0, 0, span, h : h + 1])
+            low_weights = weights.astype(jnp.bfloat16)
+            grads = nt(do_ref[0, span, lanes], v_ref[0, :, lanes])
+            both = weights * grads
+            delta = jnp.sum(both, axis=1, keepdims=True)
+            score_grad = (both - weights * delta).astype(jnp.bfloat16)
+            value_part = nn(do_turned[lanes, span], low_weights)
+            key_part = nn(q_turned[lanes, span], score_grad)
+            if start == 0:
+                dvt[lanes, :] = value_part
+                dkt[lanes, :] = key_part
+            else:
+                dvt[lanes, :] += value_part
+                dkt[lanes, :] += key_part
+            bucket = bucket_sums(score_grad.astype(jnp.float32), mirror_ref[...], start, rows, length)
+            high = bucket.astype(jnp.bfloat16)
+            rest = (bucket - high.astype(jnp.float32)).astype(jnp.bfloat16)
+            parts.append((nn(score_grad, k_ref[0, :, lanes]) + nn(high, back) + nn(rest, back)) * scale)
+            table = table + nn(q_turned[lanes, span], high) + nn(q_turned[lanes, span], rest)
+        dq_ref[0, span, :] = jnp.concatenate(parts, axis=1).astype(jnp.bfloat16)
+    dk_ref[0] = jnp.transpose(dkt[...]).astype(jnp.bfloat16)
+    dv_ref[0] = jnp.transpose(dvt[...]).astype(jnp.bfloat16)
+    table_ref[0, 0] = table
+
+
+def width_of(length):
+    return min(BACK_ROWS, length) + 2 * LANES
+
+
+def head_block(length):
+    return pl.BlockSpec((1, length, PAIR * HEAD), lambda i, j: (i, 0, j))
+
+
+def padded_table(rel_table):
+    return jnp.pad(rel_table.astype(jnp.bfloat16), ((0, LANES - BUCKETS), (0, 0)))
+
+
+def attend(query, key, value, rel_low):
+    clips, length, width = query.shape
+    pairs = width // (PAIR * HEAD)
+    block = head_block(length)
+    return pl.pallas_call(
+        attend_kernel,
+        grid=(clips, pairs),
+        in_specs=[block, block, block, pl.BlockSpec((LANES, HEAD), lambda i, j: (0, 0))],
+        out_specs=[block, pl.BlockSpec((1, 1, length, PAIR), lambda i, j: (i, j, 0, 0))],
+        out_shape=[
+            jax.ShapeDtypeStruct(query.shape, jnp.bfloat16),
+            jax.ShapeDtypeStruct((clips, pairs, length, PAIR), jnp.float32),
+        ],
+        compiler_params=pltpu.CompilerParams(vmem_limit_bytes=48 << 20),
+        cost_estimate=pl.CostEstimate(flops=4 * clips * width * length * length * 4, bytes_accessed=8 * query.size, transcendentals=clips * pairs * PAIR * length * length),
+        name="attend",
+    )(query, key, value, rel_low)
+
+
+def attend_back(query, key, value, out_grad, logs, rel_low):
+    clips, length, width = query.shape
+    pairs = width // (PAIR * HEAD)
+    block = head_block(length)
+    shape = jax.ShapeDtypeStruct(query.shape, jnp.bfloat16)
+    return pl.pallas_call(
+        attend_back_kernel,
+        grid=(clips, pairs),
+        in_specs=[
+            block, block, block, block,
+            pl.BlockSpec((1, 1, length, PAIR), lambda i, j: (i, j, 0, 0)),
+            pl.BlockSpec((LANES, HEAD), lambda i, j: (0, 0)),
+            pl.BlockSpec((LANES, HEAD), lambda i, j: (0, 0)),
+            pl.BlockSpec((width_of(length),) * 2, lambda i, j: (0, 0)),
+        ],
+        out_specs=[block, block, block, pl.BlockSpec((1, 1, HEAD, LANES), lambda i, j: (i, j, 0, 0))],
+        out_shape=[shape, shape, shape, jax.ShapeDtypeStruct((clips, pairs, HEAD, LANES), jnp.float32)],
+        scratch_shapes=[pltpu.VMEM((PAIR * HEAD, length), jnp.float32)] * 2,
+        compiler_params=pltpu.CompilerParams(vmem_limit_bytes=48 << 20),
+        cost_estimate=pl.CostEstimate(flops=10 * clips * width * length * length * 4, bytes_accessed=14 * query.size, transcendentals=clips * pairs * PAIR * length * length),
+        name="attend_back",
+    )(query, key, value, out_grad, logs, rel_low, rel_low[::-1], mirror_of(width_of(length)))
 
 
 def feed_forward(values, norm_gain, norm_shift, weight_up, bias_up, weight_down, bias_down):
@@ -129,16 +289,6 @@
     )
 
 
-def split_heads(array, clip_count, length, head_count):
-    shaped = array.reshape(clip_count, length, head_count, HEAD).transpose(0, 2, 1, 3)
-    return shaped.reshape(clip_count * head_count, length, HEAD)
-
-
-def merge_heads(array, clip_count, length, head_count):
-    shaped = array.reshape(clip_count, head_count, length, HEAD).transpose(0, 2, 1, 3)
-    return shaped.reshape(clip_count, length, head_count * HEAD)
-
-
 def body(
     tokens,
     cotangent,
@@ -159,11 +309,7 @@
 ):
     clip_count, segment, model_width = tokens.shape
     row_count = clip_count * segment
-    groups = lax.axis_size("seq")
-    length = segment * groups
-    head_count = model_width // groups // HEAD
     rim_width = KERNEL - 1
-    score_scale = HEAD ** (-0.5)
     up_one, down_one, qkv_full, out_full, conv_first, conv_second, up_two, down_two = (
         lax.all_gather(ffn1_up.astype(jnp.bfloat16), "fsdp", axis=0, tiled=True),
         lax.all_gather(ffn1_down.astype(jnp.bfloat16), "fsdp", axis=0, tiled=True),
@@ -207,29 +353,8 @@
         lax.all_to_all(keys_seq, "seq", split_axis=2, concat_axis=1, tiled=True),
         lax.all_to_all(values_seq, "seq", split_axis=2, concat_axis=1, tiled=True),
     )
-    query_items = split_heads(query_heads, clip_count, length, head_count)
-    key_items = split_heads(key_heads, clip_count, length, head_count)
-    value_items = split_heads(value_heads, clip_count, length, head_count)
-    rel_low = rel_table.astype(jnp.bfloat16)
-    rel_wide = rel_low.astype(jnp.float32)
-
-    def head_scores(query_head, key_head):
-        direct = times_transposed(query_head, key_head)
-        position = times_transposed(query_head, rel_low)
-        return (direct + spread_band(position, length)) * score_scale
-
-    def attend(operands):
-        query_head, key_head, value_head = operands
-        scores = head_scores(query_head, key_head)
-        highest = jnp.max(scores, axis=-1, keepdims=True)
-        weights_exp = jnp.exp(scores - highest)
-        row_total = jnp.sum(weights_exp, axis=-1, keepdims=True)
-        weights_soft = (weights_exp / row_total).astype(jnp.bfloat16)
-        head_out = product(weights_soft, value_head).astype(jnp.bfloat16)
-        return (head_out, highest[:, 0] + jnp.log(row_total[:, 0]))
-
-    head_outputs, log_totals = lax.map(attend, (query_items, key_items, value_items))
-    merged = merge_heads(head_outputs, clip_count, length, head_count)
+    rel_low = padded_table(rel_table)
+    merged, log_totals = attend(query_heads, key_heads, value_heads, rel_low)
     attn_seq = lax.all_to_all(merged, "seq", split_axis=1, concat_axis=2, tiled=True)
     attn_rows = attn_seq.reshape(row_count, model_width)
     after_two = after_one + product(attn_rows, out_full) + model_biases[3]
@@ -289,52 +414,27 @@
         .reshape(clip_count, segment, model_width)
     )
     merged_heads = lax.all_to_all(merged_grad, "seq", split_axis=2, concat_axis=1, tiled=True)
-    grad_items = split_heads(merged_heads, clip_count, length, head_count)
-
-    def attend_back(operands):
-        query_head, key_head, value_head, out_head, log_total = operands
-        scores = head_scores(query_head, key_head)
-        weights_soft = jnp.exp(scores - log_total[:, None])
-        weights_low = weights_soft.astype(jnp.bfloat16)
-        value_part = contract_rows(weights_low, out_head)
-        weights_grad = times_transposed(out_head, value_head)
-        delta_rows = jnp.sum(weights_soft * weights_grad, axis=-1, keepdims=True)
-        score_grad = (weights_soft * (weights_grad - delta_rows)).astype(jnp.bfloat16)
-        bucket_grad = collect_band(score_grad.astype(jnp.float32), length) * score_scale
-        query_part = product(score_grad, key_head) * score_scale
-        query_part = query_part + jnp.dot(bucket_grad, rel_wide, precision=lax.Precision.HIGHEST)
-        key_part = contract_rows(score_grad, query_head) * score_scale
-        table_part = jnp.dot(
-            bucket_grad.T, query_head.astype(jnp.float32), precision=lax.Precision.HIGHEST
-        )
-        return (
-            query_part.astype(jnp.bfloat16),
-            key_part.astype(jnp.bfloat16),
-            value_part.astype(jnp.bfloat16),
-            table_part,
-        )
-
-    query_back, key_back, value_back, table_parts = lax.map(
-        attend_back, (query_items, key_items, value_items, grad_items, log_totals)
-    )
-    table_grad = jnp.sum(table_parts, axis=0)
+    query_back, key_back, value_back, table_parts = attend_back(
+        query_heads, key_heads, value_heads, merged_heads, log_totals, rel_low
+    )
+    table_grad = jnp.sum(table_parts, axis=(0, 1)).T[::-1][:BUCKETS]
     query_seq_grad, key_seq_grad, value_seq_grad = (
         lax.all_to_all(
-            merge_heads(query_back, clip_count, length, head_count),
+            query_back,
             "seq",
             split_axis=1,
             concat_axis=2,
             tiled=True,
         ),
         lax.all_to_all(
-            merge_heads(key_back, clip_count, length, head_count),
+            key_back,
             "seq",
             split_axis=1,
             concat_axis=2,
             tiled=True,
         ),
         lax.all_to_all(
-            merge_heads(value_back, clip_count, length, head_count),
+            value_back,
             "seq",
             split_axis=1,
             concat_axis=2,

time: 2990 us -> 2100 us (0.70)
  local copies, waits for them, and re-layouts: 970 us -> 118 us
  matrix products: 421 us -> 298 us
  waiting for transfers between devices: 1350 us -> 1430 us
  Pallas kernels: 0 us -> 73.8 us
  other arithmetic: 155 us -> 109 us
    reshape x56 -> x0, local copies, waits for them, and re-layouts: 388 us -> none  [the longest x32 241 us: spread_band(): padded.reshape(length * (row_width + 1))[:length * row_width]]
    slice x56 -> x2, local copies, waits for them, and re-layouts: 161 us -> 0.77 us  [body(): table_grad = jnp.sum(table_parts, axis=(0, 1)).T[::-1][:BUCKETS]]
    while x155 -> x0, local copies, waits for them, and re-layouts: 151 us -> none
    pad x32 -> x1, local copies, waits for them, and re-layouts: 117 us -> 0.02 us  [padded_table(): jnp.pad(rel_table.astype(jnp.bfloat16), ((0, LANES - BUCKETS), (0, 0)))]
    dot_general x48 -> x8, matrix products: 131 us -> 56.9 us  [times_transposed(): lax.dot_general(former, latter, (((1,), (1,)), ((), ())), preferred_eleme...]
    pallas_call x0 -> x2, Pallas kernels: none -> 73.8 us  [the longest x1 48.2 us: attend_back(): pl.pallas_call(attend_back_kernel, grid=(clips, pairs), in_specs=[block,...]
    all_gather x1, waiting for transfers between devices: 0.01 us -> 63.9 us  [body(): lax.all_gather(ffn2_down.astype(jnp.bfloat16), 'fsdp', axis=0, tiled=True)]
    conv_general_dilated x3, matrix products: 59.1 us -> 118 us  [depthwise(): lax.conv_general_dilated(wide_rows, kernel_now[:, None, :], (1,), 'VALID'...]
  transfers between devices with their start and end apart: 35 -> 35, of which waited for: 21 -> 24; matrix products, arithmetic and copies ran while one was open for 49% -> 22% of each run, Pallas kernels for 0% -> 4%
where the time goes in v1:
time: 2100 us; the launch traced here: 2090 us
  waiting for transfers between devices  1430 us (68%)
  matrix products  298 us (14%)
  local copies, waits for them, and re-layouts  118 us (6%)
  other arithmetic  109 us (5%)
  Pallas kernels  73.8 us (4%)
  starting transfers between devices  34 us (2%)
    psum x2, waiting for transfers between devices, body(): lax.psum((gains_stack, shifts_stack, hidden_stack, model_stack, kernel_gr...  206 us
    conv_general_dilated x3, matrix products, depthwise(): lax.conv_general_dilated(wide_rows, kernel_now[:, None, :], (1,), 'VALID'...  118 us
    reduce_scatter x1, waiting for transfers between devices, body(): lax.psum_scatter(down_two_grad.astype(jnp.bfloat16), 'seq', scatter_dimen...  101 us
    reduce_scatter x1, waiting for transfers between devices, body(): lax.psum_scatter(down_one_grad.astype(jnp.bfloat16), 'seq', scatter_dimen...  101 us
    reduce_scatter x1, waiting for transfers between devices, body(): lax.psum_scatter(up_one_grad.astype(jnp.bfloat16), 'seq', scatter_dimensi...  101 us
    reduce_scatter x1, waiting for transfers between devices, body(): lax.psum_scatter(up_two_grad.astype(jnp.bfloat16), 'seq', scatter_dimensi...  90.3 us
    reduce_scatter x1, waiting for transfers between devices, body(): lax.psum_scatter(partial_sums[6].astype(jnp.bfloat16), 'fsdp', scatter_di...  74.1 us
    reduce_scatter x1, waiting for transfers between devices, body(): lax.psum_scatter(partial_sums[0].astype(jnp.bfloat16), 'fsdp', scatter_di...  73.9 us
  transfers between devices with their start and end apart: 35, of which 24 were waited for; matrix products, arithmetic and copies ran while one was open for 22% of the time, Pallas kernels for 4%

profile of v1, /device:TPU:0, one launch (start us, length us, event | category | flops | bytes accessed | tf_op | source)
XLA Modules:
  0.0 2091.3 jit_solution(1695476761786740704)
XLA Ops:
  17.5 70.9 %all-gather.9.cloned.1.call-done = bf16[1024,4096]{1,0:T(8,128)(2,1)} async-done(((bf16[64,4096]{1,0:T(8,128)(2,1)}), bf16[1024,4096]{1,0:T(8,128)(2,1)}) %all-gather.9.cloned.1.call-update) | async-done | bytes 8388624 | tf_op jit(solution)/shard_map/all_gather | solution.py:314
  98.8 65.6 %all-gather.11.cloned.1.call-done = bf16[4096,1024]{1,0:T(8,128)(2,1)} async-done(((bf16[256,1024]{1,0:T(8,128)(2,1)}), bf16[4096,1024]{1,0:T(8,128)(2,1)}) %all-gather.11.cloned.1.call-update) | async-done | bytes 8388624 | tf_op jit(solution)/shard_map/all_gather | solution.py:315
  174.5 52.8 %all-gather.13.cloned.1.call-done = bf16[1024,3072]{1,0:T(8,128)(2,1)} async-done(((bf16[64,3072]{1,0:T(8,128)(2,1)}), bf16[1024,3072]{1,0:T(8,128)(2,1)}) %all-gather.13.cloned.1.call-update) | async-done | bytes 6291472 | tf_op jit(solution)/shard_map/all_gather | solution.py:316
  315.6 25.6 %attend.1 = (bf16[1,1024,512]{2,1,0:T(8,128)(2,1)S(1)}, f32[1,4,1024,2]{3,2,1,0:T(8,128)}) custom-call(bf16[1,1024,512]{2,1,0:T(8,128)(2,1)S(1)} %bitcast.232, bf16[1,1024,512]{2,1,0:T(8,128)(2,1)S(1)} %bitcast.234, bf16[1,1024,512]{2,1,0:T(8,128)(2,1)S(1)} %bitcast.236, bf16[128,64]{1,0:T(8,128)(2,1)S(1)} %pad.10.rel_ref), custom_call_target="tpu_custom_call" | custom-call | flops 8589934592 | bytes 4194304 | tf_op jit(solution)/shard_map/attend/pallas_call | solution.py:221
  350.8 15.9 all_to_all.141
  386.9 42.2 %fusion.92 = (f32[512]{0:T(512)S(1)}, f32[1,512,1024]{2,0,1:T(1,128)S(1)}) fusion(f32[31,1,1024]{2,0,1:T(8,128)S(1)} %bitcast.275, bf16[1,542,1024]{2,1,0:T(8,128)(2,1)S(1)} %pad_maximum_fusion), kind=kOutput, calls=%fused_computation.190 | convolution fusion | flops 195558912 | bytes 3336192 | tf_op jit(solution)/shard_map/jvp()/conv_general_dilated | solution.py:58
  452.9 63.9 %all-gather.23.cloned.1.call-done = bf16[4096,1024]{1,0:T(8,128)(2,1)} async-done(((bf16[256,1024]{1,0:T(8,128)(2,1)}), bf16[4096,1024]{1,0:T(8,128)(2,1)}) %all-gather.23.cloned.1.call-update) | async-done | bytes 8388624 | tf_op jit(solution)/shard_map/all_gather | solution.py:321
  565.2 26.7 %fusion.18 = f32[1,512,1024]{2,0,1:T(1,128)S(1)} fusion(bf16[1,542,1024]{2,1,0:T(8,128)(2,1)S(1)} %pad_maximum_fusion.1, f32[31,1,1024]{2,0,1:T(8,128)S(1)} %bitcast.276), kind=kOutput, calls=%fused_computation.46 | convolution fusion | flops 195035136 | bytes 3334144 | tf_op jit(solution)/shard_map/conv_general_dilated | solution.py:58
  652.3 48.2 %attend_back.1 = (bf16[1,1024,512]{2,1,0:T(8,128)(2,1)S(1)}, bf16[1,1024,512]{2,1,0:T(8,128)(2,1)S(1)}, bf16[1,1024,512]{2,1,0:T(8,128)(2,1)S(1)}, f32[1,4,64,128]{3,2,1,0:T(8,128)S(1)}) custom-call(bf16[1,1024,512]{2,1,0:T(8,128)(2,1)S(1)} %bitcast.233, bf16[1,1024,512]{2,1,0:T(8,128)(2,1)S(1)} %bitcast.235, bf16[1,1024,512]{2,1,0:T(8,128)(2,1)} %bitcast.237, ...), custom_call_target="tpu_custom_call" | custom-call | flops 21474836480 | bytes 7340032 | tf_op jit(solution)/shard_map/attend_back/pallas_call | solution.py:241
  866.4 90.3 %reduce-scatter.41.cloned.1.call-done = bf16[1024,2048]{1,0:T(8,128)(2,1)} async-done(((bf16[1024,4096]{1,0:T(8,128)(2,1)}), bf16[1024,2048]{1,0:T(8,128)(2,1)}) %reduce-scatter.41.cloned.1.call-update) | async-done | bytes 4194320 | tf_op jit(solution)/shard_map/reduce_scatter | solution.py:478
  956.8 101.5 %reduce-scatter.45.cloned.1.call-done = bf16[4096,512]{1,0:T(8,128)(2,1)} async-done(((bf16[4096,1024]{1,0:T(8,128)(2,1)}), bf16[4096,512]{1,0:T(8,128)(2,1)}) %reduce-scatter.45.cloned.1.call-update) | async-done | bytes 4194320 | tf_op jit(solution)/shard_map/reduce_scatter | solution.py:481
  1058.3 101.3 %reduce-scatter.17.cloned.1.call-done = bf16[1024,2048]{1,0:T(8,128)(2,1)} async-done(((bf16[1024,4096]{1,0:T(8,128)(2,1)}), bf16[1024,2048]{1,0:T(8,128)(2,1)}) %reduce-scatter.17.cloned.1.call-update) | async-done | bytes 4194320 | tf_op jit(solution)/shard_map/reduce_scatter | solution.py:460
  1159.7 101.5 %reduce-scatter.21.cloned.1.call-done = bf16[4096,512]{1,0:T(8,128)(2,1)} async-done(((bf16[4096,1024]{1,0:T(8,128)(2,1)}), bf16[4096,512]{1,0:T(8,128)(2,1)}) %reduce-scatter.21.cloned.1.call-update) | async-done | bytes 4194320 | tf_op jit(solution)/shard_map/reduce_scatter | solution.py:463
  1261.5 49.4 %fusion.35 = f32[31,1,1024]{2,1,0:T(1,128)S(1)} fusion(bf16[1,512,1024]{2,1,0:T(8,128)(2,1)} %copy-done.30, bf16[1,542,1024]{2,1,0:T(8,128)(2,1)} %copy-done.36), kind=kOutput, calls=%fused_computation.70 | convolution fusion | flops 32505856 | bytes 2285568 | tf_op jit(solution)/shard_map/transpose(jvp())/conv_general_dilated | solution.py:58
  1314.9 79.1 %all-reduce.9.cloned.1.call-done = (f32[6,1024]{1,0:T(8,128)}, f32[6,1024]{1,0:T(8,128)}, f32[2,4096]{1,0:T(2,128)}, f32[5,1024]{1,0:T(8,128)}, f32[73,64]{0,1:T(8,128)}) async-done(((f32[6,1024]{1,0:T(8,128)}, f32[6,1024]{1,0:T(8,128)}, f32[2,4096]{1,0:T(2,128)}, f32[5,1024]{1,0:T(8,128)}, f32[73,64]{0,1:T(8,128)}), (f32[6,1024]{1,0:T(8,128)}, f32[6,1024]{1,0:T(8,128)}, f32[2,4096]{1,0:T(2,128)}, ...) | async-done | bytes 121104 | tf_op jit(solution)/shard_map/psum | solution.py:519
  1398.2 58.3 %reduce-scatter.39.cloned.1.call-done = bf16[64,512]{1,0:T(8,128)(2,1)} async-done(((bf16[1024,512]{1,0:T(8,128)(2,1)}), bf16[64,512]{1,0:T(8,128)(2,1)}) %reduce-scatter.39.cloned.1.call-update) | async-done | bytes 65552 | tf_op jit(solution)/shard_map/reduce_scatter | solution.py:501
  1458.0 59.0 %reduce-scatter.31.cloned.1.call-done = bf16[64,512]{1,0:T(8,128)(2,1)} async-done(((bf16[1024,512]{1,0:T(8,128)(2,1)}), bf16[64,512]{1,0:T(8,128)(2,1)}) %reduce-scatter.31.cloned.1.call-update) | async-done | bytes 65552 | tf_op jit(solution)/shard_map/reduce_scatter | solution.py:495
  1518.5 62.7 %reduce-scatter.35.cloned.1.call-done = bf16[64,1024]{1,0:T(8,128)(2,1)} async-done(((bf16[1024,1024]{1,0:T(8,128)(2,1)}), bf16[64,1024]{1,0:T(8,128)(2,1)}) %reduce-scatter.35.cloned.1.call-update) | async-done | bytes 131088 | tf_op jit(solution)/shard_map/reduce_scatter | solution.py:498
  1582.8 67.9 %reduce-scatter.27.cloned.1.call-done = bf16[64,1536]{1,0:T(8,128)(2,1)} async-done(((bf16[1024,1536]{1,0:T(8,128)(2,1)}), bf16[64,1536]{1,0:T(8,128)(2,1)}) %reduce-scatter.27.cloned.1.call-update) | async-done | bytes 196624 | tf_op jit(solution)/shard_map/reduce_scatter | solution.py:492
  1652.4 74.1 %reduce-scatter.43.cloned.1.call-done = bf16[64,2048]{1,0:T(8,128)(2,1)} async-done(((bf16[1024,2048]{1,0:T(8,128)(2,1)}), bf16[64,2048]{1,0:T(8,128)(2,1)}) %reduce-scatter.43.cloned.1.call-update) | async-done | bytes 262160 | tf_op jit(solution)/shard_map/reduce_scatter | solution.py:504
  1728.2 73.4 %reduce-scatter.47.cloned.1.call-done = bf16[256,512]{1,0:T(8,128)(2,1)} async-done(((bf16[4096,512]{1,0:T(8,128)(2,1)}), bf16[256,512]{1,0:T(8,128)(2,1)}) %reduce-scatter.47.cloned.1.call-update) | async-done | bytes 262160 | tf_op jit(solution)/shard_map/reduce_scatter | solution.py:507
  1803.4 73.9 %reduce-scatter.19.cloned.1.call-done = bf16[64,2048]{1,0:T(8,128)(2,1)} async-done(((bf16[1024,2048]{1,0:T(8,128)(2,1)}), bf16[64,2048]{1,0:T(8,128)(2,1)}) %reduce-scatter.19.cloned.1.call-update) | async-done | bytes 262160 | tf_op jit(solution)/shard_map/reduce_scatter | solution.py:486
  1879.1 73.5 %reduce-scatter.23.cloned.1.call-done = bf16[256,512]{1,0:T(8,128)(2,1)} async-done(((bf16[4096,512]{1,0:T(8,128)(2,1)}), bf16[256,512]{1,0:T(8,128)(2,1)}) %reduce-scatter.23.cloned.1.call-update) | async-done | bytes 262160 | tf_op jit(solution)/shard_map/reduce_scatter | solution.py:489
  1954.4 126.7 %all-reduce.7.cloned.1.call-done = f32[31,1024]{1,0:T(8,128)} async-done(((f32[31,1024]{1,0:T(8,128)}), f32[31,1024]{1,0:T(8,128)}) %all-reduce.7.cloned.1.call-update) | async-done | bytes 126992 | tf_op jit(solution)/shard_map/psum | solution.py:519
  (448 shorter events, 471.2 us)
Async XLA Ops:
  9.5 154.8 %all-gather.11.cloned.1.call-start = ((), (), s32[]{:S(2)}) async-start(), calls=%async_computation.25 | async-start | bytes 8912896 | tf_op jit(solution)/shard_map/all_gather | solution.py:315
  10.4 216.9 %all-gather.13.cloned.1.call-start = ((), (), s32[]{:S(2)}) async-start(), calls=%async_computation.26 | async-start | bytes 6684672 | tf_op jit(solution)/shard_map/all_gather | solution.py:316
  11.3 357.9 %all-gather.15.cloned.1.call-start = ((), (), s32[]{:S(2)}) async-start(), calls=%async_computation.27 | async-start | bytes 2228224 | tf_op jit(solution)/shard_map/all_gather | solution.py:317
  12.1 362.7 %all-gather.17.cloned.1.call-start = ((), (), s32[]{:S(2)}) async-start(), calls=%async_computation.28 | async-start | bytes 4456448 | tf_op jit(solution)/shard_map/all_gather | solution.py:318
  13.9 415.7 %all-gather.19.cloned.1.call-start = ((), (), s32[]{:S(2)}) async-start(), calls=%async_computation.29 | async-start | bytes 2228224 | tf_op jit(solution)/shard_map/all_gather | solution.py:319
  14.7 426.1 %all-gather.21.cloned.1.call-start = ((), (), s32[]{:S(2)}) async-start(), calls=%async_computation.30 | async-start | bytes 8912896 | tf_op jit(solution)/shard_map/all_gather | solution.py:320
  15.7 501.1 %all-gather.23.cloned.1.call-start = ((), (), s32[]{:S(2)}) async-start(), calls=%async_computation.31 | async-start | bytes 8912896 | tf_op jit(solution)/shard_map/all_gather | solution.py:321
  293.8 569.9 %reduce-scatter.37.cloned.1.call-start = ((), (), s32[]{:S(2)}) async-start(), calls=%async_computation.42 | async-start | bytes 3145728 | tf_op jit(solution)/shard_map/reduce_scatter | solution.py:475
  563.4 301.0 %reduce-scatter.29.cloned.1.call-start = ((), (), s32[]{:S(2)}) async-start(), calls=%async_computation.38 | async-start | bytes 3145728 | tf_op jit(solution)/shard_map/reduce_scatter | solution.py:469
  605.3 259.8 %reduce-scatter.33.cloned.1.call-start = ((), (), s32[]{:S(2)}) async-start(), calls=%async_computation.40 | async-start | bytes 6291456 | tf_op jit(solution)/shard_map/reduce_scatter | solution.py:472
  776.6 180.1 %reduce-scatter.41.cloned.1.call-start = ((), (), s32[]{:S(2)}) async-start(), calls=%async_computation.44 | async-start | bytes 12582912 | tf_op jit(solution)/shard_map/reduce_scatter | solution.py:478
  788.1 270.2 %reduce-scatter.45.cloned.1.call-start = ((), (), s32[]{:S(2)}) async-start(), calls=%async_computation.46 | async-start | bytes 12582912 | tf_op jit(solution)/shard_map/reduce_scatter | solution.py:481
  800.4 359.2 %reduce-scatter.17.cloned.1.call-start = ((), (), s32[]{:S(2)}) async-start(), calls=%async_computation.32 | async-start | bytes 12582912 | tf_op jit(solution)/shard_map/reduce_scatter | solution.py:460
  834.9 426.3 %reduce-scatter.21.cloned.1.call-start = ((), (), s32[]{:S(2)}) async-start(), calls=%async_computation.34 | async-start | bytes 12582912 | tf_op jit(solution)/shard_map/reduce_scatter | solution.py:463
  847.5 546.5 %all-reduce.9.cloned.1.call-start = ((), (), s32[]{:S(2)}) async-start(), calls=%async_computation.49 | async-start | bytes 327680 | tf_op jit(solution)/shard_map/psum | solution.py:519
  863.7 592.8 %reduce-scatter.39.cloned.1.call-start = ((), (), s32[]{:S(2)}) async-start(), calls=%async_computation.43 | async-start | bytes 1114112 | tf_op jit(solution)/shard_map/reduce_scatter | solution.py:501
  864.3 652.7 %reduce-scatter.31.cloned.1.call-start = ((), (), s32[]{:S(2)}) async-start(), calls=%async_computation.39 | async-start | bytes 1114112 | tf_op jit(solution)/shard_map/reduce_scatter | solution.py:495
  865.0 716.2 %reduce-scatter.35.cloned.1.call-start = ((), (), s32[]{:S(2)}) async-start(), calls=%async_computation.41 | async-start | bytes 2228224 | tf_op jit(solution)/shard_map/reduce_scatter | solution.py:498
  865.6 785.1 %reduce-scatter.27.cloned.1.call-start = ((), (), s32[]{:S(2)}) async-start(), calls=%async_computation.37 | async-start | bytes 3342336 | tf_op jit(solution)/shard_map/reduce_scatter | solution.py:492
  866.3 860.1 %reduce-scatter.43.cloned.1.call-start = ((), (), s32[]{:S(2)}) async-start(), calls=%async_computation.45 | async-start | bytes 4456448 | tf_op jit(solution)/shard_map/reduce_scatter | solution.py:504
  956.8 844.9 %reduce-scatter.47.cloned.1.call-start = ((), (), s32[]{:S(2)}) async-start(), calls=%async_computation.47 | async-start | bytes 4456448 | tf_op jit(solution)/shard_map/reduce_scatter | solution.py:507
  1058.3 819.1 %reduce-scatter.19.cloned.1.call-start = ((), (), s32[]{:S(2)}) async-start(), calls=%async_computation.33 | async-start | bytes 4456448 | tf_op jit(solution)/shard_map/reduce_scatter | solution.py:486
  1159.7 792.9 %reduce-scatter.23.cloned.1.call-start = ((), (), s32[]{:S(2)}) async-start(), calls=%async_computation.35 | async-start | bytes 4456448 | tf_op jit(solution)/shard_map/reduce_scatter | solution.py:489
  1261.2 819.8 %all-reduce.7.cloned.1.call-start = ((), (), s32[]{:S(2)}) async-start(), calls=%async_computation.48 | async-start | bytes 262144 | tf_op jit(solution)/shard_map/psum | solution.py:519
  (110 other events, 4561.9 us)
Sparse Core Ops, SparseCore 0:
  10.8 77.5 all-gather.8
  91.1 73.1 all-gather.10
  167.2 60.0 all-gather.12
  229.9 40.0 all-gather.14
  272.6 49.2 all-gather.16
  324.5 39.8 all-gather.18
  367.1 73.6 all-gather.20
  443.6 73.1 all-gather.22
  637.3 56.2 reduce-scatter.32
  776.8 78.3 reduce-scatter.24
  857.5 99.2 reduce-scatter.40
  959.0 99.2 reduce-scatter.44
  1060.4 99.2 reduce-scatter.16
  1161.9 99.2 reduce-scatter.20
  1269.2 124.8 all-reduce.8
  1397.5 58.9 reduce-scatter.38
  1460.5 56.3 reduce-scatter.30
  1520.5 60.5 reduce-scatter.34
  1585.5 65.1 reduce-scatter.26
  1655.0 71.3 reduce-scatter.42
  1730.3 71.2 reduce-scatter.46
  1805.8 71.4 reduce-scatter.18
  1881.2 71.3 reduce-scatter.22
  1959.5 121.5 all-reduce.6
  (2 shorter events, 60.8 us)

commit v2 on v1

v2 whole, which is shorter than its diff:
```python
import functools
from functools import partial

import jax
import jax.numpy as jnp
from jax import lax
from jax.experimental import pallas as pl
from jax.experimental.pallas import tpu as pltpu
from jax.sharding import PartitionSpec as P

HEAD = 64
KERNEL = 31
LEFT = 64
RIGHT = 8
BUCKETS = 73


EPSILON = 1e-05


def passed_along(value, axis, by):
    length = lax.axis_size(axis)
    pairs = [(i, i + by) for i in range(length) if 0 <= i + by < length]
    return lax.ppermute(value, axis, pairs)


def layer_norm(values, norm_gain, norm_shift):
    center = values - jnp.mean(values, axis=-1, keepdims=True)
    spread = jnp.mean(center * center, axis=-1, keepdims=True)
    return center * lax.rsqrt(spread + EPSILON) * norm_gain + norm_shift


def product(former, latter):
    return jnp.dot(former, latter, preferred_element_type=jnp.float32)


def contract_rows(former, latter):
    return lax.dot_general(
        former, latter, (((0,), (0,)), ((), ())), preferred_element_type=jnp.float32
    )


def times_transposed(former, latter):
    return lax.dot_general(
        former, latter, (((1,), (1,)), ((), ())), preferred_element_type=jnp.float32
    )


def glu_function(gate_input):
    half_width = gate_input.shape[1] // 2
    return gate_input[:, :half_width] * jax.nn.sigmoid(gate_input[:, half_width:])


def conv_tail(mixed_rows, norm_gain, norm_shift):
    return jax.nn.silu(layer_norm(mixed_rows, norm_gain, norm_shift))


def depthwise(wide_rows, kernel_now):
    return lax.conv_general_dilated(
        wide_rows,
        kernel_now[:, None, :],
        (1,),
        "VALID",
        dimension_numbers=("NWC", "WIO", "NWC"),
        feature_group_count=wide_rows.shape[2],
        precision=lax.Precision.HIGHEST,
    )


MESH = pl.DeviceIdType.MESH
PIECE = 512


class Place:
    def __init__(self):
        self.x = lax.axis_index("seq")
        self.f = lax.axis_index("fsdp")
        self.c = lax.rem(self.f, 2)
        self.y = lax.rem(lax.div(self.f, 2), 2)
        self.z = lax.div(self.f, 4)

    def across(self):
        return (1 - self.x, self.f)

    def twin(self):
        return (self.x, self.f + 1 - 2 * self.c)

    def beside(self):
        return (self.x, self.f + 2 - 4 * self.y)

    def along(self, step):
        return (self.x, lax.rem(self.z + step, 4) * 4 + self.y * 2 + self.c)

    def greet(self):
        barrier = pltpu.get_barrier_semaphore()
        peers = [self.across(), self.twin(), self.beside()] + [self.along(s) for s in (1, 2, 3)]
        for peer in peers:
            pl.semaphore_signal(barrier, inc=1, device_id=peer, device_id_type=MESH)
        pl.semaphore_wait(barrier, len(peers))


def chunks_of(shapes, lines):
    found = []
    for index, (rows, width) in enumerate(shapes):
        for line in range(0, rows, lines):
            for column in range(0, width // 2, PIECE):
                found.append((index, line, column, len(found) % 3 != 2))
    return found


class Sent:
    def __init__(self, source, target, send_sem, recv_sem, device):
        self.parts = dict(src_ref=source, dst_ref=target, send_sem=send_sem, recv_sem=recv_sem, device_id=device, device_id_type=MESH)

    def start(self):
        pltpu.make_async_remote_copy(**self.parts).start()

    def wait_recv(self):
        pltpu.make_async_remote_copy(**self.parts).wait_recv()

    def wait_send(self):
        pltpu.make_async_remote_copy(**self.parts).wait_send()


def send(source, target, send_sem, recv_sem, device):
    copy = Sent(source, target, send_sem, recv_sem, device)
    copy.start()
    return copy


def gather_kernel(count, chunks, lines, *refs):
    shards, wholes = refs[:count], refs[count : 2 * count]
    own_sem, z_send, z_recv, y_send, y_recv, x_send, x_recv, c_send, c_recv = refs[2 * count :]
    me = Place()
    me.greet()
    live = {}

    def halves(chunk):
        index, line, column, early = chunk
        half = shards[index].shape[1] // 2
        if early:
            return [pl.ds(pl.multiple_of(me.x * half + column, PIECE), PIECE)]
        return [pl.ds(column, PIECE), pl.ds(half + column, PIECE)]

    def both(chunk):
        half = shards[chunk[0]].shape[1] // 2
        return [pl.ds(chunk[2], PIECE), pl.ds(half + chunk[2], PIECE)]

    def first(t):
        index, line, column, early = chunks[t]
        shard, whole = shards[index], wholes[index]
        rows = pl.ds(line, lines)
        live[t, "own"] = []
        for j, cols in enumerate(halves(chunks[t])):
            copy = pltpu.make_async_copy(shard.at[rows, cols], whole.at[me.z, me.y, me.c, rows, cols], own_sem.at[t, j])
            copy.start()
            live[t, "own"].append(copy)
        live[t, "z"] = [
            send(shard.at[rows, cols], whole.at[me.z, me.y, me.c, rows, cols], z_send.at[t, j, s - 1], z_recv.at[t, j, s - 1], me.along(s))
            for j, cols in enumerate(halves(chunks[t]))
            for s in (1, 2, 3)
        ]

    def second(t):
        index, line, column, early = chunks[t]
        whole, rows = wholes[index], pl.ds(line, lines)
        for copy in live[t, "own"]:
            copy.wait()
        for copy in live[t, "z"]:
            copy.wait_recv()
        live[t, "y"] = [
            send(whole.at[:, me.y, me.c, rows, cols], whole.at[:, me.y, me.c, rows, cols], y_send.at[t, j], y_recv.at[t, j], me.beside())
            for j, cols in enumerate(halves(chunks[t]))
        ]

    def third(t):
        index, line, column, early = chunks[t]
        whole, rows = wholes[index], pl.ds(line, lines)
        for copy in live[t, "y"]:
            copy.wait_recv()
        if early:
            (cols,) = halves(chunks[t])
            view = whole.at[:, :, me.c, rows, cols]
            live[t, "x"] = [send(view, view, x_send.at[t], x_recv.at[t], me.across())]
        else:
            live[t, "x"] = []

    def fourth(t):
        index, line, column, early = chunks[t]
        whole, rows = wholes[index], pl.ds(line, lines)
        for copy in live[t, "x"]:
            copy.wait_recv()
        live[t, "c"] = [
            send(whole.at[:, :, me.c, rows, cols], whole.at[:, :, me.c, rows, cols], c_send.at[t, j], c_recv.at[t, j], me.twin())
            for j, cols in enumerate(both(chunks[t]))
        ]

    total = len(chunks)
    for step in range(total + 3):
        for lag, phase in enumerate((first, second, third, fourth)):
            if 0 <= step - lag < total:
                phase(step - lag)
    for t in range(total):
        for copy in live[t, "c"]:
            copy.wait_recv()
        for kind in "zyxc":
            for copy in live[t, kind]:
                copy.wait_send()


def gather_whole(shards, identity):
    shapes = [shard.shape for shard in shards]
    lines = min(rows for rows, _ in shapes)
    chunks = chunks_of(shapes, lines)
    count, total = len(shards), len(chunks)
    dma = pltpu.SemaphoreType.DMA
    anywhere = pl.BlockSpec(memory_space=pl.ANY)
    wholes = pl.pallas_call(
        functools.partial(gather_kernel, count, chunks, lines),
        in_specs=[anywhere] * count,
        out_specs=[anywhere] * count,
        out_shape=[jax.ShapeDtypeStruct((4, 2, 2, *shape), jnp.bfloat16) for shape in shapes],
        scratch_shapes=[
            dma((total, 2)), dma((total, 2, 3)), dma((total, 2, 3)), dma((total, 2)), dma((total, 2)),
            dma((total,)), dma((total,)), dma((total, 2)), dma((total, 2)),
        ],
        compiler_params=pltpu.CompilerParams(collective_id=identity, has_side_effects=True, vmem_limit_bytes=4 << 20),
        name="gather_whole",
    )(*shards)
    return [whole.reshape(-1, whole.shape[-1]) for whole in wholes]


SLOTS = 6


def scatter_kernel(count, chunks, lines, *refs):
    grads, small, outs, small_out = refs[:count], refs[count], refs[count + 1 : 2 * count + 1], refs[2 * count + 1]
    (held, core_in, early_in, late_in, mid_in, end_in, done, load_sem, done_sem,
     c_send, c_recv, x_send, x_recv, y_send, y_recv, z_send, z_recv,
     small_held, small_in, small_z, small_send, small_recv, small_z_send, small_z_recv) = refs[2 * count + 2 :]
    me = Place()
    me.greet()
    live = {}
    order = [sum(other[3] == chunk[3] for other in chunks[:t]) for t, chunk in enumerate(chunks)]

    def columns(chunk, j):
        return pl.ds(j * (grads[chunk[0]].shape[-1] // 2) + chunk[2], PIECE)

    def sums(former, latter):
        return (former.astype(jnp.float32) + latter.astype(jnp.float32)).astype(jnp.bfloat16)

    def first(t):
        index, line, column, early = chunks[t]
        grad, rows, slot = grads[index], pl.ds(line, lines), t % SLOTS
        if t >= SLOTS:
            for kind in "zyx":
                for copy in live[t - SLOTS, kind]:
                    copy.wait_send()
        live[t, "c"], live[t, "load"] = [], []
        for j in range(2):
            cols = columns(chunks[t], j)
            live[t, "c"].append(send(grad.at[:, :, 1 - me.c, rows, cols], core_in.at[t, j], c_send.at[t, j], c_recv.at[t, j], me.twin()))
            load = pltpu.make_async_copy(grad.at[:, :, me.c, rows, cols], held.at[slot, j], load_sem.at[t, j])
            load.start()
            live[t, "load"].append(load)

    def second(t):
        early, slot = chunks[t][3], t % SLOTS
        for j in range(2):
            live[t, "load"][j].wait()
            live[t, "c"][j].wait_recv()
            for z in range(4):
                held[slot, j, z] = sums(held[slot, j, z], core_in[t, j, z])
        if early:
            live[t, "x"] = [send(held.at[slot, 1 - me.x], early_in.at[order[t]], x_send.at[t], x_recv.at[t], me.across())]
        else:
            live[t, "y"] = [send(held.at[slot, :, :, 1 - me.y], late_in.at[order[t]], y_send.at[t], y_recv.at[t], me.beside())]

    def third(t):
        early, slot = chunks[t][3], t % SLOTS
        if early:
            live[t, "x"][0].wait_recv()
            for z in range(4):
                held[slot, me.x, z] = sums(held[slot, me.x, z], early_in[order[t], z])
            live[t, "y"] = [send(held.at[slot, me.x, :, 1 - me.y], mid_in.at[t, 0], y_send.at[t], y_recv.at[t], me.beside())]
        else:
            live[t, "y"][0].wait_recv()
            for j in range(2):
                for z in range(4):
                    held[slot, j, z, me.y] = sums(held[slot, j, z, me.y], late_in[order[t], j, z])
            live[t, "z"] = [
                send(held.at[slot, :, lax.rem(me.z + s, 4), me.y], mid_in.at[t, s - 1, 0:2], z_send.at[t, s - 1], z_recv.at[t, s - 1], me.along(s))
                for s in (1, 2, 3)
            ]

    def fourth(t):
        early, slot = chunks[t][3], t % SLOTS
        if early:
            live[t, "y"][0].wait_recv()
            for z in range(4):
                held[slot, me.x, z, me.y] = sums(held[slot, me.x, z, me.y], mid_in[t, 0, z])
            live[t, "z"] = [
                send(held.at[slot, me.x, lax.rem(me.z + s, 4), me.y], end_in.at[t, s - 1], z_send.at[t, s - 1], z_recv.at[t, s - 1], me.along(s))
                for s in (1, 2, 3)
            ]
        else:
            for copy in live[t, "z"]:
                copy.wait_recv()
            for j in range(2):
                value = held[slot, j, me.z, me.y].astype(jnp.float32)
                for s in range(3):
                    value = value + mid_in[t, s, j].astype(jnp.float32)
                held[slot, j, me.z, me.y] = value.astype(jnp.bfloat16)
            live[t, "x"] = [send(held.at[slot, 1 - me.x, me.z, me.y], end_in.at[t, 0], x_send.at[t], x_recv.at[t], me.across())]

    def fifth(t):
        index, line, column, early = chunks[t]
        slot = t % SLOTS
        value = held[slot, me.x, me.z, me.y].astype(jnp.float32)
        if early:
            for copy in live[t, "z"]:
                copy.wait_recv()
            for s in range(3):
                value = value + end_in[t, s].astype(jnp.float32)
        else:
            live[t, "x"][0].wait_recv()
            value = value + end_in[t, 0].astype(jnp.float32)
        done[t] = value
        copy = pltpu.make_async_copy(done.at[t], outs[index].at[pl.ds(line, lines), pl.ds(column, PIECE)], done_sem.at[t])
        copy.start()
        live[t, "done"] = [copy]

    def small_step(stage):
        if stage > 0:
            live["small", stage - 1].wait_recv()
            small_held[stage] = small_held[stage - 1] + small_in[stage - 1]
        if stage < 3:
            peer = (me.twin, me.across, me.beside)[stage]()
            live["small", stage] = send(small_held.at[stage], small_in.at[stage], small_send.at[stage], small_recv.at[stage], peer)
        else:
            small_z[me.z] = small_held[3]
            for s in (1, 2, 3):
                live["small z", s] = send(small_held.at[3], small_z.at[me.z], small_z_send.at[s - 1], small_z_recv.at[s - 1], me.along(s))

    def small_end():
        for s in (1, 2, 3):
            live["small z", s].wait_recv()
            live["small z", s].wait_send()
            live["small", s - 1].wait_send()
        small_out[...] = (small_z[0] + small_z[1]) + (small_z[2] + small_z[3])

    total = len(chunks)
    small_held[0] = small[...]
    for step in range(total + 4):
        if step < 4:
            small_step(step)
        for lag, phase in enumerate((first, second, third, fourth, fifth)):
            if 0 <= step - lag < total:
                phase(step - lag)
    small_end()
    for t in range(total):
        live[t, "done"][0].wait()
        for copy in live[t, "c"]:
            copy.wait_send()
        if t + SLOTS >= total:
            for kind in "zyx":
                for copy in live[t, kind]:
                    copy.wait_send()


def scatter_sums(grads, small, identity):
    shapes = [(grad.shape[0] // 16, grad.shape[1]) for grad in grads]
    lines = min(rows for rows, _ in shapes)
    chunks = chunks_of(shapes, lines)
    count, total = len(grads), len(chunks)
    dma = pltpu.SemaphoreType.DMA
    anywhere = pl.BlockSpec(memory_space=pl.ANY)
    low = jnp.bfloat16
    early_count = sum(chunk[3] for chunk in chunks)
    return pl.pallas_call(
        functools.partial(scatter_kernel, count, chunks, lines),
        in_specs=[anywhere] * count + [pl.BlockSpec(memory_space=pltpu.VMEM)],
        out_specs=[anywhere] * count + [pl.BlockSpec(memory_space=pltpu.VMEM)],
        out_shape=[jax.ShapeDtypeStruct((rows, width // 2), jnp.float32) for rows, width in shapes]
        + [jax.ShapeDtypeStruct(small.shape, jnp.float32)],
        scratch_shapes=[
            pltpu.VMEM((SLOTS, 2, 4, 2, lines, PIECE), low),
            pltpu.VMEM((total, 2, 4, 2, lines, PIECE), low),
            pltpu.VMEM((max(1, early_count), 4, 2, lines, PIECE), low),
            pltpu.VMEM((max(1, total - early_count), 2, 4, lines, PIECE), low),
            pltpu.VMEM((total, 3, 4, lines, PIECE), low),
            pltpu.VMEM((total, 3, lines, PIECE), low),
            pltpu.VMEM((total, lines, PIECE), jnp.float32),
            dma((total, 2)), dma((total,)),
            dma((total, 2)), dma((total, 2)), dma((total,)), dma((total,)),
            dma((total,)), dma((total,)), dma((total, 3)), dma((total, 3)),
            pltpu.VMEM((4, *small.shape), jnp.float32), pltpu.VMEM((3, *small.shape), jnp.float32), pltpu.VMEM((4, *small.shape), jnp.float32),
            dma((3,)), dma((3,)), dma((3,)), dma((3,)),
        ],
        compiler_params=pltpu.CompilerParams(collective_id=identity, has_side_effects=True, vmem_limit_bytes=60 << 20),
        name="scatter_sums",
    )(*[grad.reshape(4, 2, 2, *shape) for grad, shape in zip(grads, shapes)], small)


PAIR = 2
LANES = 128
FWD_ROWS = 256
BACK_ROWS = 256


def nt(former, latter):
    return lax.dot_general(former, latter, (((1,), (1,)), ((), ())), preferred_element_type=jnp.float32)


def nn(former, latter):
    return lax.dot_general(former, latter, (((1,), (0,)), ((), ())), preferred_element_type=jnp.float32)


def window_of(start, rows, length):
    low, high = start - LANES, start + rows + LANES
    return max(low, 0), min(high, length), max(low, 0) - low


def window_buckets(rows):
    width = rows + 2 * LANES
    places = lax.broadcasted_iota(jnp.int32, (rows, width), 1)
    lines = lax.broadcasted_iota(jnp.int32, (rows, width), 0)
    return places - lines - (LANES - LEFT)


def biased_scores(scores, position, start, rows, length):
    width = rows + 2 * LANES
    low, high, skip = window_of(start, rows, length)
    wide = jnp.concatenate([position, jnp.zeros((rows, width - LANES), jnp.float32)], axis=1)
    band = pltpu.roll(wide, LANES - LEFT, 1, stride=1, stride_axis=0)
    first, last = position[:, 0:1], position[:, BUCKETS - 1 : BUCKETS]
    bucket = window_buckets(rows)
    band = jnp.where(bucket <= 0, first, jnp.where(bucket >= BUCKETS - 1, last, band))
    pieces = []
    if low > 0:
        pieces.append(scores[:, :low] + first)
    pieces.append(scores[:, low:high] + band[:, skip : skip + high - low])
    if high < length:
        pieces.append(scores[:, high:] + last)
    return pieces[0] if len(pieces) == 1 else jnp.concatenate(pieces, axis=1)


def bucket_sums(score_grad, mirror, start, rows, length):
    width = rows + 2 * LANES
    low, high, skip = window_of(start, rows, length)
    inner = score_grad[:, low:high]
    pieces = []
    if skip > 0:
        pieces.append(jnp.zeros((rows, skip), jnp.float32))
    pieces.append(inner)
    if skip + high - low < width:
        pieces.append(jnp.zeros((rows, width - skip - high + low), jnp.float32))
    wide = pieces[0] if len(pieces) == 1 else jnp.concatenate(pieces, axis=1)
    bucket = window_buckets(rows)
    first = jnp.sum(jnp.where(bucket <= 0, wide, 0.0), axis=1, keepdims=True)
    last = jnp.sum(jnp.where(bucket >= BUCKETS - 1, wide, 0.0), axis=1, keepdims=True)
    if low > 0:
        first = first + jnp.sum(score_grad[:, :low], axis=1, keepdims=True)
    if high < length:
        last = last + jnp.sum(score_grad[:, high:], axis=1, keepdims=True)
    turned = nn(wide.astype(jnp.bfloat16), mirror)
    band = pltpu.roll(turned, (LANES + LANES - LEFT) % width, 1, stride=1, stride_axis=0)[:, :LANES]
    bucket = LANES - 1 - lax.broadcasted_iota(jnp.int32, (rows, LANES), 1)
    return jnp.where(bucket == 0, first, jnp.where(bucket == BUCKETS - 1, last, jnp.where(bucket < BUCKETS, band, 0.0)))


def mirror_of(width):
    lines = lax.broadcasted_iota(jnp.int32, (width, width), 0)
    places = lax.broadcasted_iota(jnp.int32, (width, width), 1)
    return jnp.where(lines + places == width - 1, 1.0, 0.0).astype(jnp.bfloat16)


def attend_pair(q_ref, k_ref, v_ref, rel_ref, out_ref, log_ref):
    length = q_ref.shape[0]
    rows = min(FWD_ROWS, length)
    scale = HEAD ** (-0.5)
    rel = rel_ref[...]
    for start in range(0, length, rows):
        outs, logs = [], []
        for h in range(PAIR):
            lanes = slice(h * HEAD, (h + 1) * HEAD)
            query = q_ref[start : start + rows, lanes] * scale
            scores = nt(query, k_ref[:, lanes])
            scores = biased_scores(scores, nt(query, rel), start, rows, length)
            highest = jnp.max(scores, axis=1, keepdims=True)
            weights = jnp.exp(scores - highest)
            total = jnp.sum(weights, axis=1, keepdims=True)
            outs.append(nn(weights.astype(jnp.bfloat16), v_ref[:, lanes]) / total)
            logs.append(highest + jnp.log(total))
        out_ref[start : start + rows, :] = jnp.concatenate(outs, axis=1).astype(jnp.bfloat16)
        log_ref[start : start + rows, :] = jnp.concatenate(logs, axis=1)


def attend_back_pair(
    q_ref, k_ref, v_ref, do_ref, log_ref, rel_ref, back_ref, mirror_ref, dq_ref, dk_ref, dv_ref, table_ref, dkt, dvt
):
    length = q_ref.shape[0]
    rows = min(BACK_ROWS, length)
    scale = HEAD ** (-0.5)
    rel, back = rel_ref[...], back_ref[...]
    q_turned = (jnp.transpose(q_ref[...].astype(jnp.float32)) * scale).astype(jnp.bfloat16)
    do_turned = jnp.transpose(do_ref[...].astype(jnp.float32)).astype(jnp.bfloat16)
    table = jnp.zeros((HEAD, LANES), jnp.float32)
    for start in range(0, length, rows):
        span = slice(start, start + rows)
        parts = []
        for h in range(PAIR):
            lanes = slice(h * HEAD, (h + 1) * HEAD)
            query = q_ref[span, lanes] * scale
            scores = nt(query, k_ref[:, lanes])
            scores = biased_scores(scores, nt(query, rel), start, rows, length)
            weights = jnp.exp(scores - log_ref[span, h : h + 1])
            low_weights = weights.astype(jnp.bfloat16)
            grads = nt(do_ref[span, lanes], v_ref[:, lanes])
            both = weights * grads
            delta = jnp.sum(both, axis=1, keepdims=True)
            score_grad = (both - weights * delta).astype(jnp.bfloat16)
            value_part = nn(do_turned[lanes, span], low_weights)
            key_part = nn(q_turned[lanes, span], score_grad)
            if start == 0:
                dvt[lanes, :] = value_part
                dkt[lanes, :] = key_part
            else:
                dvt[lanes, :] += value_part
                dkt[lanes, :] += key_part
            bucket = bucket_sums(score_grad.astype(jnp.float32), mirror_ref[...], start, rows, length)
            high = bucket.astype(jnp.bfloat16)
            rest = (bucket - high.astype(jnp.float32)).astype(jnp.bfloat16)
            parts.append((nn(score_grad, k_ref[:, lanes]) + nn(high, back) + nn(rest, back)) * scale)
            table = table + nn(q_turned[lanes, span], high) + nn(q_turned[lanes, span], rest)
        dq_ref[span, :] = jnp.concatenate(parts, axis=1).astype(jnp.bfloat16)
    dk_ref[...] = jnp.transpose(dkt[...]).astype(jnp.bfloat16)
    dv_ref[...] = jnp.transpose(dvt[...]).astype(jnp.bfloat16)
    table_ref[...] = table


def attend_kernel(q_ref, k_ref, v_ref, rel_ref, out_ref, log_ref):
    attend_pair(q_ref.at[0], k_ref.at[0], v_ref.at[0], rel_ref, out_ref.at[0], log_ref.at[0, 0])


def attend_back_kernel(
    q_ref, k_ref, v_ref, do_ref, log_ref, rel_ref, back_ref, mirror_ref, dq_ref, dk_ref, dv_ref, table_ref, dkt, dvt
):
    attend_back_pair(
        q_ref.at[0], k_ref.at[0], v_ref.at[0], do_ref.at[0], log_ref.at[0, 0], rel_ref, back_ref, mirror_ref,
        dq_ref.at[0], dk_ref.at[0], dv_ref.at[0], table_ref.at[0, 0], dkt, dvt,
    )


def width_of(length):
    return min(BACK_ROWS, length) + 2 * LANES


def head_block(length):
    return pl.BlockSpec((1, length, PAIR * HEAD), lambda i, j: (i, 0, j))


def padded_table(rel_table):
    return jnp.pad(rel_table.astype(jnp.bfloat16), ((0, LANES - BUCKETS), (0, 0)))


def attend(query, key, value, rel_low):
    clips, length, width = query.shape
    pairs = width // (PAIR * HEAD)
    block = head_block(length)
    return pl.pallas_call(
        attend_kernel,
        grid=(clips, pairs),
        in_specs=[block, block, block, pl.BlockSpec((LANES, HEAD), lambda i, j: (0, 0))],
        out_specs=[block, pl.BlockSpec((1, 1, length, PAIR), lambda i, j: (i, j, 0, 0))],
        out_shape=[
            jax.ShapeDtypeStruct(query.shape, jnp.bfloat16),
            jax.ShapeDtypeStruct((clips, pairs, length, PAIR), jnp.float32),
        ],
        compiler_params=pltpu.CompilerParams(vmem_limit_bytes=48 << 20),
        cost_estimate=pl.CostEstimate(flops=4 * clips * width * length * length * 4, bytes_accessed=8 * query.size, transcendentals=clips * pairs * PAIR * length * length),
        name="attend",
    )(query, key, value, rel_low)


def attend_back(query, key, value, out_grad, logs, rel_low):
    clips, length, width = query.shape
    pairs = width // (PAIR * HEAD)
    block = head_block(length)
    shape = jax.ShapeDtypeStruct(query.shape, jnp.bfloat16)
    return pl.pallas_call(
        attend_back_kernel,
        grid=(clips, pairs),
        in_specs=[
            block, block, block, block,
            pl.BlockSpec((1, 1, length, PAIR), lambda i, j: (i, j, 0, 0)),
            pl.BlockSpec((LANES, HEAD), lambda i, j: (0, 0)),
            pl.BlockSpec((LANES, HEAD), lambda i, j: (0, 0)),
            pl.BlockSpec((width_of(length),) * 2, lambda i, j: (0, 0)),
        ],
        out_specs=[block, block, block, pl.BlockSpec((1, 1, HEAD, LANES), lambda i, j: (i, j, 0, 0))],
        out_shape=[shape, shape, shape, jax.ShapeDtypeStruct((clips, pairs, HEAD, LANES), jnp.float32)],
        scratch_shapes=[pltpu.VMEM((PAIR * HEAD, length), jnp.float32)] * 2,
        compiler_params=pltpu.CompilerParams(vmem_limit_bytes=48 << 20),
        cost_estimate=pl.CostEstimate(flops=10 * clips * width * length * length * 4, bytes_accessed=14 * query.size, transcendentals=clips * pairs * PAIR * length * length),
        name="attend_back",
    )(query, key, value, out_grad, logs, rel_low, rel_low[::-1], mirror_of(width_of(length)))


def strip(index):
    return pl.ds(pl.multiple_of(index * LANES, LANES), LANES)


def meet_across(me):
    barrier = pltpu.get_barrier_semaphore()
    pl.semaphore_signal(barrier, inc=1, device_id=me.across(), device_id_type=MESH)
    pl.semaphore_wait(barrier, 1)


def attend_split_kernel(
    pairs, p_ref, rel_ref, out_ref, kept_ref, log_ref, qkv, outs, own_sem, send_sem, recv_sem, kept_sem, out_sem, back_send, back_recv
):
    me = Place()
    step = pl.program_id(0)
    segment = p_ref.shape[0]
    mine, theirs = pl.ds(me.x * segment, segment), pl.ds((1 - me.x) * segment, segment)

    def leaving(i):
        return [
            Sent(p_ref.at[:, strip((2 * part + 1 - me.x) * pairs + i)], qkv.at[i, part, mine, :], send_sem.at[i, part], recv_sem.at[i, part], me.across())
            for part in range(3)
        ]

    def staying(i):
        return [
            pltpu.make_async_copy(p_ref.at[:, strip((2 * part + me.x) * pairs + i)], qkv.at[i, part, mine, :], own_sem.at[i, part])
            for part in range(3)
        ]

    def returns(i):
        there = out_ref.at[:, strip(me.x * pairs + i)]
        return (
            Sent(outs.at[i, theirs, :], there, back_send.at[i], back_recv.at[i], me.across()),
            pltpu.make_async_copy(outs.at[i, mine, :], there, out_sem.at[i]),
            pltpu.make_async_copy(qkv.at[i], kept_ref.at[i], kept_sem.at[i]),
        )

    @pl.when(step == 0)
    def _():
        meet_across(me)
        for i in range(pairs):
            for copy in leaving(i) + staying(i):
                copy.start()

    for copy in leaving(step):
        copy.wait_recv()
    for copy in staying(step):
        copy.wait()
    attend_pair(qkv.at[step, 0], qkv.at[step, 1], qkv.at[step, 2], rel_ref, outs.at[step], log_ref.at[0])
    for copy in returns(step):
        copy.start()

    @pl.when(step == pairs - 1)
    def _():
        for i in range(pairs):
            for copy in leaving(i):
                copy.wait_send()
            sent, kept, own = returns(i)
            sent.wait_send()
            sent.wait_recv()
            kept.wait()
            own.wait()


def attend_split(projected, rel_low, identity):
    segment, width = projected.shape[0], projected.shape[1] // 3
    length, pairs = 2 * segment, width // (2 * PAIR * HEAD)
    dma, anywhere = pltpu.SemaphoreType.DMA, pl.BlockSpec(memory_space=pl.ANY)
    return pl.pallas_call(
        functools.partial(attend_split_kernel, pairs),
        grid=(pairs,),
        in_specs=[anywhere, pl.BlockSpec((LANES, HEAD), lambda i: (0, 0))],
        out_specs=[anywhere, anywhere, pl.BlockSpec((1, length, PAIR), lambda i: (i, 0, 0))],
        out_shape=[
            jax.ShapeDtypeStruct((segment, width), jnp.bfloat16),
            jax.ShapeDtypeStruct((pairs, 3, length, LANES), jnp.bfloat16),
            jax.ShapeDtypeStruct((pairs, length, PAIR), jnp.float32),
        ],
        scratch_shapes=[
            pltpu.VMEM((pairs, 3, length, LANES), jnp.bfloat16),
            pltpu.VMEM((pairs, length, LANES), jnp.bfloat16),
            dma((pairs, 3)), dma((pairs, 3)), dma((pairs, 3)), dma((pairs,)), dma((pairs,)), dma((pairs,)), dma((pairs,)),
        ],
        compiler_params=pltpu.CompilerParams(collective_id=identity, has_side_effects=True, vmem_limit_bytes=48 << 20),
        name="attend_split",
    )(projected, rel_low)


def attend_back_split_kernel(
    pairs, do_ref, kept_ref, log_ref, rel_ref, back_ref, mirror_ref, dp_ref, table_ref,
    grads, qkv, outs, dkt, dvt, own_sem, send_sem, recv_sem, kept_sem, out_sem, back_send, back_recv
):
    me = Place()
    step = pl.program_id(0)
    segment = do_ref.shape[0]
    mine, theirs = pl.ds(me.x * segment, segment), pl.ds((1 - me.x) * segment, segment)

    def leaving(i):
        return Sent(do_ref.at[:, strip((1 - me.x) * pairs + i)], grads.at[i, mine, :], send_sem.at[i], recv_sem.at[i], me.across())

    def staying(i):
        return (
            pltpu.make_async_copy(do_ref.at[:, strip(me.x * pairs + i)], grads.at[i, mine, :], own_sem.at[i]),
            pltpu.make_async_copy(kept_ref.at[i], qkv.at[i], kept_sem.at[i]),
        )

    def returns(i, part):
        there = dp_ref.at[:, strip((2 * part + me.x) * pairs + i)]
        return (
            Sent(outs.at[i, part, theirs, :], there, back_send.at[i, part], back_recv.at[i, part], me.across()),
            pltpu.make_async_copy(outs.at[i, part, mine, :], there, out_sem.at[i, part]),
        )

    @pl.when(step == 0)
    def _():
        meet_across(me)
        for i in range(pairs):
            leaving(i).start()
            for copy in staying(i):
                copy.start()

    leaving(step).wait_recv()
    for copy in staying(step):
        copy.wait()
    attend_back_pair(
        qkv.at[step, 0], qkv.at[step, 1], qkv.at[step, 2], grads.at[step], log_ref.at[0], rel_ref, back_ref, mirror_ref,
        outs.at[step, 0], outs.at[step, 1], outs.at[step, 2], table_ref.at[0], dkt, dvt,
    )
    for part in range(3):
        for copy in returns(step, part):
            copy.start()

    @pl.when(step == pairs - 1)
    def _():
        for i in range(pairs):
            leaving(i).wait_send()
            for part in range(3):
                sent, own = returns(i, part)
                sent.wait_send()
                sent.wait_recv()
                own.wait()


def attend_back_split(out_grad, kept, logs, rel_low, identity):
    segment, width = out_grad.shape
    pairs, _, length, _ = kept.shape
    dma, anywhere = pltpu.SemaphoreType.DMA, pl.BlockSpec(memory_space=pl.ANY)
    table = pl.BlockSpec((LANES, HEAD), lambda i: (0, 0))
    return pl.pallas_call(
        functools.partial(attend_back_split_kernel, pairs),
        grid=(pairs,),
        in_specs=[
            anywhere, anywhere, pl.BlockSpec((1, length, PAIR), lambda i: (i, 0, 0)), table, table,
            pl.BlockSpec((width_of(length),) * 2, lambda i: (0, 0)),
        ],
        out_specs=[anywhere, pl.BlockSpec((1, HEAD, LANES), lambda i: (i, 0, 0))],
        out_shape=[
            jax.ShapeDtypeStruct((segment, 3 * width), jnp.bfloat16),
            jax.ShapeDtypeStruct((pairs, HEAD, LANES), jnp.float32),
        ],
        scratch_shapes=[
            pltpu.VMEM((pairs, length, LANES), jnp.bfloat16),
            pltpu.VMEM((pairs, 3, length, LANES), jnp.bfloat16),
            pltpu.VMEM((pairs, 3, length, LANES), jnp.bfloat16),
            pltpu.VMEM((LANES, length), jnp.float32),
            pltpu.VMEM((LANES, length), jnp.float32),
            dma((pairs,)), dma((pairs,)), dma((pairs,)), dma((pairs,)), dma((pairs, 3)), dma((pairs, 3)), dma((pairs, 3)),
        ],
        compiler_params=pltpu.CompilerParams(collective_id=identity, has_side_effects=True, vmem_limit_bytes=48 << 20),
        name="attend_back_split",
    )(out_grad, kept, logs, rel_low, rel_low[::-1], mirror_of(width_of(length)))


def feed_forward(values, norm_gain, norm_shift, weight_up, bias_up, weight_down, bias_down):
    normed = layer_norm(values, norm_gain, norm_shift).astype(jnp.bfloat16)
    hidden = product(normed, weight_up) + bias_up
    active = jax.nn.silu(hidden).astype(jnp.bfloat16)
    branch = product(active, weight_down) + bias_down
    return (branch, (normed, hidden, active))


def feed_backward(residual_grad, values, kept_parts, norm_gain, norm_shift, weight_up, weight_down):
    normed, hidden, active = kept_parts
    branch_grad = (0.5 * residual_grad).astype(jnp.bfloat16)
    down_grad = contract_rows(active, branch_grad)
    down_bias_grad = jnp.sum(branch_grad.astype(jnp.float32), axis=0)
    active_grad = times_transposed(branch_grad, weight_down)
    silu_pull = jax.vjp(jax.nn.silu, hidden)[1]
    hidden_grad = silu_pull(active_grad)[0].astype(jnp.bfloat16)
    up_grad = contract_rows(normed, hidden_grad)
    up_bias_grad = jnp.sum(hidden_grad.astype(jnp.float32), axis=0)
    normed_grad = times_transposed(hidden_grad, weight_up)
    norm_pull = jax.vjp(layer_norm, values, norm_gain, norm_shift)[1]
    values_grad, gain_grad, shift_grad = norm_pull(normed_grad)
    return (
        residual_grad + values_grad,
        up_grad,
        up_bias_grad,
        down_grad,
        down_bias_grad,
        gain_grad,
        shift_grad,
    )


def heads_of(projected, clip_count, segment, rel_low):
    parts = [
        lax.all_to_all(part.reshape(clip_count, segment, -1), "seq", split_axis=2, concat_axis=1, tiled=True)
        for part in jnp.split(projected, 3, axis=1)
    ]
    merged, log_totals = attend(*parts, rel_low)
    attn_seq = lax.all_to_all(merged, "seq", split_axis=1, concat_axis=2, tiled=True)
    return attn_seq.reshape(clip_count * segment, -1), parts, log_totals


def heads_back(out_grad, parts, log_totals, clip_count, segment, rel_low):
    merged = lax.all_to_all(
        out_grad.reshape(clip_count, segment, -1), "seq", split_axis=2, concat_axis=1, tiled=True
    )
    *grads, table_parts = attend_back(*parts, merged, log_totals, rel_low)
    grads = [
        lax.all_to_all(grad, "seq", split_axis=1, concat_axis=2, tiled=True).reshape(clip_count * segment, -1)
        for grad in grads
    ]
    return jnp.concatenate(grads, axis=1), jnp.sum(table_parts, axis=0)


def spread_sums(grads, small):
    sums = []
    for grad in grads:
        part = lax.psum_scatter(grad, "seq", scatter_dimension=1, tiled=True)
        part = lax.psum_scatter(part, "fsdp", scatter_dimension=0, tiled=True)
        sums.append(part.astype(jnp.float32))
    return (*sums, lax.psum(small, ("seq", "fsdp")))


def stacked(rows):
    lines = jnp.concatenate([row.reshape(-1, rows[0].shape[-1]) for row in rows])
    return jnp.pad(lines, ((0, -lines.shape[0] % 8), (0, 0)))


def body(
    tokens,
    cotangent,
    ffn1_up,
    ffn1_down,
    qkv_weight,
    out_weight,
    conv_in,
    conv_out,
    ffn2_up,
    ffn2_down,
    norm_gains,
    norm_biases,
    hidden_biases,
    model_biases,
    dw_kernel,
    rel_table,
):
    clip_count, segment, model_width = tokens.shape
    row_count = clip_count * segment
    rim_width = KERNEL - 1
    close = lax.axis_size("seq") == 2 and lax.axis_size("fsdp") == 16 and clip_count == 1
    low = jnp.bfloat16
    shards = [
        weight.astype(low)
        for weight in (ffn1_up, ffn1_down, qkv_weight, out_weight, conv_in, conv_out, ffn2_up, ffn2_down)
    ]
    if close:
        weights = gather_whole(shards, 0)
    else:
        weights = [lax.all_gather(shard, "fsdp", axis=0, tiled=True) for shard in shards]
    up_one, down_one, qkv_full, out_full, conv_first, conv_second, up_two, down_two = weights
    input_rows = tokens.reshape(row_count, model_width).astype(jnp.float32)
    branch_one, kept_one = feed_forward(
        input_rows,
        norm_gains[0],
        norm_biases[0],
        up_one,
        hidden_biases[0],
        down_one,
        model_biases[0],
    )
    after_one = input_rows + 0.5 * branch_one
    normed_attn = layer_norm(after_one, norm_gains[1], norm_biases[1]).astype(low)
    project_bias = jnp.concatenate([model_biases[1], jnp.zeros_like(model_biases[1]), model_biases[2]])
    projected = (product(normed_attn, qkv_full) + project_bias).astype(low)
    rel_low = padded_table(rel_table)
    if close:
        attn_rows, kept_heads, log_totals = attend_split(projected, rel_low, 1)
    else:
        attn_rows, kept_heads, log_totals = heads_of(projected, clip_count, segment, rel_low)
    after_two = after_one + product(attn_rows, out_full) + model_biases[3]
    normed_conv = layer_norm(after_two, norm_gains[2], norm_biases[2]).astype(low)
    gate_input = product(normed_conv, conv_first)
    glu_out = glu_function(gate_input).astype(low).reshape(clip_count, segment, model_width)
    glu_before = passed_along(glu_out[:, segment - rim_width :], "seq", 1)
    glu_wide = jnp.concatenate([glu_before, glu_out], axis=1).astype(jnp.float32)
    mixed_rows, kernel_pull = jax.vjp(partial(depthwise, glu_wide), dw_kernel)
    mixed_flat = mixed_rows.reshape(row_count, model_width)
    swished = conv_tail(mixed_flat, norm_gains[3], norm_biases[3]).astype(low)
    after_three = after_two + product(swished, conv_second)
    branch_two, kept_two = feed_forward(
        after_three,
        norm_gains[4],
        norm_biases[4],
        up_two,
        hidden_biases[1],
        down_two,
        model_biases[4],
    )
    after_four = after_three + 0.5 * branch_two
    final_rows, final_pull = jax.vjp(layer_norm, after_four, norm_gains[5], norm_biases[5])
    output = final_rows.astype(low).reshape(clip_count, segment, model_width)
    grad_four, gain_five, shift_five = final_pull(
        cotangent.reshape(row_count, model_width).astype(jnp.float32)
    )
    grad_three, up_two_grad, up_two_bias, down_two_grad, down_two_bias, gain_four, shift_four = (
        feed_backward(
            grad_four, after_three, kept_two, norm_gains[4], norm_biases[4], up_two, down_two
        )
    )
    conv_grad = grad_three.astype(low)
    conv_second_grad = contract_rows(swished, conv_grad)
    swished_grad = times_transposed(conv_grad, conv_second)
    tail_pull = jax.vjp(conv_tail, mixed_flat, norm_gains[3], norm_biases[3])[1]
    mixed_grad, gain_three, shift_three = tail_pull(swished_grad)
    mixed_low = mixed_grad.astype(low).reshape(clip_count, segment, model_width)
    mixed_after = passed_along(mixed_low[:, 0:rim_width], "seq", -1)
    mixed_wide = jnp.concatenate([mixed_low, mixed_after], axis=1).astype(jnp.float32)
    glu_grad = depthwise(mixed_wide, dw_kernel[::-1])
    kernel_grad = kernel_pull(mixed_low.astype(jnp.float32))[0]
    glu_pull = jax.vjp(glu_function, gate_input)[1]
    gate_grad = glu_pull(glu_grad.reshape(row_count, model_width))[0].astype(low)
    conv_first_grad = contract_rows(normed_conv, gate_grad)
    conv_norm_pull = jax.vjp(layer_norm, after_two, norm_gains[2], norm_biases[2])[1]
    values_grad, gain_two, shift_two = conv_norm_pull(times_transposed(gate_grad, conv_first))
    grad_two = grad_three + values_grad
    sums_of = partial(scatter_sums, identity=2) if close else spread_sums
    later_small = stacked(
        [gain_two, gain_three, gain_four, gain_five, shift_two, shift_three, shift_four, shift_five]
        + [up_two_bias, down_two_bias, kernel_grad]
    )
    conv_first_sum, conv_second_sum, up_two_sum, down_two_sum, later_sum = sums_of(
        [grad.astype(low) for grad in (conv_first_grad, conv_second_grad, up_two_grad, down_two_grad)],
        later_small,
    )
    attn_grad = grad_two.astype(low)
    out_grad = contract_rows(attn_rows, attn_grad)
    out_bias_grad = jnp.sum(attn_grad.astype(jnp.float32), axis=0)
    merged_grad = times_transposed(attn_grad, out_full).astype(low)
    if close:
        projected_grad, table_parts = attend_back_split(merged_grad, kept_heads, log_totals, rel_low, 3)
    else:
        projected_grad, table_parts = heads_back(
            merged_grad, kept_heads, log_totals, clip_count, segment, rel_low
        )
    table_grad = jnp.sum(table_parts, axis=0).T[::-1][:BUCKETS]
    qkv_grad = contract_rows(normed_attn, projected_grad)
    query_bias_grad = jnp.sum(projected_grad[:, :model_width].astype(jnp.float32), axis=0)
    value_bias_grad = jnp.sum(projected_grad[:, 2 * model_width :].astype(jnp.float32), axis=0)
    attn_norm_pull = jax.vjp(layer_norm, after_one, norm_gains[1], norm_biases[1])[1]
    values_grad, gain_one, shift_one = attn_norm_pull(times_transposed(projected_grad, qkv_full))
    grad_one = grad_two + values_grad
    grad_zero, up_one_grad, up_one_bias, down_one_grad, down_one_bias, gain_zero, shift_zero = (
        feed_backward(
            grad_one, input_rows, kept_one, norm_gains[0], norm_biases[0], up_one, down_one
        )
    )
    input_grad = grad_zero.astype(low).reshape(clip_count, segment, model_width)
    table_flat = table_grad.reshape(-1)
    table_rows = jnp.pad(table_flat, (0, -table_flat.size % model_width)).reshape(-1, model_width)
    early_small = stacked(
        [gain_zero, gain_one, shift_zero, shift_one, up_one_bias]
        + [down_one_bias, query_bias_grad, value_bias_grad, out_bias_grad, table_rows]
    )
    sums_of = partial(scatter_sums, identity=4) if close else spread_sums
    up_one_sum, down_one_sum, qkv_sum, out_sum, early_sum = sums_of(
        [grad.astype(low) for grad in (up_one_grad, down_one_grad, qkv_grad, out_grad)],
        early_small,
    )
    hidden_rows = up_one_bias.size // model_width
    after_hidden = 4 + hidden_rows
    table_at = after_hidden + 4
    table_sum = early_sum[table_at : table_at + table_rows.shape[0]].reshape(-1)[: table_flat.size]
    later_hidden = 8 + hidden_rows
    return (
        output,
        input_grad,
        up_one_sum,
        down_one_sum,
        qkv_sum,
        out_sum,
        conv_first_sum,
        conv_second_sum,
        up_two_sum,
        down_two_sum,
        jnp.concatenate([early_sum[0:2], later_sum[0:4]]),
        jnp.concatenate([early_sum[2:4], later_sum[4:5]]),
        later_sum[5:8],
        jnp.stack([early_sum[4:after_hidden].reshape(-1), later_sum[8:later_hidden].reshape(-1)]),
        early_sum[after_hidden : after_hidden + 3],
        jnp.concatenate([early_sum[after_hidden + 3 : table_at], later_sum[later_hidden : later_hidden + 1]]),
        later_sum[later_hidden + 1 : later_hidden + 1 + KERNEL],
        table_sum.reshape(table_grad.shape),
    )


def solution(mesh):
    in_specs = (
        P("fsdp", "seq", None),
        P("fsdp", "seq", None),
        P("fsdp", None),
        P("fsdp", None),
        P("fsdp", None),
        P("fsdp", None),
        P("fsdp", None),
        P("fsdp", None),
        P("fsdp", None),
        P("fsdp", None),
        P(),
        P(),
        P(),
        P(),
        P(),
        P(),
    )
    out_specs = (
        P("fsdp", "seq", None),
        P("fsdp", "seq", None),
        P("fsdp", "seq"),
        P("fsdp", "seq"),
        P("fsdp", "seq"),
        P("fsdp", "seq"),
        P("fsdp", "seq"),
        P("fsdp", "seq"),
        P("fsdp", "seq"),
        P("fsdp", "seq"),
        P(),
        P(),
        P(),
        P(),
        P(),
        P(),
        P(),
        P(),
    )
    return jax.shard_map(body, mesh=mesh, in_specs=in_specs, out_specs=out_specs, check_vma=False)
```

time: 2100 us -> 1000 us (0.48)
  waiting for transfers between devices: 1430 us -> 1.69 us
  Pallas kernels: 73.8 us -> 623 us
  other arithmetic: 109 us -> 31.2 us
  local copies, waits for them, and re-layouts: 118 us -> 57.1 us
  starting transfers between devices: 34 us -> 3.49 us
  matrix products: 298 us -> 274 us
    reduce_scatter x16 -> x0, waiting for transfers between devices: 937 us -> none  [the longest x1 101 us: body(): lax.psum_scatter(down_two_grad.astype(jnp.bfloat16), 'seq', scatter_dimen...]
    pallas_call x2 -> x5, Pallas kernels: 73.8 us -> 623 us  [the longest x2 292 us: scatter_sums(): pl.pallas_call(functools.partial(scatter_kernel, count, chunks, lines), i...]
    all_gather x8 -> x0, waiting for transfers between devices: 259 us -> none  [the longest x1 70.9 us: body(): lax.all_gather(ffn1_up.astype(jnp.bfloat16), 'fsdp', axis=0, tiled=True)]
    psum x2 -> x0, waiting for transfers between devices: 206 us -> none  [body(): lax.psum((gains_stack, shifts_stack, hidden_stack, model_stack, kernel_gr...]
    unnamed x9 -> x4, other arithmetic: 61.7 us -> 0.01 us
    unnamed x230 -> x260, local copies, waits for them, and re-layouts: 72.8 us -> 43.7 us
    all_to_all x7 -> x0, starting transfers between devices: 28.1 us -> none  [the longest x1 4.58 us: body(): lax.all_to_all(key_back, 'seq', split_axis=1, concat_axis=2, tiled=True)]
  transfers between devices with their start and end apart: 35 -> 2, of which waited for: 24 -> 1; matrix products, arithmetic and copies ran while one was open for 22% -> 1% of each run, Pallas kernels for 4% -> 0%
where the time goes in v2:
time: 1000 us; the launch traced here: 993 us
  Pallas kernels  623 us (62%)
  matrix products  274 us (27%)
  local copies, waits for them, and re-layouts  57.1 us (6%)
  other arithmetic  31.2 us (3%)
    pallas_call x2, Pallas kernels, scatter_sums(): pl.pallas_call(functools.partial(scatter_kernel, count, chunks, lines), i...  292 us
    pallas_call x1, Pallas kernels, gather_whole(): pl.pallas_call(functools.partial(gather_kernel, count, chunks, lines), in...  222 us
    conv_general_dilated x3, matrix products, depthwise(): lax.conv_general_dilated(wide_rows, kernel_now[:, None, :], (1,), 'VALID'...  116 us
    pallas_call x1, Pallas kernels, attend_back_split(): pl.pallas_call(functools.partial(attend_back_split_kernel, pairs), grid=(...  60.2 us
    dot_general x8, matrix products, contract_rows(): lax.dot_general(former, latter, (((0,), (0,)), ((), ())), preferred_eleme...  56.2 us
    dot_general x8, matrix products, times_transposed(): lax.dot_general(former, latter, (((1,), (1,)), ((), ())), preferred_eleme...  53.7 us
    pallas_call x1, Pallas kernels, attend_split(): pl.pallas_call(functools.partial(attend_split_kernel, pairs), grid=(pairs...  48.9 us
    dot_general x8, matrix products, product(): return jnp.dot(former, latter, preferred_element_type=jnp.float32)  47.6 us
  transfers between devices with their start and end apart: 2, of which 1 were waited for; matrix products, arithmetic and copies ran while one was open for 1% of the time, Pallas kernels for 0%

profile of v2, /device:TPU:0, one launch (start us, length us, event | category | flops | bytes accessed | tf_op | source)
XLA Modules:
  0.0 992.7 jit_solution(425479936590338025)
XLA Ops:
  6.3 221.8 %gather_whole.1 = (bf16[4,2,2,64,4096]{4,3,2,1,0:T(8,128)(2,1)S(1)}, bf16[4,2,2,256,1024]{4,3,2,1,0:T(8,128)(2,1)S(1)}, bf16[4,2,2,64,3072]{4,3,2,1,0:T(8,128)(2...) custom-call(bf16[64,4096]{1,0:T(8,128)(2,1)S(1)} %convert_element_ty, ...), custom_call_target="tpu_custom_call" | custom-call | tf_op jit(solution)/shard_map/gather_whole/pallas_call | solution.py:218
  241.9 9.8 fusion.47
  252.8 7.8 fusion.105
  262.1 7.8 add_convert_fusion.p_ref
  269.9 48.9 %attend_split.1 = (bf16[512,1024]{1,0:T(8,128)(2,1)S(1)}, bf16[4,3,1024,128]{3,2,1,0:T(8,128)(2,1)}, f32[4,1024,2]{2,1,0:T(8,128)S(1)}) custom-call(bf16[512,3072]{1,0:T(8,128)(2,1)} %add_convert_fusion.p_ref, bf16[128,64]{1,0:T(8,128)(2,1)S(1)} %pad.22.rel_ref), custom_call_target="tpu_custom_call" | custom-call | tf_op jit(solution)/shard_map/attend_split/pallas_call | solution.py:679
  334.7 42.2 %fusion.107 = (f32[512]{0:T(512)S(1)}, f32[1,512,1024]{2,0,1:T(1,128)S(1)}) fusion(f32[31,1,1024]{2,0,1:T(8,128)S(1)} %bitcast.220, bf16[1,542,1024]{2,1,0:T(8,128)(2,1)S(1)} %pad_maximum_fusion), kind=kOutput, calls=%fused_computation.210 | convolution fusion | flops 195558912 | bytes 3336192 | tf_op jit(solution)/shard_map/jvp()/conv_general_dilated | solution.py:59
  382.0 7.0 fusion.90
  389.0 7.7 fusion.109
  404.5 10.9 %convert_reduce_fusion = (f32[4096]{0:T(1024)S(1)}, bf16[512,4096]{1,0:T(8,128)(2,1)}) fusion(f32[512,4096]{1,0:T(8,128)} %fusion.90, f32[4096]{0:T(1024)S(1)} %bitcast.250, bf16[512,1024]{1,0:T(8,128)(2,1)} %get-tuple-element.140, bf16[4096,1024]{1,0:T(8,128)(2,1)S(1)} %bitcast.200), kind=kOutput, calls=%fused_computation.8 | convolution fusion | flops 4322226176 | bytes 22052864 | tf_op jit(solution)/shard_map/dot_general | solution.py:44
  415.4 8.8 multiply_reduce_fusion
  424.2 9.3 convolution_convert_fusion.1
  433.5 11.6 %convolution_convert_fusion = bf16[4096,1024]{1,0:T(8,128)(2,1)} fusion(bf16[512,1024]{1,0:T(8,128)(2,1)S(1)} %copy-done.53, f32[512,4096]{1,0:T(8,128)} %fusion.90, f32[4096]{0:T(1024)S(1)} %bitcast.251), kind=kOutput, calls=%fused_computation.14 | convolution fusion | flops 4311744512 | bytes 17842176 | tf_op jit(solution)/shard_map/dot_general | solution.py:38
  454.8 47.8 %fusion.37 = f32[31,1,1024]{2,1,0:T(1,128)S(1)} fusion(bf16[1,512,1024]{2,1,0:T(8,128)(2,1)S(1)} %fusion.44, bf16[1,542,1024]{2,1,0:T(8,128)(2,1)S(1)} %copy-done.49), kind=kOutput, calls=%fused_computation.70 | convolution fusion | flops 32505856 | bytes 2285568 | tf_op jit(solution)/shard_map/transpose(jvp())/conv_general_dilated | solution.py:59
  510.0 26.4 %fusion.18 = f32[1,512,1024]{2,0,1:T(1,128)S(1)} fusion(bf16[1,542,1024]{2,1,0:T(8,128)(2,1)S(1)} %pad_maximum_fusion.1, f32[31,1,1024]{2,0,1:T(8,128)S(1)} %bitcast.221), kind=kOutput, calls=%fused_computation.47 | convolution fusion | flops 195035136 | bytes 3334144 | tf_op jit(solution)/shard_map/conv_general_dilated | solution.py:59
  548.7 60.2 %attend_back_split.1 = (bf16[512,3072]{1,0:T(8,128)(2,1)}, f32[4,64,128]{2,1,0:T(8,128)S(1)}) custom-call(bf16[512,1024]{1,0:T(8,128)(2,1)S(1)} %convolution_convert_fusion.8.do_ref, bf16[4,3,1024,128]{3,2,1,0:T(8,128)(2,1)} %get-tuple-element.50.kept_ref, f32[4,1024,2]{2,1,0:T(8,128)S(1)} %get-tuple-element.51.log_ref, bf16[128,64]{1,0:T(8,128)(2,1)S(1)} %pad.22.rel_ref, ...), custom_call_target="tpu_custom_call" | custom-call | tf_op jit(solution)/shard_map/attend_back_split/pallas_call | solution.py:759
  608.9 7.4 multiply_reduce_fusion.3
  619.8 11.3 %convert_reduce_fusion.1 = (f32[4096]{0:T(1024)S(1)}, bf16[512,4096]{1,0:T(8,128)(2,1)}) fusion(f32[512,4096]{1,0:T(8,128)} %fusion.47, f32[4096]{0:T(1024)S(1)} %bitcast.247, bf16[4096,1024]{1,0:T(8,128)(2,1)S(1)} %bitcast.192, f32[512,1024]{1,0:T(8,128)} %get-tuple-element.146), kind=kOutput, calls=%fused_computation.9 | convolution fusion | flops 4323274752 | bytes 23101440 | tf_op jit(solution)/shard_map/dot_general | solution.py:44
  631.2 8.3 fusion.92
  639.6 7.7 convolution_convert_fusion.3
  647.2 11.4 %convolution_convert_fusion.2 = bf16[4096,1024]{1,0:T(8,128)(2,1)} fusion(f32[512,1024]{1,0:T(8,128)S(1)} %copy-done.31, f32[512,4096]{1,0:T(8,128)} %fusion.47, f32[4096]{0:T(1024)S(1)} %bitcast.248), kind=kOutput, calls=%fused_computation.16 | convolution fusion | flops 4312793088 | bytes 18890752 | tf_op jit(solution)/shard_map/dot_general | solution.py:38
  658.7 5.8 convolution_convert_fusion.4
  668.8 4.6 convolution_convert_fusion.5
  674.6 145.5 %scatter_sums.3 = (f32[64,1024]{1,0:T(8,128)}, f32[64,512]{1,0:T(8,128)}, f32[64,2048]{1,0:T(8,128)}, f32[256,512]{1,0:T(8,128)}, f32[48,1024]{1,0:T(8,128)}) custom-call(bf16[4,2,2,64,2048]{4,3,2,1,0:T(8,128)(2,1)} %bitcast.214, bf16[4,2,2,64,1024]{4,3,2,1,0:T(8,128)(2,1)} %bitcast.216, bf16[4,2,2,64,4096]{4,3,2,1,0:T(8,128)(2,1)} %bitcast.211, ...), custom_call_target="tpu_custom_call" | custom-call | tf_op jit(solution)/shard_map/scatter_sums/pallas_call | solution.py:380
  827.2 146.8 %scatter_sums.2 = (f32[64,2048]{1,0:T(8,128)}, f32[256,512]{1,0:T(8,128)}, f32[64,1536]{1,0:T(8,128)}, f32[64,512]{1,0:T(8,128)}, f32[24,1024]{1,0:T(8,128)}) custom-call(bf16[4,2,2,64,4096]{4,3,2,1,0:T(8,128)(2,1)} %bitcast.209, bf16[4,2,2,256,1024]{4,3,2,1,0:T(8,128)(2,1)} %bitcast.210, bf16[4,2,2,64,3072]{4,3,2,1,0:T(8,128)(2,1)} %bitcast.213, ...), custom_call_target="tpu_custom_call" | custom-call | tf_op jit(solution)/shard_map/scatter_sums/pallas_call | solution.py:380
  (373 shorter events, 113.8 us)
Async XLA Ops:
  4.8 237.0 %copy-start.112 = (f32[1,1024]{1,0:T(1,128)}, f32[1,1024]{1,0:T(1,128)S(1)}, u32[]{:S(2)}) copy-start(f32[1,1024]{1,0:T(1,128)S(1)} %get-tuple-element.174) | copy-start | bytes 12292
  4.8 257.2 %copy-start.110 = (f32[1,1024]{1,0:T(1,128)}, f32[1,1024]{1,0:T(1,128)S(1)}, u32[]{:S(2)}) copy-start(f32[1,1024]{1,0:T(1,128)S(1)} %get-tuple-element.173) | copy-start | bytes 12292
  4.9 317.7 %copy-start.108 = (f32[1,1024]{1,0:T(1,128)}, f32[1,1024]{1,0:T(1,128)S(1)}, u32[]{:S(2)}) copy-start(f32[1,1024]{1,0:T(1,128)S(1)} %get-tuple-element.172) | copy-start | bytes 12292
  5.1 236.8 %copy-start.71 = (f32[1,1024]{1,0:T(1,128)}, f32[1,1024]{1,0:T(1,128)S(1)}, u32[]{:S(2)}) copy-start(f32[1,1024]{1,0:T(1,128)S(1)} %get-tuple-element.168) | copy-start | bytes 12292
  5.1 257.0 %copy-start.99 = (f32[1,1024]{1,0:T(1,128)}, f32[1,1024]{1,0:T(1,128)S(1)}, u32[]{:S(2)}) copy-start(f32[1,1024]{1,0:T(1,128)S(1)} %get-tuple-element.167) | copy-start | bytes 12292
  5.1 317.5 %copy-start.97 = (f32[1,1024]{1,0:T(1,128)}, f32[1,1024]{1,0:T(1,128)S(1)}, u32[]{:S(2)}) copy-start(f32[1,1024]{1,0:T(1,128)S(1)} %get-tuple-element.166) | copy-start | bytes 12292
  5.3 246.4 %copy-start.73 = (f32[512]{0:T(512)}, f32[512]{0:T(512)S(1)}, u32[]{:S(2)}) copy-start(f32[512]{0:T(512)S(1)} %broadcast_multiply_fusion.5) | copy-start | bytes 6148
  6.3 245.3 %copy-start.77 = (f32[512]{0:T(512)}, f32[512]{0:T(512)S(1)}, u32[]{:S(2)}) copy-start(f32[512]{0:T(512)S(1)} %fusion.76) | copy-start | bytes 6148
  6.3 246.3 %copy-start.94 = (f32[1,4096]{1,0:T(1,128)}, f32[1,4096]{1,0:T(1,128)S(1)}, u32[]{:S(2)}) copy-start(f32[1,4096]{1,0:T(1,128)S(1)} %get-tuple-element.177) | copy-start | bytes 49156
  269.9 48.9 %copy-start.10 = (bf16[4,2,2,64,1024]{4,3,2,1,0:T(8,128)(2,1)S(1)}, bf16[4,2,2,64,1024]{4,3,2,1,0:T(8,128)(2,1)}, u32[]{:S(2)}) copy-start(bf16[4,2,2,64,1024]{4,3,2,1,0:T(8,128)(2,1)} %copy-done.9) | copy-start | bytes 6291460
  327.2 6.0 collective-permute-start
  334.7 42.2 %copy-start.48 = (bf16[1,542,1024]{2,1,0:T(8,128)(2,1)}, bf16[1,542,1024]{2,1,0:T(8,128)(2,1)S(1)}, u32[]{:S(2)}) copy-start(bf16[1,542,1024]{2,1,0:T(8,128)(2,1)S(1)} %pad_maximum_fusion) | copy-start | bytes 3330052
  334.7 42.8 %copy-start.36 = (f32[512,1024]{1,0:T(8,128)S(1)}, f32[512,1024]{1,0:T(8,128)}, u32[]{:S(2)}) copy-start(f32[512,1024]{1,0:T(8,128)} %copy-done.35) | copy-start | bytes 6291460
  448.9 54.9 %copy-start.19 = (f32[512,1024]{1,0:T(8,128)}, f32[512,1024]{1,0:T(8,128)S(1)}, u32[]{:S(2)}) copy-start(f32[512,1024]{1,0:T(8,128)S(1)} %add_add_fusion.8) | copy-start | bytes 6291460
  454.3 48.3 %copy-start.42 = (bf16[1,512,1024]{2,1,0:T(8,128)(2,1)}, bf16[1,512,1024]{2,1,0:T(8,128)(2,1)S(1)}, u32[]{:S(2)}) copy-start(bf16[1,512,1024]{2,1,0:T(8,128)(2,1)S(1)} %fusion.44) | copy-start | bytes 3145732
  502.5 6.2 collective-permute-start.1
  510.0 26.5 %copy-start.25 = (f32[512,2048]{1,0:T(8,128)S(1)}, f32[512,2048]{1,0:T(8,128)}, u32[]{:S(2)}) copy-start(f32[512,2048]{1,0:T(8,128)} %copy-done.24) | copy-start | bytes 12582916
  548.6 60.2 %copy-start.33 = (f32[512,1024]{1,0:T(8,128)S(1)}, f32[512,1024]{1,0:T(8,128)}, u32[]{:S(2)}) copy-start(f32[512,1024]{1,0:T(8,128)} %copy-done.32) | copy-start | bytes 6291460
  548.7 60.2 %copy-start.84 = (f32[512]{0:T(512)S(1)}, f32[512]{0:T(512)}, u32[]{:S(2)}) copy-start(f32[512]{0:T(512)} %copy-done.83) | copy-start | bytes 6148
  548.7 60.2 %copy-start.100 = (f32[1,1024]{1,0:T(1,128)S(1)}, f32[1,1024]{1,0:T(1,128)}, u32[]{:S(2)}) copy-start(f32[1,1024]{1,0:T(1,128)} %copy-done.99) | copy-start | bytes 12292
  548.7 60.2 %copy-start.102 = (f32[512]{0:T(512)S(1)}, f32[512]{0:T(512)}, u32[]{:S(2)}) copy-start(f32[512]{0:T(512)} %copy-done.101) | copy-start | bytes 6148
  548.7 71.1 %slice-start.2 = ((s8[8388608]{0:T(1024)(128)(4,1)}), s8[4194304]{0:T(1024)(128)(4,1)S(1)}, s32[]{:S(2)}) async-start(s8[8388608]{0:T(1024)(128)(4,1)} %bitcast.190), calls=%async_computation.2 | async-start | bytes 8388608
  674.6 148.5 %copy-start.80 = (f32[512]{0:T(512)S(1)}, f32[512]{0:T(512)}, u32[]{:S(2)}) copy-start(f32[512]{0:T(512)} %copy-done.79) | copy-start | bytes 6148
  827.2 150.5 %copy-start.66 = (f32[48,1024]{1,0:T(8,128)S(1)}, f32[48,1024]{1,0:T(8,128)}, u32[]{:S(2)}) copy-start(f32[48,1024]{1,0:T(8,128)} %get-tuple-element.63) | copy-start | bytes 589828
  (101 other events, 496.9 us)

commit v3 on v2

--- a/solution.py
+++ b/solution.py
@@ -53,18 +53,6 @@
 
 def conv_tail(mixed_rows, norm_gain, norm_shift):
     return jax.nn.silu(layer_norm(mixed_rows, norm_gain, norm_shift))
-
-
-def depthwise(wide_rows, kernel_now):
-    return lax.conv_general_dilated(
-        wide_rows,
-        kernel_now[:, None, :],
-        (1,),
-        "VALID",
-        dimension_numbers=("NWC", "WIO", "NWC"),
-        feature_group_count=wide_rows.shape[2],
-        precision=lax.Precision.HIGHEST,
-    )
 
 
 MESH = pl.DeviceIdType.MESH
@@ -230,66 +218,94 @@
     return [whole.reshape(-1, whole.shape[-1]) for whole in wholes]
 
 
-SLOTS = 6
+SLOTS = 5
 
 
 def scatter_kernel(count, chunks, lines, *refs):
-    grads, small, outs, small_out = refs[:count], refs[count], refs[count + 1 : 2 * count + 1], refs[2 * count + 1]
-    (held, core_in, early_in, late_in, mid_in, end_in, done, load_sem, done_sem,
+    lefts, rights, small = refs[:count], refs[count : 2 * count], refs[2 * count]
+    outs, small_out = refs[2 * count + 1 : 3 * count + 1], refs[3 * count + 1]
+    (turned, held, core_in, early_in, late_in, y_in, z_in, end_in, done, done_sem,
      c_send, c_recv, x_send, x_recv, y_send, y_recv, z_send, z_recv,
-     small_held, small_in, small_z, small_send, small_recv, small_z_send, small_z_recv) = refs[2 * count + 2 :]
+     small_held, small_in, small_z, small_send, small_recv, small_z_send, small_z_recv) = refs[3 * count + 2 :]
     me = Place()
     me.greet()
     live = {}
     order = [sum(other[3] == chunk[3] for other in chunks[:t]) for t, chunk in enumerate(chunks)]
 
     def columns(chunk, j):
-        return pl.ds(j * (grads[chunk[0]].shape[-1] // 2) + chunk[2], PIECE)
+        return pl.ds(j * (rights[chunk[0]].shape[1] // 2) + chunk[2], PIECE)
 
     def sums(former, latter):
         return (former.astype(jnp.float32) + latter.astype(jnp.float32)).astype(jnp.bfloat16)
 
+    def turn(t):
+        index, line, column, early = chunks[t]
+        left, rows = lefts[index], lefts[index].shape[1] // 16
+        if rows > lines:
+            if line % (2 * lines) == 0:
+
+                @pl.loop(0, 16)
+                def _(i):
+                    block = jnp.transpose(left[:, pl.ds(pl.multiple_of(i * rows + line, 2 * lines), 2 * lines)])
+                    turned[0, pl.ds(pl.multiple_of(i * lines, lines), lines), :] = block[:lines]
+                    turned[1, pl.ds(pl.multiple_of(i * lines, lines), lines), :] = block[lines:]
+
+            return line // lines % 2
+        if column == 0:
+
+            @pl.loop(0, 8)
+            def _(i):
+                span = pl.ds(pl.multiple_of(i * 2 * lines, 2 * lines), 2 * lines)
+                turned[0, span, :] = jnp.transpose(left[:, span])
+
+        return 0
+
     def first(t):
-        index, line, column, early = chunks[t]
-        grad, rows, slot = grads[index], pl.ds(line, lines), t % SLOTS
+        slot = t % SLOTS
         if t >= SLOTS:
-            for kind in "zyx":
+            for kind in "czyx":
                 for copy in live[t - SLOTS, kind]:
                     copy.wait_send()
-        live[t, "c"], live[t, "load"] = [], []
+        which = turn(t)
+        right = rights[chunks[t][0]]
+        live[t, "c"] = []
         for j in range(2):
             cols = columns(chunks[t], j)
-            live[t, "c"].append(send(grad.at[:, :, 1 - me.c, rows, cols], core_in.at[t, j], c_send.at[t, j], c_recv.at[t, j], me.twin()))
-            load = pltpu.make_async_copy(grad.at[:, :, me.c, rows, cols], held.at[slot, j], load_sem.at[t, j])
-            load.start()
-            live[t, "load"].append(load)
+
+            @pl.loop(0, 4)
+            def _(z):
+                part = nn(turned[which, pl.ds(pl.multiple_of(z * 4 * lines, 4 * lines), 4 * lines), :], right[:, cols]).astype(jnp.bfloat16)
+                for y in range(2):
+                    for core in range(2):
+                        held[slot, core, j, z, y] = part[(2 * y + core) * lines : (2 * y + core + 1) * lines]
+
+            live[t, "c"].append(send(held.at[slot, 1 - me.c, j], core_in.at[t, j], c_send.at[t, j], c_recv.at[t, j], me.twin()))
 
     def second(t):
         early, slot = chunks[t][3], t % SLOTS
         for j in range(2):
-            live[t, "load"][j].wait()
             live[t, "c"][j].wait_recv()
             for z in range(4):
-                held[slot, j, z] = sums(held[slot, j, z], core_in[t, j, z])
+                held[slot, me.c, j, z] = sums(held[slot, me.c, j, z], core_in[t, j, z])
         if early:
-            live[t, "x"] = [send(held.at[slot, 1 - me.x], early_in.at[order[t]], x_send.at[t], x_recv.at[t], me.across())]
+            live[t, "x"] = [send(held.at[slot, me.c, 1 - me.x], early_in.at[order[t]], x_send.at[t], x_recv.at[t], me.across())]
         else:
-            live[t, "y"] = [send(held.at[slot, :, :, 1 - me.y], late_in.at[order[t]], y_send.at[t], y_recv.at[t], me.beside())]
+            live[t, "y"] = [send(held.at[slot, me.c, :, :, 1 - me.y], late_in.at[order[t]], y_send.at[t], y_recv.at[t], me.beside())]
 
     def third(t):
         early, slot = chunks[t][3], t % SLOTS
         if early:
             live[t, "x"][0].wait_recv()
             for z in range(4):
-                held[slot, me.x, z] = sums(held[slot, me.x, z], early_in[order[t], z])
-            live[t, "y"] = [send(held.at[slot, me.x, :, 1 - me.y], mid_in.at[t, 0], y_send.at[t], y_recv.at[t], me.beside())]
+                held[slot, me.c, me.x, z] = sums(held[slot, me.c, me.x, z], early_in[order[t], z])
+            live[t, "y"] = [send(held.at[slot, me.c, me.x, :, 1 - me.y], y_in.at[order[t]], y_send.at[t], y_recv.at[t], me.beside())]
         else:
             live[t, "y"][0].wait_recv()
             for j in range(2):
                 for z in range(4):
-                    held[slot, j, z, me.y] = sums(held[slot, j, z, me.y], late_in[order[t], j, z])
+                    held[slot, me.c, j, z, me.y] = sums(held[slot, me.c, j, z, me.y], late_in[order[t], j, z])
             live[t, "z"] = [
-                send(held.at[slot, :, lax.rem(me.z + s, 4), me.y], mid_in.at[t, s - 1, 0:2], z_send.at[t, s - 1], z_recv.at[t, s - 1], me.along(s))
+                send(held.at[slot, me.c, :, lax.rem(me.z + s, 4), me.y], z_in.at[order[t], s - 1], z_send.at[t, s - 1], z_recv.at[t, s - 1], me.along(s))
                 for s in (1, 2, 3)
             ]
 
@@ -298,25 +314,25 @@
         if early:
             live[t, "y"][0].wait_recv()
             for z in range(4):
-                held[slot, me.x, z, me.y] = sums(held[slot, me.x, z, me.y], mid_in[t, 0, z])
+                held[slot, me.c, me.x, z, me.y] = sums(held[slot, me.c, me.x, z, me.y], y_in[order[t], z])
             live[t, "z"] = [
-                send(held.at[slot, me.x, lax.rem(me.z + s, 4), me.y], end_in.at[t, s - 1], z_send.at[t, s - 1], z_recv.at[t, s - 1], me.along(s))
+                send(held.at[slot, me.c, me.x, lax.rem(me.z + s, 4), me.y], end_in.at[t, s - 1], z_send.at[t, s - 1], z_recv.at[t, s - 1], me.along(s))
                 for s in (1, 2, 3)
             ]
         else:
             for copy in live[t, "z"]:
                 copy.wait_recv()
             for j in range(2):
-                value = held[slot, j, me.z, me.y].astype(jnp.float32)
+                value = held[slot, me.c, j, me.z, me.y].astype(jnp.float32)
                 for s in range(3):
-                    value = value + mid_in[t, s, j].astype(jnp.float32)
-                held[slot, j, me.z, me.y] = value.astype(jnp.bfloat16)
-            live[t, "x"] = [send(held.at[slot, 1 - me.x, me.z, me.y], end_in.at[t, 0], x_send.at[t], x_recv.at[t], me.across())]
+                    value = value + z_in[order[t], s, j].astype(jnp.float32)
+                held[slot, me.c, j, me.z, me.y] = value.astype(jnp.bfloat16)
+            live[t, "x"] = [send(held.at[slot, me.c, 1 - me.x, me.z, me.y], end_in.at[t, 0], x_send.at[t], x_recv.at[t], me.across())]
 
     def fifth(t):
         index, line, column, early = chunks[t]
         slot = t % SLOTS
-        value = held[slot, me.x, me.z, me.y].astype(jnp.float32)
+        value = held[slot, me.c, me.x, me.z, me.y].astype(jnp.float32)
         if early:
             for copy in live[t, "z"]:
                 copy.wait_recv()
@@ -360,46 +376,50 @@
     small_end()
     for t in range(total):
         live[t, "done"][0].wait()
-        for copy in live[t, "c"]:
-            copy.wait_send()
         if t + SLOTS >= total:
-            for kind in "zyx":
+            for kind in "czyx":
                 for copy in live[t, kind]:
                     copy.wait_send()
 
 
-def scatter_sums(grads, small, identity):
-    shapes = [(grad.shape[0] // 16, grad.shape[1]) for grad in grads]
+def scatter_sums(factors, small, identity):
+    shapes = [(left.shape[1] // 16, right.shape[1]) for left, right in factors]
     lines = min(rows for rows, _ in shapes)
     chunks = chunks_of(shapes, lines)
-    count, total = len(grads), len(chunks)
+    count, total = len(factors), len(chunks)
+    tokens = factors[0][0].shape[0]
     dma = pltpu.SemaphoreType.DMA
-    anywhere = pl.BlockSpec(memory_space=pl.ANY)
+    anywhere, near = pl.BlockSpec(memory_space=pl.ANY), pl.BlockSpec(memory_space=pltpu.VMEM)
     low = jnp.bfloat16
-    early_count = sum(chunk[3] for chunk in chunks)
+    early = sum(chunk[3] for chunk in chunks)
+    late = total - early
     return pl.pallas_call(
         functools.partial(scatter_kernel, count, chunks, lines),
-        in_specs=[anywhere] * count + [pl.BlockSpec(memory_space=pltpu.VMEM)],
-        out_specs=[anywhere] * count + [pl.BlockSpec(memory_space=pltpu.VMEM)],
+        in_specs=[near] * (2 * count + 1),
+        out_specs=[anywhere] * count + [near],
         out_shape=[jax.ShapeDtypeStruct((rows, width // 2), jnp.float32) for rows, width in shapes]
         + [jax.ShapeDtypeStruct(small.shape, jnp.float32)],
         scratch_shapes=[
-            pltpu.VMEM((SLOTS, 2, 4, 2, lines, PIECE), low),
+            pltpu.VMEM((2, 16 * lines, tokens), low),
+            pltpu.VMEM((SLOTS, 2, 2, 4, 2, lines, PIECE), low),
             pltpu.VMEM((total, 2, 4, 2, lines, PIECE), low),
-            pltpu.VMEM((max(1, early_count), 4, 2, lines, PIECE), low),
-            pltpu.VMEM((max(1, total - early_count), 2, 4, lines, PIECE), low),
-            pltpu.VMEM((total, 3, 4, lines, PIECE), low),
+            pltpu.VMEM((early, 4, 2, lines, PIECE), low),
+            pltpu.VMEM((late, 2, 4, lines, PIECE), low),
+            pltpu.VMEM((early, 4, lines, PIECE), low),
+            pltpu.VMEM((late, 3, 2, lines, PIECE), low),
             pltpu.VMEM((total, 3, lines, PIECE), low),
             pltpu.VMEM((total, lines, PIECE), jnp.float32),
-            dma((total, 2)), dma((total,)),
+            dma((total,)),
             dma((total, 2)), dma((total, 2)), dma((total,)), dma((total,)),
             dma((total,)), dma((total,)), dma((total, 3)), dma((total, 3)),
-            pltpu.VMEM((4, *small.shape), jnp.float32), pltpu.VMEM((3, *small.shape), jnp.float32), pltpu.VMEM((4, *small.shape), jnp.float32),
+            pltpu.VMEM((4, *small.shape), jnp.float32),
+            pltpu.VMEM((3, *small.shape), jnp.float32),
+            pltpu.VMEM((4, *small.shape), jnp.float32),
             dma((3,)), dma((3,)), dma((3,)), dma((3,)),
         ],
         compiler_params=pltpu.CompilerParams(collective_id=identity, has_side_effects=True, vmem_limit_bytes=60 << 20),
         name="scatter_sums",
-    )(*[grad.reshape(4, 2, 2, *shape) for grad, shape in zip(grads, shapes)], small)
+    )(*[left for left, _ in factors], *[right for _, right in factors], small)
 
 
 PAIR = 2
@@ -781,6 +801,89 @@
     )(out_grad, kept, logs, rel_low, rel_low[::-1], mirror_of(width_of(length)))
 
 
+TAPS = 32
+TILE = 128
+
+
+def conv_kernel(wide_ref, taps_ref, out_ref, spread):
+    length = out_ref.shape[1]
+    spread[...] = wide_ref[0].astype(jnp.float32)
+    for start in range(0, length, TILE):
+        total = jnp.zeros((TILE, LANES), jnp.float32)
+        for r in range(KERNEL):
+            total = total + taps_ref[r : r + 1, :] * spread[start + r + 2 : start + r + 2 + TILE, :]
+        out_ref[0, start : start + TILE, :] = total
+
+
+def conv_back_kernel(grad_ref, wide_ref, taps_ref, value_ref, gate_ref, dvalue_ref, dgate_ref, kernel_ref, spread, grads, sums):
+    length = value_ref.shape[0]
+    spread[...] = wide_ref[0].astype(jnp.float32)
+    grads[...] = grad_ref[0].astype(jnp.float32)
+
+    @pl.when(pl.program_id(1) == 0)
+    def _():
+        sums[...] = jnp.zeros_like(sums)
+
+    for start in range(0, length, TILE):
+        own = grads[start : start + TILE, :]
+        total = jnp.zeros((TILE, LANES), jnp.float32)
+        for r in range(KERNEL):
+            total = total + taps_ref[r : r + 1, :] * grads[start + KERNEL - 1 - r : start + KERNEL - 1 - r + TILE, :]
+            both = own * spread[start + r + 2 : start + r + 2 + TILE, :]
+            sums[r] += jnp.sum(both.reshape(TILE // 8, 8, LANES), axis=0)
+        span = slice(start, start + TILE)
+        opened = jax.nn.sigmoid(gate_ref[span, :])
+        dvalue_ref[span, :] = (total * opened).astype(jnp.bfloat16)
+        dgate_ref[span, :] = (total * value_ref[span, :] * (opened * (1.0 - opened))).astype(jnp.bfloat16)
+    kernel_ref[...] = jnp.sum(sums[...], axis=1)
+
+
+def padded_taps(dw_kernel):
+    return jnp.pad(dw_kernel, ((0, TAPS - KERNEL), (0, 0)))
+
+
+def depthwise(wide, dw_kernel):
+    clips, lines, width = wide.shape
+    length = lines - TAPS
+    return pl.pallas_call(
+        conv_kernel,
+        grid=(width // LANES, clips),
+        in_specs=[
+            pl.BlockSpec((1, lines, LANES), lambda i, j: (j, 0, i)),
+            pl.BlockSpec((TAPS, LANES), lambda i, j: (0, i)),
+        ],
+        out_specs=pl.BlockSpec((1, length, LANES), lambda i, j: (j, 0, i)),
+        out_shape=jax.ShapeDtypeStruct((clips, length, width), jnp.float32),
+        scratch_shapes=[pltpu.VMEM((lines, LANES), jnp.float32)],
+        cost_estimate=pl.CostEstimate(flops=2 * KERNEL * clips * length * width, bytes_accessed=6 * clips * length * width, transcendentals=0),
+        name="depthwise",
+    )(wide, padded_taps(dw_kernel))
+
+
+def depthwise_back(grad_wide, wide, dw_kernel, gate_input):
+    clips, lines, width = wide.shape
+    length, blocks = lines - TAPS, width // LANES
+    tall = pl.BlockSpec((1, lines, LANES), lambda i, j: (j, 0, i))
+    half = pl.BlockSpec((length, LANES), lambda i, j: (j, i))
+    taps = pl.BlockSpec((TAPS, LANES), lambda i, j: (0, i))
+    shape = jax.ShapeDtypeStruct((clips * length, width), jnp.bfloat16)
+    dvalue, dgate, kernel_grad = pl.pallas_call(
+        conv_back_kernel,
+        grid=(blocks, clips),
+        in_specs=[tall, tall, taps, half, pl.BlockSpec((length, LANES), lambda i, j: (j, blocks + i))],
+        out_specs=[half, half, taps],
+        out_shape=[shape, shape, jax.ShapeDtypeStruct((TAPS, width), jnp.float32)],
+        scratch_shapes=[
+            pltpu.VMEM((lines, LANES), jnp.float32),
+            pltpu.VMEM((lines, LANES), jnp.float32),
+            pltpu.VMEM((TAPS, 8, LANES), jnp.float32),
+        ],
+        cost_estimate=pl.CostEstimate(flops=4 * KERNEL * clips * length * width, bytes_accessed=16 * clips * length * width, transcendentals=clips * length * width),
+        name="depthwise_back",
+    )(grad_wide, wide, padded_taps(dw_kernel), gate_input, gate_input)
+    return jnp.concatenate([dvalue, dgate], axis=1), kernel_grad[:KERNEL]
+
+
 def feed_forward(values, norm_gain, norm_shift, weight_up, bias_up, weight_down, bias_down):
     normed = layer_norm(values, norm_gain, norm_shift).astype(jnp.bfloat16)
     hidden = product(normed, weight_up) + bias_up
@@ -792,21 +895,19 @@
 def feed_backward(residual_grad, values, kept_parts, norm_gain, norm_shift, weight_up, weight_down):
     normed, hidden, active = kept_parts
     branch_grad = (0.5 * residual_grad).astype(jnp.bfloat16)
-    down_grad = contract_rows(active, branch_grad)
     down_bias_grad = jnp.sum(branch_grad.astype(jnp.float32), axis=0)
     active_grad = times_transposed(branch_grad, weight_down)
     silu_pull = jax.vjp(jax.nn.silu, hidden)[1]
     hidden_grad = silu_pull(active_grad)[0].astype(jnp.bfloat16)
-    up_grad = contract_rows(normed, hidden_grad)
     up_bias_grad = jnp.sum(hidden_grad.astype(jnp.float32), axis=0)
     normed_grad = times_transposed(hidden_grad, weight_up)
     norm_pull = jax.vjp(layer_norm, values, norm_gain, norm_shift)[1]
     values_grad, gain_grad, shift_grad = norm_pull(normed_grad)
     return (
         residual_grad + values_grad,
-        up_grad,
+        (normed, hidden_grad),
         up_bias_grad,
-        down_grad,
+        (active, branch_grad),
         down_bias_grad,
         gain_grad,
         shift_grad,
@@ -835,10 +936,10 @@
     return jnp.concatenate(grads, axis=1), jnp.sum(table_parts, axis=0)
 
 
-def spread_sums(grads, small):
+def spread_sums(factors, small):
     sums = []
-    for grad in grads:
-        part = lax.psum_scatter(grad, "seq", scatter_dimension=1, tiled=True)
+    for left, right in factors:
+        part = lax.psum_scatter(contract_rows(left, right).astype(jnp.bfloat16), "seq", scatter_dimension=1, tiled=True)
         part = lax.psum_scatter(part, "fsdp", scatter_dimension=0, tiled=True)
         sums.append(part.astype(jnp.float32))
     return (*sums, lax.psum(small, ("seq", "fsdp")))
@@ -905,9 +1006,9 @@
     gate_input = product(normed_conv, conv_first)
     glu_out = glu_function(gate_input).astype(low).reshape(clip_count, segment, model_width)
     glu_before = passed_along(glu_out[:, segment - rim_width :], "seq", 1)
-    glu_wide = jnp.concatenate([glu_before, glu_out], axis=1).astype(jnp.float32)
-    mixed_rows, kernel_pull = jax.vjp(partial(depthwise, glu_wide), dw_kernel)
-    mixed_flat = mixed_rows.reshape(row_count, model_width)
+    margin = jnp.zeros((clip_count, TAPS - rim_width, model_width), low)
+    glu_wide = jnp.concatenate([margin, glu_before, glu_out], axis=1)
+    mixed_flat = depthwise(glu_wide, dw_kernel).reshape(row_count, model_width)
     swished = conv_tail(mixed_flat, norm_gains[3], norm_biases[3]).astype(low)
     after_three = after_two + product(swished, conv_second)
     branch_two, kept_two = feed_forward(
@@ -925,24 +1026,19 @@
     grad_four, gain_five, shift_five = final_pull(
         cotangent.reshape(row_count, model_width).astype(jnp.float32)
     )
-    grad_three, up_two_grad, up_two_bias, down_two_grad, down_two_bias, gain_four, shift_four = (
+    grad_three, up_two_factors, up_two_bias, down_two_factors, down_two_bias, gain_four, shift_four = (
         feed_backward(
             grad_four, after_three, kept_two, norm_gains[4], norm_biases[4], up_two, down_two
         )
     )
     conv_grad = grad_three.astype(low)
-    conv_second_grad = contract_rows(swished, conv_grad)
     swished_grad = times_transposed(conv_grad, conv_second)
     tail_pull = jax.vjp(conv_tail, mixed_flat, norm_gains[3], norm_biases[3])[1]
     mixed_grad, gain_three, shift_three = tail_pull(swished_grad)
     mixed_low = mixed_grad.astype(low).reshape(clip_count, segment, model_width)
     mixed_after = passed_along(mixed_low[:, 0:rim_width], "seq", -1)
-    mixed_wide = jnp.concatenate([mixed_low, mixed_after], axis=1).astype(jnp.float32)
-    glu_grad = depthwise(mixed_wide, dw_kernel[::-1])
-    kernel_grad = kernel_pull(mixed_low.astype(jnp.float32))[0]
-    glu_pull = jax.vjp(glu_function, gate_input)[1]
-    gate_grad = glu_pull(glu_grad.reshape(row_count, model_width))[0].astype(low)
-    conv_first_grad = contract_rows(normed_conv, gate_grad)
+    mixed_wide = jnp.concatenate([mixed_low, mixed_after, margin], axis=1)
+    gate_grad, kernel_grad = depthwise_back(mixed_wide, glu_wide, dw_kernel, gate_input)
     conv_norm_pull = jax.vjp(layer_norm, after_two, norm_gains[2], norm_biases[2])[1]
     values_grad, gain_two, shift_two = conv_norm_pull(times_transposed(gate_grad, conv_first))
     grad_two = grad_three + values_grad
@@ -952,11 +1048,10 @@
         + [up_two_bias, down_two_bias, kernel_grad]
     )
     conv_first_sum, conv_second_sum, up_two_sum, down_two_sum, later_sum = sums_of(
-        [grad.astype(low) for grad in (conv_first_grad, conv_second_grad, up_two_grad, down_two_grad)],
+        [(normed_conv, gate_grad), (swished, conv_grad), up_two_factors, down_two_factors],
         later_small,
     )
     attn_grad = grad_two.astype(low)
-    out_grad = contract_rows(attn_rows, attn_grad)
     out_bias_grad = jnp.sum(attn_grad.astype(jnp.float32), axis=0)
     merged_grad = times_transposed(attn_grad, out_full).astype(low)
     if close:
@@ -966,13 +1061,12 @@
             merged_grad, kept_heads, log_totals, clip_count, segment, rel_low
         )
     table_grad = jnp.sum(table_parts, axis=0).T[::-1][:BUCKETS]
-    qkv_grad = contract_rows(normed_attn, projected_grad)
     query_bias_grad = jnp.sum(projected_grad[:, :model_width].astype(jnp.float32), axis=0)
     value_bias_grad = jnp.sum(projected_grad[:, 2 * model_width :].astype(jnp.float32), axis=0)
     attn_norm_pull = jax.vjp(layer_norm, after_one, norm_gains[1], norm_biases[1])[1]
     values_grad, gain_one, shift_one = attn_norm_pull(times_transposed(projected_grad, qkv_full))
     grad_one = grad_two + values_grad
-    grad_zero, up_one_grad, up_one_bias, down_one_grad, down_one_bias, gain_zero, shift_zero = (
+    grad_zero, up_one_factors, up_one_bias, down_one_factors, down_one_bias, gain_zero, shift_zero = (
         feed_backward(
             grad_one, input_rows, kept_one, norm_gains[0], norm_biases[0], up_one, down_one
         )
@@ -986,7 +1080,7 @@
     )
     sums_of = partial(scatter_sums, identity=4) if close else spread_sums
     up_one_sum, down_one_sum, qkv_sum, out_sum, early_sum = sums_of(
-        [grad.astype(low) for grad in (up_one_grad, down_one_grad, qkv_grad, out_grad)],
+        [up_one_factors, down_one_factors, (normed_attn, projected_grad), (attn_rows, attn_grad)],
         early_small,
     )
     hidden_rows = up_one_bias.size // model_width

time: 1000 us -> 853 us (0.85)
  matrix products: 274 us -> 99.6 us
  Pallas kernels: 623 us -> 649 us
    conv_general_dilated x3 -> x0, matrix products: 116 us -> none  [depthwise(): lax.conv_general_dilated(wide_rows, kernel_now[:, None, :], (1,), 'VALID'...]
    dot_general x8 -> x0, matrix products: 56.2 us -> none  [contract_rows(): lax.dot_general(former, latter, (((0,), (0,)), ((), ())), preferred_eleme...]
    pallas_call x0 -> x2, Pallas kernels: none -> 20.9 us  [the longest x1 12.9 us: depthwise_back(): pl.pallas_call(conv_back_kernel, grid=(blocks, clips), in_specs=[tall, ta...]
    unnamed x260 -> x192, local copies, waits for them, and re-layouts: 43.7 us -> 34.5 us
  transfers between devices with their start and end apart: 2 -> 2, of which waited for: 1 -> 2; matrix products, arithmetic and copies ran while one was open for 1% -> 0% of each run, Pallas kernels for 0% -> 0%
where the time goes in v3:
time: 853 us; the launch traced here: 842 us
  Pallas kernels  649 us (76%)
  matrix products  99.6 us (12%)
  local copies, waits for them, and re-layouts  47.7 us (6%)
  other arithmetic  34.7 us (4%)
    pallas_call x2, Pallas kernels, scatter_sums(): pl.pallas_call(functools.partial(scatter_kernel, count, chunks, lines), i...  298 us
    pallas_call x1, Pallas kernels, gather_whole(): pl.pallas_call(functools.partial(gather_kernel, count, chunks, lines), in...  222 us
    pallas_call x1, Pallas kernels, attend_back_split(): pl.pallas_call(functools.partial(attend_back_split_kernel, pairs), grid=(...  59.5 us
    dot_general x8, matrix products, times_transposed(): lax.dot_general(former, latter, (((1,), (1,)), ((), ())), preferred_eleme...  54.4 us
    pallas_call x1, Pallas kernels, attend_split(): pl.pallas_call(functools.partial(attend_split_kernel, pairs), grid=(pairs...  48.8 us
    dot_general x8, matrix products, product(): return jnp.dot(former, latter, preferred_element_type=jnp.float32)  45.2 us
    unnamed x192, local copies, waits for them, and re-layouts  34.5 us
  transfers between devices with their start and end apart: 2, of which 2 were waited for; matrix products, arithmetic and copies ran while one was open for 0% of the time, Pallas kernels for 0%

profile of v3, /device:TPU:0, one launch (start us, length us, event | category | flops | bytes accessed | tf_op | source)
XLA Modules:
  0.0 842.4 jit_solution(14426149882483811805)
XLA Ops:
  6.6 221.8 %gather_whole.1 = (bf16[4,2,2,64,4096]{4,3,2,1,0:T(8,128)(2,1)S(1)}, bf16[4,2,2,256,1024]{4,3,2,1,0:T(8,128)(2,1)S(1)}, bf16[4,2,2,64,3072]{4,3,2,1,0:T(8,128)(2...) custom-call(bf16[64,4096]{1,0:T(8,128)(2,1)S(1)} %convert_element_ty, ...), custom_call_target="tpu_custom_call" | custom-call | tf_op jit(solution)/shard_map/gather_whole/pallas_call | solution.py:206
  228.4 3.2 copy-done.3
  239.5 8.7 %multiply_convert_fusion.1 = (bf16[512,4096]{1,0:T(8,128)(2,1)S(1)}, f32[512,4096]{1,0:T(8,128)}) fusion(f32[4096]{0:T(1024)S(1)} %bitcast.229, bf16[1024,4096]{1,0:T(8,128)(2,1)S(1)} %bitcast.170, bf16[1,512,1024]{2,1,0:T(8,128)(2,1)S(1)} %copy-done.31, f32[1024]{0:T(1024)S(1)} %bitcast.217, f32[1024]{0:T(1024)S(1)} %bitcast.201, f32[512]{0:T(512)S(1)} %fusion.53, ...), kind=kOutput, calls=%fused_computation.12 | convolution fusion | flops 4310695936 | bytes 22048768 | tf_op jit(solution)/shard_map/dot_general | solution.py:34
  249.0 4.7 fusion.78
  255.1 7.9 add_convert_fusion.p_ref
  263.0 48.8 %attend_split.1 = (bf16[512,1024]{1,0:T(8,128)(2,1)S(1)}, bf16[4,3,1024,128]{3,2,1,0:T(8,128)(2,1)}, f32[4,1024,2]{2,1,0:T(8,128)S(1)}) custom-call(bf16[512,3072]{1,0:T(8,128)(2,1)} %add_convert_fusion.p_ref, bf16[128,64]{1,0:T(8,128)(2,1)S(1)} %pad.21.rel_ref), custom_call_target="tpu_custom_call" | custom-call | tf_op jit(solution)/shard_map/attend_split/pallas_call | solution.py:699
  326.3 8.0 depthwise.1
  338.3 3.9 fusion.80
  342.9 11.6 %multiply_convert_fusion = (bf16[512,4096]{1,0:T(8,128)(2,1)S(1)}, f32[512,4096]{1,0:T(8,128)}) fusion(f32[4096]{0:T(1024)S(1)} %bitcast.231, bf16[512,1024]{1,0:T(8,128)(2,1)S(1)} %add_convert_fusion.4.refs_2_, bf16[1024,4096]{1,0:T(8,128)(2,1)} %bitcast.176), kind=kOutput, calls=%fused_computation.10 | convolution fusion | flops 4307550208 | bytes 22036480 | tf_op jit(solution)/shard_map/dot_general | solution.py:34
  354.6 4.7 fusion.81
  364.1 11.0 %convert_reduce_fusion = (f32[4096]{0:T(1024)S(1)}, bf16[512,4096]{1,0:T(8,128)(2,1)}) fusion(f32[512,4096]{1,0:T(8,128)} %get-tuple-element.205, f32[4096]{0:T(1024)S(1)} %bitcast.232, bf16[512,1024]{1,0:T(8,128)(2,1)S(1)} %get-tuple-element.145.refs_7_, bf16[4096,1024]{1,0:T(8,128)(2,1)S(1)} %bitcast.183), kind=kOutput, calls=%fused_computation.8 | convolution fusion | flops 4322226176 | bytes 22052864 | tf_op jit(solution)/shard_map/dot_general | solution.py:44
  375.1 8.0 multiply_reduce_fusion
  388.1 3.5 multiply_reduce_fusion.1
  393.9 4.7 collective-permute-done.1
  401.0 12.9 %depthwise_back.1 = (bf16[512,1024]{1,0:T(8,128)(2,1)}, bf16[512,1024]{1,0:T(8,128)(2,1)}, f32[32,1024]{1,0:T(8,128)}) custom-call(bf16[1,544,1024]{2,1,0:T(8,128)(2,1)} %pad_maximum_fusion.1.grad_ref, bf16[1,544,1024]{2,1,0:T(8,128)(2,1)} %pad_maximum_fusion.wide_ref, f32[32,1024]{1,0:T(8,128)} %pad.22.taps_ref, f32[512,2048]{1,0:T(8,128)} %copy-done.15, ...), custom_call_target="tpu_custom_call" | custom-call | flops 65011712 | bytes 8388608 | tf_op jit(solution)/shard_map/depthwise_back/pallas_call | solution.py:870
  416.9 5.2 multiply_reduce_fusion.2
  426.4 59.5 %attend_back_split.1 = (bf16[512,3072]{1,0:T(8,128)(2,1)}, f32[4,64,128]{2,1,0:T(8,128)S(1)}) custom-call(bf16[512,1024]{1,0:T(8,128)(2,1)S(1)} %convolution_convert_fusion.do_ref, bf16[4,3,1024,128]{3,2,1,0:T(8,128)(2,1)} %get-tuple-element.55.kept_ref, f32[4,1024,2]{2,1,0:T(8,128)S(1)} %get-tuple-element.56.log_ref, bf16[128,64]{1,0:T(8,128)(2,1)S(1)} %pad.21.rel_ref, ...), custom_call_target="tpu_custom_call" | custom-call | tf_op jit(solution)/shard_map/attend_back_split/pallas_call | solution.py:779
  486.0 7.1 multiply_reduce_fusion.3
  495.1 147.8 %scatter_sums.3 = (f32[64,1024]{1,0:T(8,128)}, f32[64,512]{1,0:T(8,128)}, f32[64,2048]{1,0:T(8,128)}, f32[256,512]{1,0:T(8,128)}, f32[48,1024]{1,0:T(8,128)}) custom-call(bf16[512,1024]{1,0:T(8,128)(2,1)} %copy-done.45, bf16[512,1024]{1,0:T(8,128)(2,1)} %get-tuple-element.168.refs_1_, bf16[512,1024]{1,0:T(8,128)(2,1)} %copy-done.46, ...), custom_call_target="tpu_custom_call" | custom-call | tf_op jit(solution)/shard_map/scatter_sums/pallas_call | solution.py:396
  650.6 12.2 %convert_reduce_fusion.1 = (f32[4096]{0:T(1024)S(1)}, bf16[512,4096]{1,0:T(8,128)(2,1)S(1)}) fusion(f32[512,4096]{1,0:T(8,128)} %get-tuple-element.197, f32[4096]{0:T(1024)S(1)} %bitcast.230, bf16[512,1024]{1,0:T(8,128)(2,1)S(1)} %get-tuple-element.151.refs_5_, bf16[4096,1024]{1,0:T(8,128)(2,1)} %bitcast.175), kind=kOutput, calls=%fused_computation.9 | convolution fusion | flops 4322226176 | bytes 22052864 | tf_op jit(solution)/shard_map/dot_general | solution.py:44
  662.9 6.0 fusion.61
  669.3 3.6 fusion.20
  674.0 150.0 %scatter_sums.2 = (f32[64,2048]{1,0:T(8,128)}, f32[256,512]{1,0:T(8,128)}, f32[64,1536]{1,0:T(8,128)}, f32[64,512]{1,0:T(8,128)}, f32[24,1024]{1,0:T(8,128)}) custom-call(bf16[512,1024]{1,0:T(8,128)(2,1)} %get-tuple-element.170.refs_0_, bf16[512,4096]{1,0:T(8,128)(2,1)} %copy-done.40, bf16[512,1024]{1,0:T(8,128)(2,1)} %copy-done.38, ...), custom_call_target="tpu_custom_call" | custom-call | tf_op jit(solution)/shard_map/scatter_sums/pallas_call | solution.py:396
  830.1 3.4 fusion.38
  (301 shorter events, 81.7 us)
Async XLA Ops:
  2.5 237.0 %copy-start.79 = (f32[1,4096]{1,0:T(1,128)}, f32[1,4096]{1,0:T(1,128)S(1)}, u32[]{:S(2)}) copy-start(f32[1,4096]{1,0:T(1,128)S(1)} %get-tuple-element.195) | copy-start | bytes 49156
  5.7 233.8 %copy-start.77 = (f32[1,1024]{1,0:T(1,128)}, f32[1,1024]{1,0:T(1,128)S(1)}, u32[]{:S(2)}) copy-start(f32[1,1024]{1,0:T(1,128)S(1)} %get-tuple-element.187) | copy-start | bytes 12292
  5.9 233.6 %copy-start.66 = (f32[1,1024]{1,0:T(1,128)}, f32[1,1024]{1,0:T(1,128)S(1)}, u32[]{:S(2)}) copy-start(f32[1,1024]{1,0:T(1,128)S(1)} %get-tuple-element.181) | copy-start | bytes 12292
  6.2 242.1 %copy-start.68 = (f32[512]{0:T(512)}, f32[512]{0:T(512)S(1)}, u32[]{:S(2)}) copy-start(f32[512]{0:T(512)S(1)} %broadcast_multiply_fusion.5) | copy-start | bytes 6148
  6.6 241.6 %copy-start.73 = (f32[512]{0:T(512)}, f32[512]{0:T(512)S(1)}, u32[]{:S(2)}) copy-start(f32[512]{0:T(512)S(1)} %fusion.23) | copy-start | bytes 6148
  6.6 241.6 %copy-start.71 = (f32[512]{0:T(512)}, f32[512]{0:T(512)S(1)}, u32[]{:S(2)}) copy-start(f32[512]{0:T(512)S(1)} %fusion.53) | copy-start | bytes 6148
  255.1 56.8 %copy-start.20 = (f32[512,1024]{1,0:T(8,128)S(1)}, f32[512,1024]{1,0:T(8,128)}, u32[]{:S(2)}) copy-start(f32[512,1024]{1,0:T(8,128)} %copy-done.19) | copy-start | bytes 6291460
  263.0 48.9 %copy-start.10 = (bf16[4,2,2,64,1024]{4,3,2,1,0:T(8,128)(2,1)S(1)}, bf16[4,2,2,64,1024]{4,3,2,1,0:T(8,128)(2,1)}, u32[]{:S(2)}) copy-start(bf16[4,2,2,64,1024]{4,3,2,1,0:T(8,128)(2,1)} %copy-done.9) | copy-start | bytes 6291460
  321.0 4.1 collective-permute-start
  342.1 12.5 %copy-start.27 = (f32[512,1024]{1,0:T(8,128)}, f32[512,1024]{1,0:T(8,128)S(1)}, u32[]{:S(2)}) copy-start(f32[512,1024]{1,0:T(8,128)S(1)} %get-tuple-element.203) | copy-start | bytes 6291460
  360.5 14.6 %slice-start.2 = ((s8[8388608]{0:T(1024)(128)(4,1)}), s8[4194304]{0:T(1024)(128)(4,1)S(1)}, s32[]{:S(2)}) async-start(s8[8388608]{0:T(1024)(128)(4,1)} %bitcast.177), calls=%async_computation.2 | async-start | bytes 8388608
  392.5 6.2 collective-permute-start.1
  423.7 62.2 %slice-start.6 = ((s8[6291456]{0:T(1024)(128)(4,1)}), s8[4194304]{0:T(1024)(128)(4,1)S(1)}, s32[]{:S(2)}) async-start(s8[6291456]{0:T(1024)(128)(4,1)} %bitcast.185), calls=%async_computation.6 | async-start | bytes 8388608
  425.1 60.9 %slice-start.7 = ((s8[6291456]{0:T(1024)(128)(4,1)}), s8[2097152]{0:T(1024)(128)(4,1)S(1)}, s32[]{:S(2)}) async-start(s8[6291456]{0:T(1024)(128)(4,1)} %bitcast.185), calls=%async_computation.7 | async-start | bytes 4194304
  426.4 59.6 %copy-start.21 = (f32[512,1024]{1,0:T(8,128)S(1)}, f32[512,1024]{1,0:T(8,128)}, u32[]{:S(2)}) copy-start(f32[512,1024]{1,0:T(8,128)} %copy-done.19) | copy-start | bytes 6291460
  495.1 150.7 %copy-start.22 = (f32[512,1024]{1,0:T(8,128)S(1)}, f32[512,1024]{1,0:T(8,128)}, u32[]{:S(2)}) copy-start(f32[512,1024]{1,0:T(8,128)} %copy-done.19) | copy-start | bytes 6291460
  648.6 14.1 %slice-start = ((s8[8388608]{0:T(1024)(128)(4,1)}), s8[4194304]{0:T(1024)(128)(4,1)S(1)}, s32[]{:S(2)}) async-start(s8[8388608]{0:T(1024)(128)(4,1)} %bitcast.171), calls=%async_computation | async-start | bytes 8388608
  650.5 12.2 %copy-start.43 = (bf16[512,1024]{1,0:T(8,128)(2,1)}, bf16[512,1024]{1,0:T(8,128)(2,1)S(1)}, u32[]{:S(2)}) copy-start(bf16[512,1024]{1,0:T(8,128)(2,1)S(1)} %get-tuple-element.151.refs_5_) | copy-start | bytes 3145732
  650.5 12.3 %slice-start.1 = ((s8[8388608]{0:T(1024)(128)(4,1)}), s8[4194304]{0:T(1024)(128)(4,1)S(1)}, s32[]{:S(2)}) async-start(s8[8388608]{0:T(1024)(128)(4,1)} %bitcast.171), calls=%async_computation.1 | async-start | bytes 8388608
  650.5 12.3 %copy-start.32 = (bf16[1,512,1024]{2,1,0:T(8,128)(2,1)S(1)}, bf16[1,512,1024]{2,1,0:T(8,128)(2,1)}, u32[]{:S(2)}) copy-start(bf16[1,512,1024]{2,1,0:T(8,128)(2,1)} %param.16) | copy-start | bytes 3145732
  650.5 12.3 %copy-start.67 = (f32[1,1024]{1,0:T(1,128)S(1)}, f32[1,1024]{1,0:T(1,128)}, u32[]{:S(2)}) copy-start(f32[1,1024]{1,0:T(1,128)} %copy-done.66) | copy-start | bytes 12292
  650.5 12.3 %copy-start.69 = (f32[512]{0:T(512)S(1)}, f32[512]{0:T(512)}, u32[]{:S(2)}) copy-start(f32[512]{0:T(512)} %copy-done.68) | copy-start | bytes 6148
  674.0 153.7 %copy-start.61 = (f32[48,1024]{1,0:T(8,128)S(1)}, f32[48,1024]{1,0:T(8,128)}, u32[]{:S(2)}) copy-start(f32[48,1024]{1,0:T(8,128)} %get-tuple-element.69) | copy-start | bytes 589828
  674.0 156.1 %copy-start.35 = (f32[512,1024]{1,0:T(8,128)S(1)}, f32[512,1024]{1,0:T(8,128)}, u32[]{:S(2)}) copy-start(f32[512,1024]{1,0:T(8,128)} %get-tuple-element.211) | copy-start | bytes 6291460
  (67 other events, 295.8 us)

commit v4 on v3

--- a/solution.py
+++ b/solution.py
@@ -56,7 +56,12 @@
 
 
 MESH = pl.DeviceIdType.MESH
-PIECE = 512
+PIECE = 256
+LAG = 2
+BLOCK = 512
+WAIT = 2
+OWN_SLOTS = 8
+AWAY_SLOTS = 3
 
 
 class Place:
@@ -87,12 +92,14 @@
         pl.semaphore_wait(barrier, len(peers))
 
 
-def chunks_of(shapes, lines):
+def chunks_of(shapes, lines, crossing, piece):
+    part, whole = crossing
     found = []
     for index, (rows, width) in enumerate(shapes):
         for line in range(0, rows, lines):
-            for column in range(0, width // 2, PIECE):
-                found.append((index, line, column, len(found) % 3 != 2))
+            for column in range(0, width // 2, piece):
+                count = len(found)
+                found.append((index, line, column, (count + 1) * part // whole > count * part // whole))
     return found
 
 
@@ -110,316 +117,423 @@
         pltpu.make_async_remote_copy(**self.parts).wait_send()
 
 
-def send(source, target, send_sem, recv_sem, device):
-    copy = Sent(source, target, send_sem, recv_sem, device)
-    copy.start()
-    return copy
-
-
-def gather_kernel(count, chunks, lines, *refs):
-    shards, wholes = refs[:count], refs[count : 2 * count]
-    own_sem, z_send, z_recv, y_send, y_recv, x_send, x_recv, c_send, c_recv = refs[2 * count :]
+class Near:
+    def __init__(self, source, target, sem):
+        self.parts = (source, target, sem)
+
+    def start(self):
+        pltpu.make_async_copy(*self.parts).start()
+
+    def wait(self):
+        pltpu.make_async_copy(*self.parts).wait()
+
+
+class Gather:
+    def __init__(self, me, shards, wholes, chunks, lines, sems):
+        self.me, self.shards, self.wholes, self.chunks, self.lines = me, shards, wholes, chunks, lines
+        (self.own_sem, self.z_send, self.z_recv, self.y_send, self.y_recv, self.x_send, self.x_recv, self.c_send, self.c_recv) = sems
+        self.steps = len(chunks) + 3 * LAG
+        self.number = 0
+        self.whole = set()
+
+    @staticmethod
+    def scratch(total):
+        dma = pltpu.SemaphoreType.DMA
+        return [
+            dma((total, 2)), dma((total, 2, 3)), dma((total, 2, 3)), dma((total, 2)), dma((total, 2)),
+            dma((total,)), dma((total,)), dma((total, 2)), dma((total, 2)),
+        ]
+
+    def halves(self, chunk):
+        index, line, column, early = chunk
+        half = self.shards[index].shape[1] // 2
+        if early:
+            return [pl.ds(pl.multiple_of(self.me.x * half + column, PIECE), PIECE)]
+        return [pl.ds(column, PIECE), pl.ds(half + column, PIECE)]
+
+    def both(self, chunk):
+        half = self.shards[chunk[0]].shape[1] // 2
+        return [pl.ds(chunk[2], PIECE), pl.ds(half + chunk[2], PIECE)]
+
+    def make(self, t, kind):
+        index, line, column, early = self.chunks[t]
+        shard, whole, rows, me = self.shards[index], self.wholes[index], pl.ds(line, self.lines), self.me
+        halves = self.halves(self.chunks[t])
+        if kind == "own":
+            return [
+                Near(shard.at[rows, cols], whole.at[me.z, me.y, me.c, rows, cols], self.own_sem.at[t, j])
+                for j, cols in enumerate(halves)
+            ]
+        if kind == "z":
+            return [
+                Sent(shard.at[rows, cols], whole.at[me.z, me.y, me.c, rows, cols], self.z_send.at[t, j, s - 1], self.z_recv.at[t, j, s - 1], me.along(s))
+                for j, cols in enumerate(halves)
+                for s in (1, 2, 3)
+            ]
+        if kind == "y":
+            views = [whole.at[:, me.y, me.c, rows, cols] for cols in halves]
+            return [Sent(view, view, self.y_send.at[t, j], self.y_recv.at[t, j], me.beside()) for j, view in enumerate(views)]
+        if kind == "x":
+            views = [whole.at[:, :, me.c, rows, halves[0]]] if early else []
+            return [Sent(view, view, self.x_send.at[t], self.x_recv.at[t], me.across()) for view in views]
+        views = [whole.at[:, :, me.c, rows, cols] for cols in self.both(self.chunks[t])]
+        return [Sent(view, view, self.c_send.at[t, j], self.c_recv.at[t, j], me.twin()) for j, view in enumerate(views)]
+
+    def start(self, t, kind):
+        for copy in self.make(t, kind):
+            copy.start()
+
+    def arrive(self, t, kind):
+        for copy in self.make(t, kind):
+            copy.wait_recv()
+
+    def first(self, t):
+        self.start(t, "own")
+        self.start(t, "z")
+
+    def second(self, t):
+        for copy in self.make(t, "own"):
+            copy.wait()
+        self.arrive(t, "z")
+        self.start(t, "y")
+
+    def third(self, t):
+        self.arrive(t, "y")
+        self.start(t, "x")
+
+    def fourth(self, t):
+        self.arrive(t, "x")
+        self.start(t, "c")
+
+    def step(self, number):
+        for stage, phase in reversed(list(enumerate((self.first, self.second, self.third, self.fourth)))):
+            if 0 <= number - LAG * stage < len(self.chunks):
+                phase(number - LAG * stage)
+
+    def run(self, number):
+        while self.number < min(number, self.steps):
+            self.step(self.number)
+            self.number += 1
+
+    def landed(self, t):
+        if t not in self.whole:
+            self.arrive(t, "c")
+            self.whole.add(t)
+
+    def finish(self):
+        for t in range(len(self.chunks)):
+            self.landed(t)
+            for kind in "zyxc":
+                for copy in self.make(t, kind):
+                    copy.wait_send()
+
+
+def gather_plan(shards, crossing):
+    shapes = [shard.shape for shard in shards]
+    lines = min(rows for rows, _ in shapes)
+    wholes = [jax.ShapeDtypeStruct((4, 2, 2, *shape), jnp.bfloat16) for shape in shapes]
+    return wholes, chunks_of(shapes, lines, crossing, PIECE), lines
+
+
+def flat(wholes):
+    return [whole.reshape(-1, whole.shape[-1]) for whole in wholes]
+
+
+class Scatter:
+    def __init__(self, me, lefts, rights, small, outs, small_out, chunks, lines, scratch):
+        self.me, self.lefts, self.rights, self.small, self.outs, self.small_out = me, lefts, rights, small, outs, small_out
+        self.chunks, self.lines = chunks, lines
+        (self.strips, self.cols, self.turned, self.own, self.away, self.core_in, self.early_in, self.late_in, self.y_in, self.z_in,
+         self.end_in, self.done, self.strip_sem, self.cols_sem, self.done_sem,
+         self.c_send, self.c_recv, self.x_send, self.x_recv, self.y_send, self.y_recv, self.z_send, self.z_recv,
+         self.small_held, self.small_in, self.small_z, self.small_send, self.small_recv, self.small_z_send, self.small_z_recv) = scratch
+        self.order = [sum(other[3] == chunk[3] for other in chunks[:t]) for t, chunk in enumerate(chunks)]
+        self.steps = len(chunks) + 1 + 4 * WAIT
+
+    @staticmethod
+    def scratch(chunks, lines, tokens, small):
+        dma, low, total = pltpu.SemaphoreType.DMA, jnp.bfloat16, len(chunks)
+        early = sum(chunk[3] for chunk in chunks)
+        late = total - early
+        return [
+            pltpu.VMEM((tokens, 32 * lines), low),
+            pltpu.VMEM((2, 2, tokens, BLOCK), low),
+            pltpu.VMEM((2, 16 * lines, tokens), low),
+            pltpu.VMEM((OWN_SLOTS, 2, 4, 2, lines, BLOCK), low),
+            pltpu.VMEM((AWAY_SLOTS, 2, 4, 2, lines, BLOCK), low),
+            pltpu.VMEM((total, 2, 4, 2, lines, BLOCK), low),
+            pltpu.VMEM((early, 4, 2, lines, BLOCK), low),
+            pltpu.VMEM((late, 2, 4, lines, BLOCK), low),
+            pltpu.VMEM((early, 4, lines, BLOCK), low),
+            pltpu.VMEM((late, 3, 2, lines, BLOCK), low),
+            pltpu.VMEM((total, 3, lines, BLOCK), low),
+            pltpu.VMEM((total, lines, BLOCK), jnp.float32),
+            dma((16,)), dma((2, 2)), dma((total,)),
+            dma((total, 2)), dma((total, 2)), dma((total,)), dma((total,)),
+            dma((total,)), dma((total,)), dma((total, 3)), dma((total, 3)),
+            pltpu.VMEM((4, *small), jnp.float32), pltpu.VMEM((3, *small), jnp.float32), pltpu.VMEM((4, *small), jnp.float32),
+            dma((3,)), dma((3,)), dma((3,)), dma((3,)),
+        ]
+
+    def columns(self, t, j):
+        index, line, column, early = self.chunks[t]
+        return pl.ds(j * (self.rights[index].shape[1] // 2) + column, BLOCK)
+
+    def turns(self, t):
+        index, line, column, early = self.chunks[t]
+        if self.lefts[index].shape[1] > 16 * self.lines:
+            return column == 0 and line % (2 * self.lines) == 0, line // self.lines % 2
+        return column == 0, 0
+
+    def loads(self, t):
+        index, line, column, early = self.chunks[t]
+        left, wide = self.lefts[index], 2 * self.lines
+        copies = [Near(self.rights[index].at[:, self.columns(t, j)], self.cols.at[t % 2, j], self.cols_sem.at[t % 2, j]) for j in range(2)]
+        if self.turns(t)[0]:
+            rows = left.shape[1] // 16
+            if rows > self.lines:
+                copies += [
+                    Near(left.at[:, pl.ds(i * rows + line, wide)], self.strips.at[:, pl.ds(i * wide, wide)], self.strip_sem.at[i])
+                    for i in range(16)
+                ]
+            else:
+                copies.append(Near(left, self.strips.at[:, pl.ds(0, 8 * wide)], self.strip_sem.at[0]))
+        return copies
+
+    def load(self, t):
+        for copy in self.loads(t):
+            copy.start()
+
+    def turn(self, t):
+        lines, me = self.lines, self.me
+        left = self.lefts[self.chunks[t][0]]
+
+        def place(core, block):
+            return pl.ds(pl.multiple_of((lax.rem(core + me.c, 2) * 8 + block) * lines, lines), lines)
+
+        if left.shape[1] > 16 * lines:
+
+            @pl.loop(0, 16)
+            def _(i):
+                block = jnp.transpose(self.strips[:, pl.ds(pl.multiple_of(i * 2 * lines, 2 * lines), 2 * lines)])
+                rows = place(lax.rem(i, 2), lax.div(i, 2))
+                self.turned[0, rows, :] = block[:lines]
+                self.turned[1, rows, :] = block[lines:]
+
+        else:
+
+            @pl.loop(0, 8)
+            def _(i):
+                block = jnp.transpose(self.strips[:, pl.ds(pl.multiple_of(i * 2 * lines, 2 * lines), 2 * lines)])
+                self.turned[0, place(0, i), :] = block[:lines]
+                self.turned[0, place(1, i), :] = block[lines:]
+
+    def make(self, t, kind):
+        index, line, column, early = self.chunks[t]
+        me, own, slot, order = self.me, self.own, t % OWN_SLOTS, self.order[t]
+        if kind == "c":
+            return [
+                Sent(self.away.at[t % AWAY_SLOTS, j], self.core_in.at[t, j], self.c_send.at[t, j], self.c_recv.at[t, j], me.twin())
+                for j in range(2)
+            ]
+        if kind == "x":
+            source, target = (
+                (own.at[slot, 1 - me.x], self.early_in.at[order]) if early
+                else (own.at[slot, 1 - me.x, me.z, me.y], self.end_in.at[t, 0])
+            )
+            return [Sent(source, target, self.x_send.at[t], self.x_recv.at[t], me.across())]
+        if kind == "y":
+            source, target = (
+                (own.at[slot, me.x, :, 1 - me.y], self.y_in.at[order]) if early
+                else (own.at[slot, :, :, 1 - me.y], self.late_in.at[order])
+            )
+            return [Sent(source, target, self.y_send.at[t], self.y_recv.at[t], me.beside())]
+        copies = []
+        for s in (1, 2, 3):
+            z = lax.rem(me.z + s, 4)
+            source, target = (
+                (own.at[slot, me.x, z, me.y], self.end_in.at[t, s - 1]) if early
+                else (own.at[slot, :, z, me.y], self.z_in.at[order, s - 1])
+            )
+            copies.append(Sent(source, target, self.z_send.at[t, s - 1], self.z_recv.at[t, s - 1], me.along(s)))
+        return copies
+
+    def finished(self, t):
+        index, line, column, early = self.chunks[t]
+        return Near(self.done.at[t], self.outs[index].at[pl.ds(line, self.lines), pl.ds(column, BLOCK)], self.done_sem.at[t])
+
+    def make_small(self, stage):
+        me = self.me
+        if stage < 3:
+            peer = (me.twin, me.across, me.beside)[stage]()
+            return [Sent(self.small_held.at[stage], self.small_in.at[stage], self.small_send.at[stage], self.small_recv.at[stage], peer)]
+        return [
+            Sent(self.small_held.at[3], self.small_z.at[me.z], self.small_z_send.at[s - 1], self.small_z_recv.at[s - 1], me.along(s))
+            for s in (1, 2, 3)
+        ]
+
+    def start(self, t, kind):
+        for copy in self.make(t, kind):
+            copy.start()
+
+    def arrive(self, t, kind):
+        for copy in self.make(t, kind):
+            copy.wait_recv()
+
+    def leave(self, t, kinds):
+        for kind in kinds:
+            for copy in self.make(t, kind):
+                copy.wait_send()
+
+    def first(self, t):
+        lines = self.lines
+        for copy in self.loads(t):
+            copy.wait()
+        fresh, which = self.turns(t)
+        if fresh:
+            self.turn(t)
+        if t >= AWAY_SLOTS:
+            self.leave(t - AWAY_SLOTS, "c")
+        if t >= OWN_SLOTS:
+            self.leave(t - OWN_SLOTS, "zyx")
+        for other in (1, 0):
+            target, slot = (self.own, t % OWN_SLOTS) if other == 0 else (self.away, t % AWAY_SLOTS)
+            for j in range(2):
+
+                @pl.loop(0, 2)
+                def _(pair):
+                    rows = pl.ds(pl.multiple_of((other * 2 + pair) * 4 * lines, 4 * lines), 4 * lines)
+                    part = nn(self.turned[which, rows, :], self.cols[t % 2, j]).astype(jnp.bfloat16)
+                    for z in range(2):
+                        for y in range(2):
+                            target[slot, j, 2 * pair + z, y] = part[(2 * z + y) * lines : (2 * z + y + 1) * lines]
+
+                if other == 1:
+                    self.make(t, "c")[j].start()
+
+    def second(self, t):
+        early, slot, own = self.chunks[t][3], t % OWN_SLOTS, self.own
+        self.arrive(t, "c")
+        for j in range(2):
+            for z in range(4):
+                own[slot, j, z] = sums(own[slot, j, z], self.core_in[t, j, z])
+        self.start(t, "x" if early else "y")
+
+    def third(self, t):
+        early, slot, me, own, order = self.chunks[t][3], t % OWN_SLOTS, self.me, self.own, self.order[t]
+        if early:
+            self.arrive(t, "x")
+            for z in range(4):
+                own[slot, me.x, z] = sums(own[slot, me.x, z], self.early_in[order, z])
+            self.start(t, "y")
+        else:
+            self.arrive(t, "y")
+            for j in range(2):
+                for z in range(4):
+                    own[slot, j, z, me.y] = sums(own[slot, j, z, me.y], self.late_in[order, j, z])
+            self.start(t, "z")
+
+    def fourth(self, t):
+        early, slot, me, own, order = self.chunks[t][3], t % OWN_SLOTS, self.me, self.own, self.order[t]
+        if early:
+            self.arrive(t, "y")
+            for z in range(4):
+                own[slot, me.x, z, me.y] = sums(own[slot, me.x, z, me.y], self.y_in[order, z])
+            self.start(t, "z")
+        else:
+            self.arrive(t, "z")
+            for j in range(2):
+                value = own[slot, j, me.z, me.y].astype(jnp.float32)
+                for s in range(3):
+                    value = value + self.z_in[order, s, j].astype(jnp.float32)
+                own[slot, j, me.z, me.y] = value.astype(jnp.bfloat16)
+            self.start(t, "x")
+
+    def fifth(self, t):
+        early, slot, me = self.chunks[t][3], t % OWN_SLOTS, self.me
+        self.arrive(t, "z" if early else "x")
+        value = self.own[slot, me.x, me.z, me.y].astype(jnp.float32)
+        for s in range(3 if early else 1):
+            value = value + self.end_in[t, s].astype(jnp.float32)
+        self.done[t] = value
+        self.finished(t).start()
+
+    def small_step(self, stage):
+        if stage == 0:
+            self.small_held[0] = self.small[...]
+        else:
+            self.make_small(stage - 1)[0].wait_recv()
+            self.small_held[stage] = self.small_held[stage - 1] + self.small_in[stage - 1]
+        if stage == 3:
+            self.small_z[self.me.z] = self.small_held[3]
+        for copy in self.make_small(stage):
+            copy.start()
+
+    def step(self, number):
+        phases = ((1, self.first), (1 + WAIT, self.second), (1 + 2 * WAIT, self.third), (1 + 3 * WAIT, self.fourth), (1 + 4 * WAIT, self.fifth))
+        for lag, phase in reversed(((0, self.load), *phases)):
+            if 0 <= number - lag < len(self.chunks):
+                phase(number - lag)
+        if number % WAIT == 0 and number // WAIT < 4:
+            self.small_step(number // WAIT)
+
+    def finish(self):
+        for copy in self.make_small(3):
+            copy.wait_recv()
+        for stage in range(4):
+            for copy in self.make_small(stage):
+                copy.wait_send()
+        self.small_out[...] = (self.small_z[0] + self.small_z[1]) + (self.small_z[2] + self.small_z[3])
+        total = len(self.chunks)
+        for t in range(total):
+            self.finished(t).wait()
+            if t + AWAY_SLOTS >= total:
+                self.leave(t, "c")
+            if t + OWN_SLOTS >= total:
+                self.leave(t, "zyx")
+
+
+def sums(former, latter):
+    return (former.astype(jnp.float32) + latter.astype(jnp.float32)).astype(jnp.bfloat16)
+
+
+def scatter_kernel(count, chunks, lines, *refs):
     me = Place()
     me.greet()
-    live = {}
-
-    def halves(chunk):
-        index, line, column, early = chunk
-        half = shards[index].shape[1] // 2
-        if early:
-            return [pl.ds(pl.multiple_of(me.x * half + column, PIECE), PIECE)]
-        return [pl.ds(column, PIECE), pl.ds(half + column, PIECE)]
-
-    def both(chunk):
-        half = shards[chunk[0]].shape[1] // 2
-        return [pl.ds(chunk[2], PIECE), pl.ds(half + chunk[2], PIECE)]
-
-    def first(t):
-        index, line, column, early = chunks[t]
-        shard, whole = shards[index], wholes[index]
-        rows = pl.ds(line, lines)
-        live[t, "own"] = []
-        for j, cols in enumerate(halves(chunks[t])):
-            copy = pltpu.make_async_copy(shard.at[rows, cols], whole.at[me.z, me.y, me.c, rows, cols], own_sem.at[t, j])
-            copy.start()
-            live[t, "own"].append(copy)
-        live[t, "z"] = [
-            send(shard.at[rows, cols], whole.at[me.z, me.y, me.c, rows, cols], z_send.at[t, j, s - 1], z_recv.at[t, j, s - 1], me.along(s))
-            for j, cols in enumerate(halves(chunks[t]))
-            for s in (1, 2, 3)
-        ]
-
-    def second(t):
-        index, line, column, early = chunks[t]
-        whole, rows = wholes[index], pl.ds(line, lines)
-        for copy in live[t, "own"]:
-            copy.wait()
-        for copy in live[t, "z"]:
-            copy.wait_recv()
-        live[t, "y"] = [
-            send(whole.at[:, me.y, me.c, rows, cols], whole.at[:, me.y, me.c, rows, cols], y_send.at[t, j], y_recv.at[t, j], me.beside())
-            for j, cols in enumerate(halves(chunks[t]))
-        ]
-
-    def third(t):
-        index, line, column, early = chunks[t]
-        whole, rows = wholes[index], pl.ds(line, lines)
-        for copy in live[t, "y"]:
-            copy.wait_recv()
-        if early:
-            (cols,) = halves(chunks[t])
-            view = whole.at[:, :, me.c, rows, cols]
-            live[t, "x"] = [send(view, view, x_send.at[t], x_recv.at[t], me.across())]
-        else:
-            live[t, "x"] = []
-
-    def fourth(t):
-        index, line, column, early = chunks[t]
-        whole, rows = wholes[index], pl.ds(line, lines)
-        for copy in live[t, "x"]:
-            copy.wait_recv()
-        live[t, "c"] = [
-            send(whole.at[:, :, me.c, rows, cols], whole.at[:, :, me.c, rows, cols], c_send.at[t, j], c_recv.at[t, j], me.twin())
-            for j, cols in enumerate(both(chunks[t]))
-        ]
-
-    total = len(chunks)
-    for step in range(total + 3):
-        for lag, phase in enumerate((first, second, third, fourth)):
-            if 0 <= step - lag < total:
-                phase(step - lag)
-    for t in range(total):
-        for copy in live[t, "c"]:
-            copy.wait_recv()
-        for kind in "zyxc":
-            for copy in live[t, kind]:
-                copy.wait_send()
-
-
-def gather_whole(shards, identity):
-    shapes = [shard.shape for shard in shards]
-    lines = min(rows for rows, _ in shapes)
-    chunks = chunks_of(shapes, lines)
-    count, total = len(shards), len(chunks)
-    dma = pltpu.SemaphoreType.DMA
-    anywhere = pl.BlockSpec(memory_space=pl.ANY)
-    wholes = pl.pallas_call(
-        functools.partial(gather_kernel, count, chunks, lines),
-        in_specs=[anywhere] * count,
-        out_specs=[anywhere] * count,
-        out_shape=[jax.ShapeDtypeStruct((4, 2, 2, *shape), jnp.bfloat16) for shape in shapes],
-        scratch_shapes=[
-            dma((total, 2)), dma((total, 2, 3)), dma((total, 2, 3)), dma((total, 2)), dma((total, 2)),
-            dma((total,)), dma((total,)), dma((total, 2)), dma((total, 2)),
-        ],
-        compiler_params=pltpu.CompilerParams(collective_id=identity, has_side_effects=True, vmem_limit_bytes=4 << 20),
-        name="gather_whole",
-    )(*shards)
-    return [whole.reshape(-1, whole.shape[-1]) for whole in wholes]
-
-
-SLOTS = 5
-
-
-def scatter_kernel(count, chunks, lines, *refs):
-    lefts, rights, small = refs[:count], refs[count : 2 * count], refs[2 * count]
-    outs, small_out = refs[2 * count + 1 : 3 * count + 1], refs[3 * count + 1]
-    (turned, held, core_in, early_in, late_in, y_in, z_in, end_in, done, done_sem,
-     c_send, c_recv, x_send, x_recv, y_send, y_recv, z_send, z_recv,
-     small_held, small_in, small_z, small_send, small_recv, small_z_send, small_z_recv) = refs[3 * count + 2 :]
-    me = Place()
-    me.greet()
-    live = {}
-    order = [sum(other[3] == chunk[3] for other in chunks[:t]) for t, chunk in enumerate(chunks)]
-
-    def columns(chunk, j):
-        return pl.ds(j * (rights[chunk[0]].shape[1] // 2) + chunk[2], PIECE)
-
-    def sums(former, latter):
-        return (former.astype(jnp.float32) + latter.astype(jnp.float32)).astype(jnp.bfloat16)
-
-    def turn(t):
-        index, line, column, early = chunks[t]
-        left, rows = lefts[index], lefts[index].shape[1] // 16
-        if rows > lines:
-            if line % (2 * lines) == 0:
-
-                @pl.loop(0, 16)
-                def _(i):
-                    block = jnp.transpose(left[:, pl.ds(pl.multiple_of(i * rows + line, 2 * lines), 2 * lines)])
-                    turned[0, pl.ds(pl.multiple_of(i * lines, lines), lines), :] = block[:lines]
-                    turned[1, pl.ds(pl.multiple_of(i * lines, lines), lines), :] = block[lines:]
-
-            return line // lines % 2
-        if column == 0:
-
-            @pl.loop(0, 8)
-            def _(i):
-                span = pl.ds(pl.multiple_of(i * 2 * lines, 2 * lines), 2 * lines)
-                turned[0, span, :] = jnp.transpose(left[:, span])
-
-        return 0
-
-    def first(t):
-        slot = t % SLOTS
-        if t >= SLOTS:
-            for kind in "czyx":
-                for copy in live[t - SLOTS, kind]:
-                    copy.wait_send()
-        which = turn(t)
-        right = rights[chunks[t][0]]
-        live[t, "c"] = []
-        for j in range(2):
-            cols = columns(chunks[t], j)
-
-            @pl.loop(0, 4)
-            def _(z):
-                part = nn(turned[which, pl.ds(pl.multiple_of(z * 4 * lines, 4 * lines), 4 * lines), :], right[:, cols]).astype(jnp.bfloat16)
-                for y in range(2):
-                    for core in range(2):
-                        held[slot, core, j, z, y] = part[(2 * y + core) * lines : (2 * y + core + 1) * lines]
-
-            live[t, "c"].append(send(held.at[slot, 1 - me.c, j], core_in.at[t, j], c_send.at[t, j], c_recv.at[t, j], me.twin()))
-
-    def second(t):
-        early, slot = chunks[t][3], t % SLOTS
-        for j in range(2):
-            live[t, "c"][j].wait_recv()
-            for z in range(4):
-                held[slot, me.c, j, z] = sums(held[slot, me.c, j, z], core_in[t, j, z])
-        if early:
-            live[t, "x"] = [send(held.at[slot, me.c, 1 - me.x], early_in.at[order[t]], x_send.at[t], x_recv.at[t], me.across())]
-        else:
-            live[t, "y"] = [send(held.at[slot, me.c, :, :, 1 - me.y], late_in.at[order[t]], y_send.at[t], y_recv.at[t], me.beside())]
-
-    def third(t):
-        early, slot = chunks[t][3], t % SLOTS
-        if early:
-            live[t, "x"][0].wait_recv()
-            for z in range(4):
-                held[slot, me.c, me.x, z] = sums(held[slot, me.c, me.x, z], early_in[order[t], z])
-            live[t, "y"] = [send(held.at[slot, me.c, me.x, :, 1 - me.y], y_in.at[order[t]], y_send.at[t], y_recv.at[t], me.beside())]
-        else:
-            live[t, "y"][0].wait_recv()
-            for j in range(2):
-                for z in range(4):
-                    held[slot, me.c, j, z, me.y] = sums(held[slot, me.c, j, z, me.y], late_in[order[t], j, z])
-            live[t, "z"] = [
-                send(held.at[slot, me.c, :, lax.rem(me.z + s, 4), me.y], z_in.at[order[t], s - 1], z_send.at[t, s - 1], z_recv.at[t, s - 1], me.along(s))
-                for s in (1, 2, 3)
-            ]
-
-    def fourth(t):
-        early, slot = chunks[t][3], t % SLOTS
-        if early:
-            live[t, "y"][0].wait_recv()
-            for z in range(4):
-                held[slot, me.c, me.x, z, me.y] = sums(held[slot, me.c, me.x, z, me.y], y_in[order[t], z])
-            live[t, "z"] = [
-                send(held.at[slot, me.c, me.x, lax.rem(me.z + s, 4), me.y], end_in.at[t, s - 1], z_send.at[t, s - 1], z_recv.at[t, s - 1], me.along(s))
-                for s in (1, 2, 3)
-            ]
-        else:
-            for copy in live[t, "z"]:
-                copy.wait_recv()
-            for j in range(2):
-                value = held[slot, me.c, j, me.z, me.y].astype(jnp.float32)
-                for s in range(3):
-                    value = value + z_in[order[t], s, j].astype(jnp.float32)
-                held[slot, me.c, j, me.z, me.y] = value.astype(jnp.bfloat16)
-            live[t, "x"] = [send(held.at[slot, me.c, 1 - me.x, me.z, me.y], end_in.at[t, 0], x_send.at[t], x_recv.at[t], me.across())]
-
-    def fifth(t):
-        index, line, column, early = chunks[t]
-        slot = t % SLOTS
-        value = held[slot, me.c, me.x, me.z, me.y].astype(jnp.float32)
-        if early:
-            for copy in live[t, "z"]:
-                copy.wait_recv()
-            for s in range(3):
-                value = value + end_in[t, s].astype(jnp.float32)
-        else:
-            live[t, "x"][0].wait_recv()
-            value = value + end_in[t, 0].astype(jnp.float32)
-        done[t] = value
-        copy = pltpu.make_async_copy(done.at[t], outs[index].at[pl.ds(line, lines), pl.ds(column, PIECE)], done_sem.at[t])
-        copy.start()
-        live[t, "done"] = [copy]
-
-    def small_step(stage):
-        if stage > 0:
-            live["small", stage - 1].wait_recv()
-            small_held[stage] = small_held[stage - 1] + small_in[stage - 1]
-        if stage < 3:
-            peer = (me.twin, me.across, me.beside)[stage]()
-            live["small", stage] = send(small_held.at[stage], small_in.at[stage], small_send.at[stage], small_recv.at[stage], peer)
-        else:
-            small_z[me.z] = small_held[3]
-            for s in (1, 2, 3):
-                live["small z", s] = send(small_held.at[3], small_z.at[me.z], small_z_send.at[s - 1], small_z_recv.at[s - 1], me.along(s))
-
-    def small_end():
-        for s in (1, 2, 3):
-            live["small z", s].wait_recv()
-            live["small z", s].wait_send()
-            live["small", s - 1].wait_send()
-        small_out[...] = (small_z[0] + small_z[1]) + (small_z[2] + small_z[3])
-
-    total = len(chunks)
-    small_held[0] = small[...]
-    for step in range(total + 4):
-        if step < 4:
-            small_step(step)
-        for lag, phase in enumerate((first, second, third, fourth, fifth)):
-            if 0 <= step - lag < total:
-                phase(step - lag)
-    small_end()
-    for t in range(total):
-        live[t, "done"][0].wait()
-        if t + SLOTS >= total:
-            for kind in "czyx":
-                for copy in live[t, kind]:
-                    copy.wait_send()
-
-
-def scatter_sums(factors, small, identity):
+    scatter = Scatter(
+        me, refs[:count], refs[count : 2 * count], refs[2 * count], refs[2 * count + 1 : 3 * count + 1], refs[3 * count + 1],
+        chunks, lines, refs[3 * count + 2 :],
+    )
+    for number in range(scatter.steps):
+        scatter.step(number)
+    scatter.finish()
+
+
+def scatter_plan(factors, small, crossing):
     shapes = [(left.shape[1] // 16, right.shape[1]) for left, right in factors]
     lines = min(rows for rows, _ in shapes)
-    chunks = chunks_of(shapes, lines)
-    count, total = len(factors), len(chunks)
-    tokens = factors[0][0].shape[0]
-    dma = pltpu.SemaphoreType.DMA
     anywhere, near = pl.BlockSpec(memory_space=pl.ANY), pl.BlockSpec(memory_space=pltpu.VMEM)
-    low = jnp.bfloat16
-    early = sum(chunk[3] for chunk in chunks)
-    late = total - early
+    outs = [jax.ShapeDtypeStruct((rows, width // 2), jnp.float32) for rows, width in shapes]
+    outs.append(jax.ShapeDtypeStruct(small.shape, jnp.float32))
+    chunks = chunks_of(shapes, lines, crossing, BLOCK)
+    count = len(factors)
+    operands = [left for left, _ in factors] + [right for _, right in factors] + [small]
+    in_specs = [anywhere] * (2 * count) + [near]
+    scratch = Scatter.scratch(chunks, lines, factors[0][0].shape[0], small.shape)
+    return operands, in_specs, outs, [anywhere] * count + [near], scratch, chunks, lines
+
+
+def scatter_sums(factors, small, identity):
+    operands, in_specs, outs, out_specs, scratch, chunks, lines = scatter_plan(factors, small, (2, 3))
     return pl.pallas_call(
-        functools.partial(scatter_kernel, count, chunks, lines),
-        in_specs=[near] * (2 * count + 1),
-        out_specs=[anywhere] * count + [near],
-        out_shape=[jax.ShapeDtypeStruct((rows, width // 2), jnp.float32) for rows, width in shapes]
-        + [jax.ShapeDtypeStruct(small.shape, jnp.float32)],
-        scratch_shapes=[
-            pltpu.VMEM((2, 16 * lines, tokens), low),
-            pltpu.VMEM((SLOTS, 2, 2, 4, 2, lines, PIECE), low),
-            pltpu.VMEM((total, 2, 4, 2, lines, PIECE), low),
-            pltpu.VMEM((early, 4, 2, lines, PIECE), low),
-            pltpu.VMEM((late, 2, 4, lines, PIECE), low),
-            pltpu.VMEM((early, 4, lines, PIECE), low),
-            pltpu.VMEM((late, 3, 2, lines, PIECE), low),
-            pltpu.VMEM((total, 3, lines, PIECE), low),
-            pltpu.VMEM((total, lines, PIECE), jnp.float32),
-            dma((total,)),
-            dma((total, 2)), dma((total, 2)), dma((total,)), dma((total,)),
-            dma((total,)), dma((total,)), dma((total, 3)), dma((total, 3)),
-            pltpu.VMEM((4, *small.shape), jnp.float32),
-            pltpu.VMEM((3, *small.shape), jnp.float32),
-            pltpu.VMEM((4, *small.shape), jnp.float32),
-            dma((3,)), dma((3,)), dma((3,)), dma((3,)),
-        ],
+        functools.partial(scatter_kernel, len(factors), chunks, lines),
+        in_specs=in_specs,
+        out_specs=out_specs,
+        out_shape=outs,
+        scratch_shapes=scratch,
         compiler_params=pltpu.CompilerParams(collective_id=identity, has_side_effects=True, vmem_limit_bytes=60 << 20),
         name="scatter_sums",
-    )(*[left for left, _ in factors], *[right for _, right in factors], small)
+    )(*operands)
 
 
 PAIR = 2
@@ -495,7 +609,7 @@
     return jnp.where(lines + places == width - 1, 1.0, 0.0).astype(jnp.bfloat16)
 
 
-def attend_pair(q_ref, k_ref, v_ref, rel_ref, out_ref, log_ref):
+def attend_pair(q_ref, k_ref, v_ref, rel_ref, out_ref, log_ref, between=lambda block: None):
     length = q_ref.shape[0]
     rows = min(FWD_ROWS, length)
     scale = HEAD ** (-0.5)
@@ -514,18 +628,19 @@
             logs.append(highest + jnp.log(total))
         out_ref[start : start + rows, :] = jnp.concatenate(outs, axis=1).astype(jnp.bfloat16)
         log_ref[start : start + rows, :] = jnp.concatenate(logs, axis=1)
+        between(start // rows)
 
 
 def attend_back_pair(
-    q_ref, k_ref, v_ref, do_ref, log_ref, rel_ref, back_ref, mirror_ref, dq_ref, dk_ref, dv_ref, table_ref, dkt, dvt
+    q_ref, k_ref, v_ref, do_ref, log_ref, rel_ref, back_ref, mirror_ref, dq_ref, dk_ref, dv_ref, table_ref, dkt, dvt, q_turned, do_turned,
+    between=lambda block: None,
 ):
     length = q_ref.shape[0]
     rows = min(BACK_ROWS, length)
     scale = HEAD ** (-0.5)
-    rel, back = rel_ref[...], back_ref[...]
-    q_turned = (jnp.transpose(q_ref[...].astype(jnp.float32)) * scale).astype(jnp.bfloat16)
-    do_turned = jnp.transpose(do_ref[...].astype(jnp.float32)).astype(jnp.bfloat16)
-    table = jnp.zeros((HEAD, LANES), jnp.float32)
+    q_turned[...] = (jnp.transpose(q_ref[...].astype(jnp.float32)) * scale).astype(jnp.bfloat16)
+    do_turned[...] = jnp.transpose(do_ref[...].astype(jnp.float32)).astype(jnp.bfloat16)
+    table_ref[...] = jnp.zeros((HEAD, LANES), jnp.float32)
     for start in range(0, length, rows):
         span = slice(start, start + rows)
         parts = []
@@ -533,7 +648,7 @@
             lanes = slice(h * HEAD, (h + 1) * HEAD)
             query = q_ref[span, lanes] * scale
             scores = nt(query, k_ref[:, lanes])
-            scores = biased_scores(scores, nt(query, rel), start, rows, length)
+            scores = biased_scores(scores, nt(query, rel_ref[...]), start, rows, length)
             weights = jnp.exp(scores - log_ref[span, h : h + 1])
             low_weights = weights.astype(jnp.bfloat16)
             grads = nt(do_ref[span, lanes], v_ref[:, lanes])
@@ -551,12 +666,12 @@
             bucket = bucket_sums(score_grad.astype(jnp.float32), mirror_ref[...], start, rows, length)
             high = bucket.astype(jnp.bfloat16)
             rest = (bucket - high.astype(jnp.float32)).astype(jnp.bfloat16)
-            parts.append((nn(score_grad, k_ref[:, lanes]) + nn(high, back) + nn(rest, back)) * scale)
-            table = table + nn(q_turned[lanes, span], high) + nn(q_turned[lanes, span], rest)
+            parts.append((nn(score_grad, k_ref[:, lanes]) + nn(high, back_ref[...]) + nn(rest, back_ref[...])) * scale)
+            table_ref[...] += nn(q_turned[lanes, span], high) + nn(q_turned[lanes, span], rest)
         dq_ref[span, :] = jnp.concatenate(parts, axis=1).astype(jnp.bfloat16)
+        between(start // rows)
     dk_ref[...] = jnp.transpose(dkt[...]).astype(jnp.bfloat16)
     dv_ref[...] = jnp.transpose(dvt[...]).astype(jnp.bfloat16)
-    table_ref[...] = table
 
 
 def attend_kernel(q_ref, k_ref, v_ref, rel_ref, out_ref, log_ref):
@@ -564,11 +679,11 @@
 
 
 def attend_back_kernel(
-    q_ref, k_ref, v_ref, do_ref, log_ref, rel_ref, back_ref, mirror_ref, dq_ref, dk_ref, dv_ref, table_ref, dkt, dvt
+    q_ref, k_ref, v_ref, do_ref, log_ref, rel_ref, back_ref, mirror_ref, dq_ref, dk_ref, dv_ref, table_ref, dkt, dvt, q_turned, do_turned
 ):
     attend_back_pair(
         q_ref.at[0], k_ref.at[0], v_ref.at[0], do_ref.at[0], log_ref.at[0, 0], rel_ref, back_ref, mirror_ref,
-        dq_ref.at[0], dk_ref.at[0], dv_ref.at[0], table_ref.at[0, 0], dkt, dvt,
+        dq_ref.at[0], dk_ref.at[0], dv_ref.at[0], table_ref.at[0, 0], dkt, dvt, q_turned, do_turned,
     )
 
 
@@ -620,7 +735,7 @@
         ],
         out_specs=[block, block, block, pl.BlockSpec((1, 1, HEAD, LANES), lambda i, j: (i, j, 0, 0))],
         out_shape=[shape, shape, shape, jax.ShapeDtypeStruct((clips, pairs, HEAD, LANES), jnp.float32)],
-        scratch_shapes=[pltpu.VMEM((PAIR * HEAD, length), jnp.float32)] * 2,
+        scratch_shapes=[pltpu.VMEM((PAIR * HEAD, length), jnp.float32)] * 2 + [pltpu.VMEM((PAIR * HEAD, length), jnp.bfloat16)] * 2,
         compiler_params=pltpu.CompilerParams(vmem_limit_bytes=48 << 20),
         cost_estimate=pl.CostEstimate(flops=10 * clips * width * length * length * 4, bytes_accessed=14 * query.size, transcendentals=clips * pairs * PAIR * length * length),
         name="attend_back",
@@ -631,96 +746,16 @@
     return pl.ds(pl.multiple_of(index * LANES, LANES), LANES)
 
 
-def meet_across(me):
-    barrier = pltpu.get_barrier_semaphore()
-    pl.semaphore_signal(barrier, inc=1, device_id=me.across(), device_id_type=MESH)
-    pl.semaphore_wait(barrier, 1)
-
-
-def attend_split_kernel(
-    pairs, p_ref, rel_ref, out_ref, kept_ref, log_ref, qkv, outs, own_sem, send_sem, recv_sem, kept_sem, out_sem, back_send, back_recv
+def attend_back_split_kernel(
+    pairs, count, chunks, lines, do_ref, kept_ref, log_ref, rel_ref, back_ref, mirror_ref, *refs
 ):
+    lefts, rights, small = refs[:count], refs[count : 2 * count], refs[2 * count]
+    dp_ref, table_ref = refs[2 * count + 1 : 2 * count + 3]
+    sums_refs, refs = refs[2 * count + 3 : 3 * count + 4], refs[3 * count + 4 :]
+    grads, qkv, outs, dkt, dvt, q_turned, do_turned, own_sem, send_sem, recv_sem, kept_sem, out_sem, back_send, back_recv = refs[:14]
     me = Place()
-    step = pl.program_id(0)
-    segment = p_ref.shape[0]
-    mine, theirs = pl.ds(me.x * segment, segment), pl.ds((1 - me.x) * segment, segment)
-
-    def leaving(i):
-        return [
-            Sent(p_ref.at[:, strip((2 * part + 1 - me.x) * pairs + i)], qkv.at[i, part, mine, :], send_sem.at[i, part], recv_sem.at[i, part], me.across())
-            for part in range(3)
-        ]
-
-    def staying(i):
-        return [
-            pltpu.make_async_copy(p_ref.at[:, strip((2 * part + me.x) * pairs + i)], qkv.at[i, part, mine, :], own_sem.at[i, part])
-            for part in range(3)
-        ]
-
-    def returns(i):
-        there = out_ref.at[:, strip(me.x * pairs + i)]
-        return (
-            Sent(outs.at[i, theirs, :], there, back_send.at[i], back_recv.at[i], me.across()),
-            pltpu.make_async_copy(outs.at[i, mine, :], there, out_sem.at[i]),
-            pltpu.make_async_copy(qkv.at[i], kept_ref.at[i], kept_sem.at[i]),
-        )
-
-    @pl.when(step == 0)
-    def _():
-        meet_across(me)
-        for i in range(pairs):
-            for copy in leaving(i) + staying(i):
-                copy.start()
-
-    for copy in leaving(step):
-        copy.wait_recv()
-    for copy in staying(step):
-        copy.wait()
-    attend_pair(qkv.at[step, 0], qkv.at[step, 1], qkv.at[step, 2], rel_ref, outs.at[step], log_ref.at[0])
-    for copy in returns(step):
-        copy.start()
-
-    @pl.when(step == pairs - 1)
-    def _():
-        for i in range(pairs):
-            for copy in leaving(i):
-                copy.wait_send()
-            sent, kept, own = returns(i)
-            sent.wait_send()
-            sent.wait_recv()
-            kept.wait()
-            own.wait()
-
-
-def attend_split(projected, rel_low, identity):
-    segment, width = projected.shape[0], projected.shape[1] // 3
-    length, pairs = 2 * segment, width // (2 * PAIR * HEAD)
-    dma, anywhere = pltpu.SemaphoreType.DMA, pl.BlockSpec(memory_space=pl.ANY)
-    return pl.pallas_call(
-        functools.partial(attend_split_kernel, pairs),
-        grid=(pairs,),
-        in_specs=[anywhere, pl.BlockSpec((LANES, HEAD), lambda i: (0, 0))],
-        out_specs=[anywhere, anywhere, pl.BlockSpec((1, length, PAIR), lambda i: (i, 0, 0))],
-        out_shape=[
-            jax.ShapeDtypeStruct((segment, width), jnp.bfloat16),
-            jax.ShapeDtypeStruct((pairs, 3, length, LANES), jnp.bfloat16),
-            jax.ShapeDtypeStruct((pairs, length, PAIR), jnp.float32),
-        ],
-        scratch_shapes=[
-            pltpu.VMEM((pairs, 3, length, LANES), jnp.bfloat16),
-            pltpu.VMEM((pairs, length, LANES), jnp.bfloat16),
-            dma((pairs, 3)), dma((pairs, 3)), dma((pairs, 3)), dma((pairs,)), dma((pairs,)), dma((pairs,)), dma((pairs,)),
-        ],
-        compiler_params=pltpu.CompilerParams(collective_id=identity, has_side_effects=True, vmem_limit_bytes=48 << 20),
-        name="attend_split",
-    )(projected, rel_low)
-
-
-def attend_back_split_kernel(
-    pairs, do_ref, kept_ref, log_ref, rel_ref, back_ref, mirror_ref, dp_ref, table_ref,
-    grads, qkv, outs, dkt, dvt, own_sem, send_sem, recv_sem, kept_sem, out_sem, back_send, back_recv
-):
-    me = Place()
+    scatter = Scatter(me, lefts, rights, small, sums_refs[:count], sums_refs[count], chunks, lines, refs[14:])
+    blocks = kept_ref.shape[2] // min(BACK_ROWS, kept_ref.shape[2])
     step = pl.program_id(0)
     segment = do_ref.shape[0]
     mine, theirs = pl.ds(me.x * segment, segment), pl.ds((1 - me.x) * segment, segment)
@@ -743,18 +778,28 @@
 
     @pl.when(step == 0)
     def _():
-        meet_across(me)
+        me.greet()
         for i in range(pairs):
             leaving(i).start()
             for copy in staying(i):
                 copy.start()
+        scatter.step(0)
+        scatter.step(1)
+
+    def between(block):
+        for i in range(pairs):
+            if 2 + i * blocks + block < scatter.steps:
+
+                @pl.when(step == i)
+                def _():
+                    scatter.step(2 + i * blocks + block)
 
     leaving(step).wait_recv()
     for copy in staying(step):
         copy.wait()
     attend_back_pair(
         qkv.at[step, 0], qkv.at[step, 1], qkv.at[step, 2], grads.at[step], log_ref.at[0], rel_ref, back_ref, mirror_ref,
-        outs.at[step, 0], outs.at[step, 1], outs.at[step, 2], table_ref.at[0], dkt, dvt,
+        outs.at[step, 0], outs.at[step, 1], outs.at[step, 2], table_ref.at[0], dkt, dvt, q_turned, do_turned, between,
     )
     for part in range(3):
         for copy in returns(step, part):
@@ -762,6 +807,9 @@
 
     @pl.when(step == pairs - 1)
     def _():
+        for number in range(2 + pairs * blocks, scatter.steps):
+            scatter.step(number)
+        scatter.finish()
         for i in range(pairs):
             leaving(i).wait_send()
             for part in range(3):
@@ -771,22 +819,24 @@
                 own.wait()
 
 
-def attend_back_split(out_grad, kept, logs, rel_low, identity):
+def attend_back_split(out_grad, kept, logs, rel_low, factors, small, identity):
     segment, width = out_grad.shape
     pairs, _, length, _ = kept.shape
+    operands, more_specs, outs, outs_specs, scratch, chunks, lines = scatter_plan(factors, small, (4, 11))
     dma, anywhere = pltpu.SemaphoreType.DMA, pl.BlockSpec(memory_space=pl.ANY)
     table = pl.BlockSpec((LANES, HEAD), lambda i: (0, 0))
     return pl.pallas_call(
-        functools.partial(attend_back_split_kernel, pairs),
+        functools.partial(attend_back_split_kernel, pairs, len(factors), chunks, lines),
         grid=(pairs,),
         in_specs=[
             anywhere, anywhere, pl.BlockSpec((1, length, PAIR), lambda i: (i, 0, 0)), table, table,
-            pl.BlockSpec((width_of(length),) * 2, lambda i: (0, 0)),
+            pl.BlockSpec((width_of(length),) * 2, lambda i: (0, 0), pipeline_mode=pl.Buffered(1)), *more_specs,
         ],
-        out_specs=[anywhere, pl.BlockSpec((1, HEAD, LANES), lambda i: (i, 0, 0))],
+        out_specs=[anywhere, pl.BlockSpec((1, HEAD, LANES), lambda i: (i, 0, 0)), *outs_specs],
         out_shape=[
             jax.ShapeDtypeStruct((segment, 3 * width), jnp.bfloat16),
             jax.ShapeDtypeStruct((pairs, HEAD, LANES), jnp.float32),
+            *outs,
         ],
         scratch_shapes=[
             pltpu.VMEM((pairs, length, LANES), jnp.bfloat16),
@@ -794,11 +844,209 @@
             pltpu.VMEM((pairs, 3, length, LANES), jnp.bfloat16),
             pltpu.VMEM((LANES, length), jnp.float32),
             pltpu.VMEM((LANES, length), jnp.float32),
+            pltpu.VMEM((LANES, length), jnp.bfloat16),
+            pltpu.VMEM((LANES, length), jnp.bfloat16),
             dma((pairs,)), dma((pairs,)), dma((pairs,)), dma((pairs,)), dma((pairs, 3)), dma((pairs, 3)), dma((pairs, 3)),
+            *scratch,
         ],
-        compiler_params=pltpu.CompilerParams(collective_id=identity, has_side_effects=True, vmem_limit_bytes=48 << 20),
+        compiler_params=pltpu.CompilerParams(collective_id=identity, has_side_effects=True, vmem_limit_bytes=62 << 20),
         name="attend_back_split",
-    )(out_grad, kept, logs, rel_low, rel_low[::-1], mirror_of(width_of(length)))
+    )(out_grad, kept, logs, rel_low, rel_low[::-1], mirror_of(width_of(length)), *operands)
+
+
+def normed_rows(values, gain, shift):
+    center = values - jnp.mean(values, axis=1, keepdims=True)
+    spread = jnp.mean(center * center, axis=1, keepdims=True)
+    return center * lax.rsqrt(spread + EPSILON) * gain + shift
+
+
+def front_kernel(
+    pairs, count, chunks, lines, tokens_ref, rel_ref, gains_ref, shifts_ref, hidden_bias_ref, model_bias_ref, *refs
+):
+    shards, refs = refs[:count], refs[count:]
+    normed_ref, hidden_ref, active_ref, after_ref, attn_ref, out_ref, kept_ref, log_ref = refs[:8]
+    wholes, refs = refs[8 : 8 + count], refs[8 + count :]
+    (branch, projected, strips, blocks, qkv, outs, strip_sem, block_sem,
+     own_sem, send_sem, recv_sem, kept_sem, out_sem, back_send, back_recv) = refs[:15]
+    me = Place()
+    gather = Gather(me, shards, wholes, chunks, lines, refs[15:])
+    me.greet()
+    segment, width = tokens_ref.shape
+    low = jnp.bfloat16
+    ROWS = 128
+
+    def chunks_for(index):
+        return [t for t, chunk in enumerate(chunks) if chunk[0] == index]
+
+    def whole_by_now(t):
+        gather.run(t + 3 * LAG + 1)
+        gather.landed(t)
+
+    def strip_copies(t):
+        index, line, column, early = chunks[t]
+        half = shards[index].shape[1] // 2
+        return [
+            Near(wholes[index].at[:, :, :, :, pl.ds(j * half + column, PIECE)], strips.at[t % 2, j], strip_sem.at[t % 2, j])
+            for j in range(2)
+        ]
+
+    def load_strips(t):
+        whole_by_now(t)
+        for copy in strip_copies(t):
+            copy.start()
+
+    def strip_spans(t):
+        index, line, column, early = chunks[t]
+        for copy in strip_copies(t):
+            copy.wait()
+        for j in range(2):
+            start = j * (shards[index].shape[1] // 2) + column
+            yield slice(start, start + PIECE), strips[t % 2, j].reshape(width, PIECE)
+
+    def widen(t):
+        for span, weight in strip_spans(t):
+            hidden = nn(normed_ref[...], weight) + hidden_bias_ref[0:1, span]
+            hidden_ref[:, span] = hidden.astype(low)
+            active_ref[:, span] = (hidden * jax.nn.sigmoid(hidden)).astype(low)
+
+    def project(t):
+        for span, weight in strip_spans(t):
+            part = span.start // width
+            value = nn(attn_ref[...], weight)
+            if part != 1:
+                value = value + model_bias_ref[part // 2 + 1 : part // 2 + 2, span.start % width : span.start % width + PIECE]
+            projected[:, span] = value.astype(low)
+
+    def in_turn(numbers, load, use):
+        load(numbers[0])
+        for former, latter in zip(numbers, numbers[1:] + [None]):
+            if latter is not None:
+                load(latter)
+            use(former)
+
+    gather.run(LAG)
+    for start in range(0, segment, ROWS):
+        rows = slice(start, start + ROWS)
+        values = tokens_ref[rows, :].astype(jnp.float32)
+        normed_ref[rows, :] = normed_rows(values, gains_ref[0:1, :], shifts_ref[0:1, :]).astype(low)
+    in_turn(chunks_for(0), load_strips, widen)
+    for t in chunks_for(1):
+        whole_by_now(t)
+    tall = wholes[1].shape[3]
+
+    def block_copy(f):
+        return Near(wholes[1].at[f // 4, f // 2 % 2, f % 2], blocks.at[f % 2], block_sem.at[f % 2])
+
+    def narrow(f):
+        block_copy(f).wait()
+        value = nn(active_ref[:, f * tall : (f + 1) * tall], blocks[f % 2])
+        if f == 0:
+            branch[...] = value
+        else:
+            branch[...] += value
+        if f % 4 == 3:
+            gather.run(gather.number + 1)
+
+    block_copy(0).start()
+    for f in range(16):
+        if f < 15:
+            block_copy(f + 1).start()
+        narrow(f)
+    for start in range(0, segment, ROWS):
+        rows = slice(start, start + ROWS)
+        values = tokens_ref[rows, :].astype(jnp.float32) + 0.5 * (branch[rows, :] + model_bias_ref[0:1, :])
+        after_ref[rows, :] = values
+        attn_ref[rows, :] = normed_rows(values, gains_ref[1:2, :], shifts_ref[1:2, :]).astype(low)
+    in_turn(chunks_for(2), load_strips, project)
+
+    mine, theirs = pl.ds(me.x * segment, segment), pl.ds((1 - me.x) * segment, segment)
+
+    def leaving(i):
+        return [
+            Sent(projected.at[:, strip((2 * part + 1 - me.x) * pairs + i)], qkv.at[i, part, mine, :], send_sem.at[i, part], recv_sem.at[i, part], me.across())
+            for part in range(3)
+        ]
+
+    def staying(i):
+        return [
+            Near(projected.at[:, strip((2 * part + me.x) * pairs + i)], qkv.at[i, part, mine, :], own_sem.at[i, part])
+            for part in range(3)
+        ]
+
+    def returns(i):
+        there = out_ref.at[:, strip(me.x * pairs + i)]
+        return (
+            Sent(outs.at[i, theirs, :], there, back_send.at[i], back_recv.at[i], me.across()),
+            Near(outs.at[i, mine, :], there, out_sem.at[i]),
+            Near(qkv.at[i], kept_ref.at[i], kept_sem.at[i]),
+        )
+
+    for i in range(pairs):
+        for copy in leaving(i) + staying(i):
+            copy.start()
+    gather.run(gather.number + 1)
+    for i in range(pairs):
+        for copy in leaving(i):
+            copy.wait_recv()
+        for copy in staying(i):
+            copy.wait()
+
+        def between(block):
+            if block % 2 == 1:
+                gather.run(gather.number + 1)
+
+        attend_pair(qkv.at[i, 0], qkv.at[i, 1], qkv.at[i, 2], rel_ref, outs.at[i], log_ref.at[i], between)
+        for copy in returns(i):
+            copy.start()
+    gather.run(gather.steps)
+    gather.finish()
+    for i in range(pairs):
+        for copy in leaving(i):
+            copy.wait_send()
+        sent, own, kept = returns(i)
+        sent.wait_send()
+        sent.wait_recv()
+        own.wait()
+        kept.wait()
+
+
+def front(tokens, rel_low, norm_gains, norm_biases, hidden_biases, model_biases, shards, identity):
+    segment, width = tokens.shape
+    hidden = shards[0].shape[1]
+    length, pairs, count = 2 * segment, width // (2 * PAIR * HEAD), len(shards)
+    wholes, chunks, lines = gather_plan(shards, (4, 7))
+    dma, low = pltpu.SemaphoreType.DMA, jnp.bfloat16
+    anywhere, near = pl.BlockSpec(memory_space=pl.ANY), pl.BlockSpec(memory_space=pltpu.VMEM)
+    *kept, = pl.pallas_call(
+        functools.partial(front_kernel, pairs, count, chunks, lines),
+        in_specs=[near] * 6 + [anywhere] * count,
+        out_specs=[near] * 5 + [anywhere] * 2 + [near] + [anywhere] * count,
+        out_shape=[
+            jax.ShapeDtypeStruct((segment, width), low),
+            jax.ShapeDtypeStruct((segment, hidden), low),
+            jax.ShapeDtypeStruct((segment, hidden), low),
+            jax.ShapeDtypeStruct((segment, width), jnp.float32),
+            jax.ShapeDtypeStruct((segment, width), low),
+            jax.ShapeDtypeStruct((segment, width), low),
+            jax.ShapeDtypeStruct((pairs, 3, length, LANES), low),
+            jax.ShapeDtypeStruct((pairs, length, PAIR), jnp.float32),
+            *wholes,
+        ],
+        scratch_shapes=[
+            pltpu.VMEM((segment, width), jnp.float32),
+            pltpu.VMEM((segment, 3 * width), low),
+            pltpu.VMEM((2, 2, 4, 2, 2, lines, PIECE), low),
+            pltpu.VMEM((2, hidden // 16, width), low),
+            pltpu.VMEM((pairs, 3, length, LANES), low),
+            pltpu.VMEM((pairs, length, LANES), low),
+            dma((2, 2)), dma((2,)),
+            dma((pairs, 3)), dma((pairs, 3)), dma((pairs, 3)), dma((pairs,)), dma((pairs,)), dma((pairs,)), dma((pairs,)),
+            *Gather.scratch(len(chunks)),
+        ],
+        compiler_params=pltpu.CompilerParams(collective_id=identity, has_side_effects=True, vmem_limit_bytes=60 << 20),
+        name="front",
+    )(tokens, rel_low, norm_gains, norm_biases, hidden_biases, model_biases, *shards)
+    return kept[:8], flat(kept[8:])
 
 
 TAPS = 32
@@ -977,30 +1225,31 @@
         weight.astype(low)
         for weight in (ffn1_up, ffn1_down, qkv_weight, out_weight, conv_in, conv_out, ffn2_up, ffn2_down)
     ]
+    rel_low = padded_table(rel_table)
+    input_rows = tokens.reshape(row_count, model_width).astype(jnp.float32)
     if close:
-        weights = gather_whole(shards, 0)
+        fronts, weights = front(
+            tokens.reshape(row_count, model_width), rel_low, norm_gains, norm_biases, hidden_biases, model_biases, shards, 0
+        )
+        normed_one, hidden_one, active_one, after_one, normed_attn, attn_rows, kept_heads, log_totals = fronts
+        kept_one = (normed_one, hidden_one.astype(jnp.float32), active_one)
     else:
         weights = [lax.all_gather(shard, "fsdp", axis=0, tiled=True) for shard in shards]
+        branch_one, kept_one = feed_forward(
+            input_rows,
+            norm_gains[0],
+            norm_biases[0],
+            weights[0],
+            hidden_biases[0],
+            weights[1],
+            model_biases[0],
+        )
+        after_one = input_rows + 0.5 * branch_one
+        normed_attn = layer_norm(after_one, norm_gains[1], norm_biases[1]).astype(low)
+        project_bias = jnp.concatenate([model_biases[1], jnp.zeros_like(model_biases[1]), model_biases[2]])
+        projected = (product(normed_attn, weights[2]) + project_bias).astype(low)
+        attn_rows, kept_heads, log_totals = heads_of(projected, clip_count, segment, rel_low)
     up_one, down_one, qkv_full, out_full, conv_first, conv_second, up_two, down_two = weights
-    input_rows = tokens.reshape(row_count, model_width).astype(jnp.float32)
-    branch_one, kept_one = feed_forward(
-        input_rows,
-        norm_gains[0],
-        norm_biases[0],
-        up_one,
-        hidden_biases[0],
-        down_one,
-        model_biases[0],
-    )
-    after_one = input_rows + 0.5 * branch_one
-    normed_attn = layer_norm(after_one, norm_gains[1], norm_biases[1]).astype(low)
-    project_bias = jnp.concatenate([model_biases[1], jnp.zeros_like(model_biases[1]), model_biases[2]])
-    projected = (product(normed_attn, qkv_full) + project_bias).astype(low)
-    rel_low = padded_table(rel_table)
-    if close:
-        attn_rows, kept_heads, log_totals = attend_split(projected, rel_low, 1)
-    else:
-        attn_rows, kept_heads, log_totals = heads_of(projected, clip_count, segment, rel_low)
     after_two = after_one + product(attn_rows, out_full) + model_biases[3]
     normed_conv = layer_norm(after_two, norm_gains[2], norm_biases[2]).astype(low)
     gate_input = product(normed_conv, conv_first)
@@ -1042,24 +1291,24 @@
     conv_norm_pull = jax.vjp(layer_norm, after_two, norm_gains[2], norm_biases[2])[1]
     values_grad, gain_two, shift_two = conv_norm_pull(times_transposed(gate_grad, conv_first))
     grad_two = grad_three + values_grad
-    sums_of = partial(scatter_sums, identity=2) if close else spread_sums
     later_small = stacked(
         [gain_two, gain_three, gain_four, gain_five, shift_two, shift_three, shift_four, shift_five]
         + [up_two_bias, down_two_bias, kernel_grad]
     )
-    conv_first_sum, conv_second_sum, up_two_sum, down_two_sum, later_sum = sums_of(
-        [(normed_conv, gate_grad), (swished, conv_grad), up_two_factors, down_two_factors],
-        later_small,
-    )
+    later_factors = [down_two_factors, up_two_factors, (swished, conv_grad), (normed_conv, gate_grad)]
     attn_grad = grad_two.astype(low)
     out_bias_grad = jnp.sum(attn_grad.astype(jnp.float32), axis=0)
     merged_grad = times_transposed(attn_grad, out_full).astype(low)
     if close:
-        projected_grad, table_parts = attend_back_split(merged_grad, kept_heads, log_totals, rel_low, 3)
+        projected_grad, table_parts, *later_sums = attend_back_split(
+            merged_grad, kept_heads, log_totals, rel_low, later_factors, later_small, 3
+        )
     else:
         projected_grad, table_parts = heads_back(
             merged_grad, kept_heads, log_totals, clip_count, segment, rel_low
         )
+        later_sums = spread_sums(later_factors, later_small)
+    down_two_sum, up_two_sum, conv_second_sum, conv_first_sum, later_sum = later_sums
     table_grad = jnp.sum(table_parts, axis=0).T[::-1][:BUCKETS]
     query_bias_grad = jnp.sum(projected_grad[:, :model_width].astype(jnp.float32), axis=0)
     value_bias_grad = jnp.sum(projected_grad[:, 2 * model_width :].astype(jnp.float32), axis=0)

time: 853 us -> 752 us (0.88)
  Pallas kernels: 649 us -> 574 us
  local copies, waits for them, and re-layouts: 47.7 us -> 31.9 us
  matrix products: 99.6 us -> 87.4 us
    pallas_call x5 -> x3, Pallas kernels: 628 us -> 554 us  [the longest x1 266 us: front(): pl.pallas_call(functools.partial(front_kernel, pairs, count, chunks, line...]
    dot_general x8 -> x5, matrix products: 45.2 us -> 25.7 us  [product(): return jnp.dot(former, latter, preferred_element_type=jnp.float32)]
    unnamed x192 -> x128, local copies, waits for them, and re-layouts: 34.5 us -> 20.9 us
  transfers between devices with their start and end apart: 2 -> 2, of which waited for: 2 -> 1; matrix products, arithmetic and copies ran while one was open for 0% -> 0% of each run, Pallas kernels for 0% -> 0%
where the time goes in v4:
time: 752 us; the launch traced here: 742 us
  Pallas kernels  574 us (76%)
  matrix products  87.4 us (12%)
  other arithmetic  38.5 us (5%)
  local copies, waits for them, and re-layouts  31.9 us (4%)
    pallas_call x1, Pallas kernels, front(): pl.pallas_call(functools.partial(front_kernel, pairs, count, chunks, line...  266 us
    pallas_call x1, Pallas kernels, attend_back_split(): pl.pallas_call(functools.partial(attend_back_split_kernel, pairs, len(fac...  161 us
    pallas_call x1, Pallas kernels, scatter_sums(): pl.pallas_call(functools.partial(scatter_kernel, len(factors), chunks, li...  127 us
    dot_general x8, matrix products, times_transposed(): lax.dot_general(former, latter, (((1,), (1,)), ((), ())), preferred_eleme...  61.7 us
    dot_general x5, matrix products, product(): return jnp.dot(former, latter, preferred_element_type=jnp.float32)  25.7 us
    unnamed x128, local copies, waits for them, and re-layouts  20.9 us
  transfers between devices with their start and end apart: 2, of which 1 were waited for; matrix products, arithmetic and copies ran while one was open for 0% of the time, Pallas kernels for 0%

profile of v4, /device:TPU:0, one launch (start us, length us, event | category | flops | bytes accessed | tf_op | source)
XLA Modules:
  0.0 741.7 jit_solution(7257045105010129939)
XLA Ops:
  1.7 2.2 convert_element_type.124.refs_0_
  11.5 266.0 %front.1 = (bf16[512,1024]{1,0:T(8,128)(2,1)}, bf16[512,4096]{1,0:T(8,128)(2,1)}, bf16[512,4096]{1,0:T(8,128)(2,1)}, f32[512,1024]{1,0:T(8,128)}, bf16[512,1024]...) custom-call(bf16[512,1024]{1,0:T(8,128)(2,1)} %bitcast.130, ...), custom_call_target="tpu_custom_call" | custom-call | tf_op jit(solution)/shard_map/front/pallas_call | solution.py:1020
  277.5 3.9 fusion.64
  284.7 2.4 fusion.67.value_ref.gate_ref
  289.2 3.2 collective-permute-start
  295.9 7.5 %depthwise.1 = f32[1,512,1024]{2,1,0:T(8,128)} custom-call(bf16[1,544,1024]{2,1,0:T(8,128)(2,1)} %pad_maximum_fusion.wide_ref, f32[32,1024]{1,0:T(8,128)} %pad.22.taps_ref), custom_call_target="tpu_custom_call" | custom-call | flops 32505856 | bytes 3145728 | tf_op jit(solution)/shard_map/depthwise/pallas_call | solution.py:1096
  307.1 3.4 fusion.65
  311.2 7.5 %multiply_convert_fusion = (bf16[512,4096]{1,0:T(8,128)(2,1)S(1)}, f32[512,4096]{1,0:T(8,128)}) fusion(f32[4096]{0:T(1024)S(1)} %bitcast.157, bf16[512,1024]{1,0:T(8,128)(2,1)S(1)} %add_convert_fusion.3.refs_1_, bf16[1024,4096]{1,0:T(8,128)(2,1)S(1)} %bitcast.183), kind=kOutput, calls=%fused_computation.15 | convolution fusion | flops 4307550208 | bytes 22036480 | tf_op jit(solution)/shard_map/dot_general | solution.py:34
  318.8 8.5 %fusion.66 = (f32[512]{0:T(512)S(1)}, f32[512,1024]{1,0:T(8,128)S(1)}) fusion(f32[512,1024]{1,0:T(8,128)S(1)} %get-tuple-element.204, f32[1024]{0:T(1024)S(1)} %bitcast.174, bf16[512,4096]{1,0:T(8,128)(2,1)S(1)} %get-tuple-element.205.refs_0_, bf16[4096,1024]{1,0:T(8,128)(2,1)} %bitcast.184), kind=kOutput, calls=%fused_computation.155 | convolution fusion | flops 4297063936 | bytes 16783360 | tf_op jit(solution)/shard_map/dot_general | solution.py:34
  330.8 12.0 %convert_reduce_fusion.1 = (f32[4096]{0:T(1024)S(1)}, bf16[512,4096]{1,0:T(8,128)(2,1)S(1)}) fusion(f32[512,4096]{1,0:T(8,128)} %get-tuple-element.206, f32[4096]{0:T(1024)S(1)} %bitcast.158, bf16[512,1024]{1,0:T(8,128)(2,1)S(1)} %get-tuple-element.165.refs_4_, bf16[4096,1024]{1,0:T(8,128)(2,1)} %bitcast.185), kind=kOutput, calls=%fused_computation.14 | convolution fusion | flops 4322226176 | bytes 22052864 | tf_op jit(solution)/shard_map/dot_general | solution.py:44
  342.9 9.5 %multiply_reduce_fusion.3 = (f32[1024]{0:T(1024)S(1)}, f32[512]{0:T(512)S(1)}, f32[1024]{0:T(1024)S(1)}, f32[512,1024]{1,0:T(8,128)S(1)}) fusion(f32[512,1024]{1,0:T(8,128)S(1)} %get-tuple-element.204, f32[512]{0:T(512)S(1)} %fusion.42, f32[512]{0:T(512)S(1)} %broadcast_multiply_fusion.3, f32[1024]{0:T(1024)S(1)} %bitcast.145, ...), kind=kOutput, calls=%fused_computation.61 | convolution fusion | flops 4299159040 | bytes 16795648 | tf_op jit(solution)/shard_map/dot_general | solution.py:44
  355.3 3.5 multiply_reduce_fusion.4
  362.5 3.4 collective-permute-done.1
  367.0 13.4 %depthwise_back.1 = (bf16[512,1024]{1,0:T(8,128)(2,1)}, bf16[512,1024]{1,0:T(8,128)(2,1)}, f32[32,1024]{1,0:T(8,128)}) custom-call(bf16[1,544,1024]{2,1,0:T(8,128)(2,1)} %pad_maximum_fusion.1.grad_ref, bf16[1,544,1024]{2,1,0:T(8,128)(2,1)} %pad_maximum_fusion.wide_ref, f32[32,1024]{1,0:T(8,128)} %pad.22.taps_ref, f32[512,2048]{1,0:T(8,128)} %copy-done, ...), custom_call_target="tpu_custom_call" | custom-call | flops 65011712 | bytes 8388608 | tf_op jit(solution)/shard_map/depthwise_back/pallas_call | solution.py:1118
  382.7 7.0 multiply_reduce_fusion.5
  390.7 2.4 fusion.53
  395.7 2.3 convolution_convert_fusion.do_ref
  398.0 160.7 %attend_back_split.1 = (bf16[512,3072]{1,0:T(8,128)(2,1)}, f32[4,64,128]{2,1,0:T(8,128)}, f32[256,512]{1,0:T(8,128)}, f32[64,2048]{1,0:T(8,128)}, f32[64,512]{1,...) custom-call(bf16[512,1024]{1,0:T(8,128)(2,1)} %convolution_convert_fusion.do_ref, ...), custom_call_target="tpu_custom_call" | custom-call | tf_op jit(solution)/shard_map/attend_back_split/pallas_call | solution.py:828
  558.8 2.0 convert_reduce_fusion.5
  561.0 7.0 multiply_reduce_fusion
  573.5 11.8 %convert_reduce_fusion = (f32[4096]{0:T(1024)S(1)}, bf16[512,4096]{1,0:T(8,128)(2,1)}) fusion(bf16[512,4096]{1,0:T(8,128)(2,1)S(1)} %copy-done.51, bf16[512,1024]{1,0:T(8,128)(2,1)S(1)} %get-tuple-element.158.refs_5_, bf16[4096,1024]{1,0:T(8,128)(2,1)} %bitcast.179), kind=kOutput, calls=%fused_computation.13 | convolution fusion | flops 4322226176 | bytes 17842176 | tf_op jit(solution)/shard_map/dot_general | solution.py:44
  585.7 8.6 %fusion.48 = (f32[1024]{0:T(1024)S(1)}, f32[512]{0:T(512)S(1)}, f32[512]{0:T(512)S(1)}, f32[512,1024]{1,0:T(8,128)S(1)}) fusion(f32[1024]{0:T(1024)S(1)} %bitcast.138, f32[512]{0:T(512)S(1)} %copy-done.50, bf16[1,512,1024]{2,1,0:T(8,128)(2,1)S(1)} %copy-done.12, bf16[512,4096]{1,0:T(8,128)(2,1)} %get-tuple-element.161.refs_4_, bf16[1024,4096]{1,0:T(8,128)(2,1)} %bitcast.178), kind=kOutput, calls=%fused_computation.141 | convolution fusion | flops 4299159552 | bytes 15742976 | tf_op jit(solution)/shard_map/dot_general | solution.py:44
  596.1 126.8 %scatter_sums.1 = (f32[64,2048]{1,0:T(8,128)}, f32[256,512]{1,0:T(8,128)}, f32[64,1536]{1,0:T(8,128)}, f32[64,512]{1,0:T(8,128)}, f32[24,1024]{1,0:T(8,128)}) custom-call(bf16[512,1024]{1,0:T(8,128)(2,1)} %get-tuple-element.66.refs_0_, bf16[512,4096]{1,0:T(8,128)(2,1)} %get-tuple-element.67.refs_1_, bf16[512,1024]{1,0:T(8,128)(2,1)} %get-tuple-element.68.refs_2_, ...), custom_call_target="tpu_custom_call" | custom-call | tf_op jit(solution)/shard_map/scatter_sums/pallas_call | solution.py:528
  732.1 3.4 fusion.32
  (225 shorter events, 61.7 us)
Async XLA Ops:
  0.7 4.1 copy-start.26
  5.6 4.6 copy-start.46
  5.6 5.2 copy-start.47
  287.1 5.4 copy-start.11
  287.1 5.6 copy-start.2
  289.2 5.6 collective-permute-start
  305.7 5.5 slice-start
  307.1 4.2 slice-start.1
  311.2 7.6 %copy-start.19 = (bf16[512,1024]{1,0:T(8,128)(2,1)}, bf16[512,1024]{1,0:T(8,128)(2,1)S(1)}, u32[]{:S(2)}) copy-start(bf16[512,1024]{1,0:T(8,128)(2,1)S(1)} %add_convert_fusion.3.refs_1_) | copy-start | bytes 3145732
  318.8 8.6 %copy-start.22 = (bf16[512,4096]{1,0:T(8,128)(2,1)}, bf16[512,4096]{1,0:T(8,128)(2,1)S(1)}, u32[]{:S(2)}) copy-start(bf16[512,4096]{1,0:T(8,128)(2,1)S(1)} %get-tuple-element.205.refs_0_) | copy-start | bytes 12582916
  330.8 12.1 %copy-start.20 = (bf16[512,1024]{1,0:T(8,128)(2,1)}, bf16[512,1024]{1,0:T(8,128)(2,1)S(1)}, u32[]{:S(2)}) copy-start(bf16[512,1024]{1,0:T(8,128)(2,1)S(1)} %get-tuple-element.165.refs_4_) | copy-start | bytes 3145732
  342.9 9.5 %copy-start.23 = (bf16[512,4096]{1,0:T(8,128)(2,1)}, bf16[512,4096]{1,0:T(8,128)(2,1)S(1)}, u32[]{:S(2)}) copy-start(bf16[512,4096]{1,0:T(8,128)(2,1)S(1)} %get-tuple-element.167.refs_5_) | copy-start | bytes 12582916
  359.7 6.2 collective-permute-start.1
  382.7 7.0 copy-start.14
  382.7 7.0 copy-start.41
  572.2 13.1 %copy-start.24 = (bf16[512,1024]{1,0:T(8,128)(2,1)}, bf16[512,1024]{1,0:T(8,128)(2,1)S(1)}, u32[]{:S(2)}) copy-start(bf16[512,1024]{1,0:T(8,128)(2,1)S(1)} %get-tuple-element.158.refs_5_) | copy-start | bytes 3145732
  573.5 11.8 %copy-start.42 = (f32[4,64,128]{2,1,0:T(8,128)S(1)}, f32[4,64,128]{2,1,0:T(8,128)}, u32[]{:S(2)}) copy-start(f32[4,64,128]{2,1,0:T(8,128)} %get-tuple-element.69) | copy-start | bytes 393220
  573.5 12.2 %copy-start.12 = (bf16[1,512,1024]{2,1,0:T(8,128)(2,1)S(1)}, bf16[1,512,1024]{2,1,0:T(8,128)(2,1)}, u32[]{:S(2)}) copy-start(bf16[1,512,1024]{2,1,0:T(8,128)(2,1)} %param.16) | copy-start | bytes 3145732
  573.5 12.2 %copy-start.49 = (f32[1,1024]{1,0:T(1,128)S(1)}, f32[1,1024]{1,0:T(1,128)}, u32[]{:S(2)}) copy-start(f32[1,1024]{1,0:T(1,128)} %get-tuple-element.187) | copy-start | bytes 12292
  573.5 12.2 %copy-start.50 = (f32[512]{0:T(512)S(1)}, f32[512]{0:T(512)}, u32[]{:S(2)}) copy-start(f32[512]{0:T(512)} %broadcast_multiply_fusion) | copy-start | bytes 6148
  596.1 128.3 %copy-start.40 = (f32[48,1024]{1,0:T(8,128)S(1)}, f32[48,1024]{1,0:T(8,128)}, u32[]{:S(2)}) copy-start(f32[48,1024]{1,0:T(8,128)} %get-tuple-element.79) | copy-start | bytes 589828
  732.1 4.2 copy-start.34
  735.5 4.4 copy-start.33
  736.3 4.4 copy-start.32
  (35 other events, 83.9 us)

commit v5 on v4

--- a/solution.py
+++ b/solution.py
@@ -57,7 +57,7 @@
 
 MESH = pl.DeviceIdType.MESH
 PIECE = 256
-LAG = 2
+LAG = 3
 BLOCK = 512
 WAIT = 2
 OWN_SLOTS = 8
@@ -93,12 +93,13 @@
 
 
 def chunks_of(shapes, lines, crossing, piece):
-    part, whole = crossing
+    shares = [(part, whole) for blocks, part, whole in crossing for _ in range(blocks)]
     found = []
     for index, (rows, width) in enumerate(shapes):
         for line in range(0, rows, lines):
             for column in range(0, width // 2, piece):
                 count = len(found)
+                part, whole = shares[min(count, len(shares) - 1)]
                 found.append((index, line, column, (count + 1) * part // whole > count * part // whole))
     return found
 
@@ -240,9 +241,9 @@
 
 
 class Scatter:
-    def __init__(self, me, lefts, rights, small, outs, small_out, chunks, lines, scratch):
+    def __init__(self, me, lefts, rights, small, outs, small_out, chunks, lines, scratch, small_from=0):
         self.me, self.lefts, self.rights, self.small, self.outs, self.small_out = me, lefts, rights, small, outs, small_out
-        self.chunks, self.lines = chunks, lines
+        self.chunks, self.lines, self.small_from, self.number = chunks, lines, small_from, 0
         (self.strips, self.cols, self.turned, self.own, self.away, self.core_in, self.early_in, self.late_in, self.y_in, self.z_in,
          self.end_in, self.done, self.strip_sem, self.cols_sem, self.done_sem,
          self.c_send, self.c_recv, self.x_send, self.x_recv, self.y_send, self.y_recv, self.z_send, self.z_recv,
@@ -474,8 +475,14 @@
         for lag, phase in reversed(((0, self.load), *phases)):
             if 0 <= number - lag < len(self.chunks):
                 phase(number - lag)
-        if number % WAIT == 0 and number // WAIT < 4:
-            self.small_step(number // WAIT)
+        stage = (number - self.small_from) // WAIT
+        if (number - self.small_from) % WAIT == 0 and 0 <= stage < 4:
+            self.small_step(stage)
+
+    def run(self, number):
+        while self.number < min(number, self.steps):
+            self.step(self.number)
+            self.number += 1
 
     def finish(self):
         for copy in self.make_small(3):
@@ -504,8 +511,7 @@
         me, refs[:count], refs[count : 2 * count], refs[2 * count], refs[2 * count + 1 : 3 * count + 1], refs[3 * count + 1],
         chunks, lines, refs[3 * count + 2 :],
     )
-    for number in range(scatter.steps):
-        scatter.step(number)
+    scatter.run(scatter.steps)
     scatter.finish()
 
 
@@ -524,7 +530,7 @@
 
 
 def scatter_sums(factors, small, identity):
-    operands, in_specs, outs, out_specs, scratch, chunks, lines = scatter_plan(factors, small, (2, 3))
+    operands, in_specs, outs, out_specs, scratch, chunks, lines = scatter_plan(factors, small, [(1, 2, 3)])
     return pl.pallas_call(
         functools.partial(scatter_kernel, len(factors), chunks, lines),
         in_specs=in_specs,
@@ -822,7 +828,7 @@
 def attend_back_split(out_grad, kept, logs, rel_low, factors, small, identity):
     segment, width = out_grad.shape
     pairs, _, length, _ = kept.shape
-    operands, more_specs, outs, outs_specs, scratch, chunks, lines = scatter_plan(factors, small, (4, 11))
+    operands, more_specs, outs, outs_specs, scratch, chunks, lines = scatter_plan(factors, small, [(1, 6, 11)])
     dma, anywhere = pltpu.SemaphoreType.DMA, pl.BlockSpec(memory_space=pl.ANY)
     table = pl.BlockSpec((LANES, HEAD), lambda i: (0, 0))
     return pl.pallas_call(
@@ -854,6 +860,9 @@
     )(out_grad, kept, logs, rel_low, rel_low[::-1], mirror_of(width_of(length)), *operands)
 
 
+CROSSING = [(24, 2, 3), (12, 1, 4), (1, 2, 3)]
+
+
 def normed_rows(values, gain, shift):
     center = values - jnp.mean(values, axis=1, keepdims=True)
     spread = jnp.mean(center * center, axis=1, keepdims=True)
@@ -1014,7 +1023,7 @@
     segment, width = tokens.shape
     hidden = shards[0].shape[1]
     length, pairs, count = 2 * segment, width // (2 * PAIR * HEAD), len(shards)
-    wholes, chunks, lines = gather_plan(shards, (4, 7))
+    wholes, chunks, lines = gather_plan(shards, CROSSING)
     dma, low = pltpu.SemaphoreType.DMA, jnp.bfloat16
     anywhere, near = pl.BlockSpec(memory_space=pl.ANY), pl.BlockSpec(memory_space=pltpu.VMEM)
     *kept, = pl.pallas_call(

time: 752 us -> 720 us (0.957)
  Pallas kernels: 574 us -> 541 us
    pallas_call x1, Pallas kernels: 266 us -> 242 us  [front(): pl.pallas_call(functools.partial(front_kernel, pairs, count, chunks, line...]
    pallas_call x1, Pallas kernels: 161 us -> 150 us  [attend_back_split(): pl.pallas_call(functools.partial(attend_back_split_kernel, pairs, len(fac...]
  transfers between devices with their start and end apart: 2 -> 2, of which waited for: 1 -> 1; matrix products, arithmetic and copies ran while one was open for 0% -> 1% of each run, Pallas kernels for 0% -> 0%
where the time goes in v5:
time: 720 us; the launch traced here: 710 us
  Pallas kernels  541 us (75%)
  matrix products  87.3 us (12%)
  other arithmetic  38.5 us (5%)
  local copies, waits for them, and re-layouts  31.9 us (4%)
    pallas_call x1, Pallas kernels, front(): pl.pallas_call(functools.partial(front_kernel, pairs, count, chunks, line...  242 us
    pallas_call x1, Pallas kernels, attend_back_split(): pl.pallas_call(functools.partial(attend_back_split_kernel, pairs, len(fac...  150 us
    pallas_call x1, Pallas kernels, scatter_sums(): pl.pallas_call(functools.partial(scatter_kernel, len(factors), chunks, li...  128 us
    dot_general x8, matrix products, times_transposed(): lax.dot_general(former, latter, (((1,), (1,)), ((), ())), preferred_eleme...  61.7 us
    dot_general x5, matrix products, product(): return jnp.dot(former, latter, preferred_element_type=jnp.float32)  25.7 us
    unnamed x128, local copies, waits for them, and re-layouts  20.9 us
  transfers between devices with their start and end apart: 2, of which 1 were waited for; matrix products, arithmetic and copies ran while one was open for 1% of the time, Pallas kernels for 0%

profile of v5, /device:TPU:0, one launch (start us, length us, event | category | flops | bytes accessed | tf_op | source)
XLA Modules:
  0.0 709.8 jit_solution(17937113360668993430)
XLA Ops:
  1.7 2.2 convert_element_type.124.refs_0_
  11.5 241.9 %front.1 = (bf16[512,1024]{1,0:T(8,128)(2,1)}, bf16[512,4096]{1,0:T(8,128)(2,1)}, bf16[512,4096]{1,0:T(8,128)(2,1)}, f32[512,1024]{1,0:T(8,128)}, bf16[512,1024]...) custom-call(bf16[512,1024]{1,0:T(8,128)(2,1)} %bitcast.130, ...), custom_call_target="tpu_custom_call" | custom-call | tf_op jit(solution)/shard_map/front/pallas_call | solution.py:1029
  253.3 3.9 fusion.64
  260.6 2.4 fusion.67.value_ref.gate_ref
  265.1 4.9 collective-permute-start
  273.5 7.5 %depthwise.1 = f32[1,512,1024]{2,1,0:T(8,128)} custom-call(bf16[1,544,1024]{2,1,0:T(8,128)(2,1)} %pad_maximum_fusion.wide_ref, f32[32,1024]{1,0:T(8,128)} %pad.22.taps_ref), custom_call_target="tpu_custom_call" | custom-call | flops 32505856 | bytes 3145728 | tf_op jit(solution)/shard_map/depthwise/pallas_call | solution.py:1105
  284.6 3.4 fusion.65
  288.8 7.5 %multiply_convert_fusion = (bf16[512,4096]{1,0:T(8,128)(2,1)S(1)}, f32[512,4096]{1,0:T(8,128)}) fusion(f32[4096]{0:T(1024)S(1)} %bitcast.157, bf16[512,1024]{1,0:T(8,128)(2,1)S(1)} %add_convert_fusion.3.refs_1_, bf16[1024,4096]{1,0:T(8,128)(2,1)S(1)} %bitcast.183), kind=kOutput, calls=%fused_computation.15 | convolution fusion | flops 4307550208 | bytes 22036480 | tf_op jit(solution)/shard_map/dot_general | solution.py:34
  296.3 8.5 %fusion.66 = (f32[512]{0:T(512)S(1)}, f32[512,1024]{1,0:T(8,128)S(1)}) fusion(f32[512,1024]{1,0:T(8,128)S(1)} %get-tuple-element.204, f32[1024]{0:T(1024)S(1)} %bitcast.174, bf16[512,4096]{1,0:T(8,128)(2,1)S(1)} %get-tuple-element.205.refs_0_, bf16[4096,1024]{1,0:T(8,128)(2,1)} %bitcast.184), kind=kOutput, calls=%fused_computation.155 | convolution fusion | flops 4297063936 | bytes 16783360 | tf_op jit(solution)/shard_map/dot_general | solution.py:34
  308.3 12.0 %convert_reduce_fusion.1 = (f32[4096]{0:T(1024)S(1)}, bf16[512,4096]{1,0:T(8,128)(2,1)S(1)}) fusion(f32[512,4096]{1,0:T(8,128)} %get-tuple-element.206, f32[4096]{0:T(1024)S(1)} %bitcast.158, bf16[512,1024]{1,0:T(8,128)(2,1)S(1)} %get-tuple-element.165.refs_4_, bf16[4096,1024]{1,0:T(8,128)(2,1)} %bitcast.185), kind=kOutput, calls=%fused_computation.14 | convolution fusion | flops 4322226176 | bytes 22052864 | tf_op jit(solution)/shard_map/dot_general | solution.py:44
  320.4 9.5 %multiply_reduce_fusion.3 = (f32[1024]{0:T(1024)S(1)}, f32[512]{0:T(512)S(1)}, f32[1024]{0:T(1024)S(1)}, f32[512,1024]{1,0:T(8,128)S(1)}) fusion(f32[512,1024]{1,0:T(8,128)S(1)} %get-tuple-element.204, f32[512]{0:T(512)S(1)} %fusion.42, f32[512]{0:T(512)S(1)} %broadcast_multiply_fusion.3, f32[1024]{0:T(1024)S(1)} %bitcast.145, ...), kind=kOutput, calls=%fused_computation.61 | convolution fusion | flops 4299159040 | bytes 16795648 | tf_op jit(solution)/shard_map/dot_general | solution.py:44
  332.8 3.5 multiply_reduce_fusion.4
  340.0 3.4 collective-permute-done.1
  344.5 13.4 %depthwise_back.1 = (bf16[512,1024]{1,0:T(8,128)(2,1)}, bf16[512,1024]{1,0:T(8,128)(2,1)}, f32[32,1024]{1,0:T(8,128)}) custom-call(bf16[1,544,1024]{2,1,0:T(8,128)(2,1)} %pad_maximum_fusion.1.grad_ref, bf16[1,544,1024]{2,1,0:T(8,128)(2,1)} %pad_maximum_fusion.wide_ref, f32[32,1024]{1,0:T(8,128)} %pad.22.taps_ref, f32[512,2048]{1,0:T(8,128)} %copy-done, ...), custom_call_target="tpu_custom_call" | custom-call | flops 65011712 | bytes 8388608 | tf_op jit(solution)/shard_map/depthwise_back/pallas_call | solution.py:1127
  360.2 7.0 multiply_reduce_fusion.5
  368.2 2.4 fusion.53
  373.2 2.3 convolution_convert_fusion.do_ref
  375.5 150.4 %attend_back_split.1 = (bf16[512,3072]{1,0:T(8,128)(2,1)}, f32[4,64,128]{2,1,0:T(8,128)}, f32[256,512]{1,0:T(8,128)}, f32[64,2048]{1,0:T(8,128)}, f32[64,512]{1,...) custom-call(bf16[512,1024]{1,0:T(8,128)(2,1)} %convolution_convert_fusion.do_ref, ...), custom_call_target="tpu_custom_call" | custom-call | tf_op jit(solution)/shard_map/attend_back_split/pallas_call | solution.py:834
  525.9 2.0 convert_reduce_fusion.5
  528.2 7.0 multiply_reduce_fusion
  540.6 11.8 %convert_reduce_fusion = (f32[4096]{0:T(1024)S(1)}, bf16[512,4096]{1,0:T(8,128)(2,1)}) fusion(bf16[512,4096]{1,0:T(8,128)(2,1)S(1)} %copy-done.51, bf16[512,1024]{1,0:T(8,128)(2,1)S(1)} %get-tuple-element.158.refs_5_, bf16[4096,1024]{1,0:T(8,128)(2,1)} %bitcast.179), kind=kOutput, calls=%fused_computation.13 | convolution fusion | flops 4322226176 | bytes 17842176 | tf_op jit(solution)/shard_map/dot_general | solution.py:44
  552.9 8.6 %fusion.48 = (f32[1024]{0:T(1024)S(1)}, f32[512]{0:T(512)S(1)}, f32[512]{0:T(512)S(1)}, f32[512,1024]{1,0:T(8,128)S(1)}) fusion(f32[1024]{0:T(1024)S(1)} %bitcast.138, f32[512]{0:T(512)S(1)} %copy-done.50, bf16[1,512,1024]{2,1,0:T(8,128)(2,1)S(1)} %copy-done.12, bf16[512,4096]{1,0:T(8,128)(2,1)} %get-tuple-element.161.refs_4_, bf16[1024,4096]{1,0:T(8,128)(2,1)} %bitcast.178), kind=kOutput, calls=%fused_computation.141 | convolution fusion | flops 4299159552 | bytes 15742976 | tf_op jit(solution)/shard_map/dot_general | solution.py:44
  563.3 127.7 %scatter_sums.1 = (f32[64,2048]{1,0:T(8,128)}, f32[256,512]{1,0:T(8,128)}, f32[64,1536]{1,0:T(8,128)}, f32[64,512]{1,0:T(8,128)}, f32[24,1024]{1,0:T(8,128)}) custom-call(bf16[512,1024]{1,0:T(8,128)(2,1)} %get-tuple-element.66.refs_0_, bf16[512,4096]{1,0:T(8,128)(2,1)} %get-tuple-element.67.refs_1_, bf16[512,1024]{1,0:T(8,128)(2,1)} %get-tuple-element.68.refs_2_, ...), custom_call_target="tpu_custom_call" | custom-call | tf_op jit(solution)/shard_map/scatter_sums/pallas_call | solution.py:534
  700.2 3.4 fusion.32
  (225 shorter events, 61.7 us)
Async XLA Ops:
  5.6 4.6 copy-start.46
  5.6 5.2 copy-start.47
  263.0 7.0 copy-start.11
  263.0 7.2 %copy-start.2 = (f32[512,1024]{1,0:T(8,128)S(1)}, f32[512,1024]{1,0:T(8,128)}, u32[]{:S(2)}) copy-start(f32[512,1024]{1,0:T(8,128)} %get-tuple-element.49) | copy-start | bytes 6291460
  265.1 4.9 copy-start.15
  265.1 7.2 %collective-permute-start = (bf16[1,30,1024]{2,1,0:T(8,128)(2,1)S(1)}, bf16[1,30,1024]{2,1,0:T(8,128)(2,1)S(1)}, u32[]{:S(2)}, u32[]{:S(2)}) collective-permute-start(bf16[1,30,1024]{2,1,0:T(8,128)(2,1)S(1)} %slice.150), channel_id=1, source_target_pairs={{0,16},{1,17},{2,18},{3,19},{4,20},{5,21},{6,22},{7,23},{8,24},{9,... | collective-permute-start | bytes 184328 | tf_op jit(solution)/shard_map/ppermute | solution.py:24
  283.2 5.5 slice-start
  284.6 4.2 slice-start.1
  288.7 7.6 %copy-start.19 = (bf16[512,1024]{1,0:T(8,128)(2,1)}, bf16[512,1024]{1,0:T(8,128)(2,1)S(1)}, u32[]{:S(2)}) copy-start(bf16[512,1024]{1,0:T(8,128)(2,1)S(1)} %add_convert_fusion.3.refs_1_) | copy-start | bytes 3145732
  296.3 8.6 %copy-start.22 = (bf16[512,4096]{1,0:T(8,128)(2,1)}, bf16[512,4096]{1,0:T(8,128)(2,1)S(1)}, u32[]{:S(2)}) copy-start(bf16[512,4096]{1,0:T(8,128)(2,1)S(1)} %get-tuple-element.205.refs_0_) | copy-start | bytes 12582916
  308.3 12.1 %copy-start.20 = (bf16[512,1024]{1,0:T(8,128)(2,1)}, bf16[512,1024]{1,0:T(8,128)(2,1)S(1)}, u32[]{:S(2)}) copy-start(bf16[512,1024]{1,0:T(8,128)(2,1)S(1)} %get-tuple-element.165.refs_4_) | copy-start | bytes 3145732
  320.4 9.5 %copy-start.23 = (bf16[512,4096]{1,0:T(8,128)(2,1)}, bf16[512,4096]{1,0:T(8,128)(2,1)S(1)}, u32[]{:S(2)}) copy-start(bf16[512,4096]{1,0:T(8,128)(2,1)S(1)} %get-tuple-element.167.refs_5_) | copy-start | bytes 12582916
  337.2 6.2 collective-permute-start.1
  360.2 7.0 copy-start.14
  360.2 7.0 copy-start.41
  539.3 13.1 %copy-start.24 = (bf16[512,1024]{1,0:T(8,128)(2,1)}, bf16[512,1024]{1,0:T(8,128)(2,1)S(1)}, u32[]{:S(2)}) copy-start(bf16[512,1024]{1,0:T(8,128)(2,1)S(1)} %get-tuple-element.158.refs_5_) | copy-start | bytes 3145732
  540.6 11.8 %copy-start.42 = (f32[4,64,128]{2,1,0:T(8,128)S(1)}, f32[4,64,128]{2,1,0:T(8,128)}, u32[]{:S(2)}) copy-start(f32[4,64,128]{2,1,0:T(8,128)} %get-tuple-element.69) | copy-start | bytes 393220
  540.6 12.2 %copy-start.12 = (bf16[1,512,1024]{2,1,0:T(8,128)(2,1)S(1)}, bf16[1,512,1024]{2,1,0:T(8,128)(2,1)}, u32[]{:S(2)}) copy-start(bf16[1,512,1024]{2,1,0:T(8,128)(2,1)} %param.16) | copy-start | bytes 3145732
  540.6 12.2 %copy-start.49 = (f32[1,1024]{1,0:T(1,128)S(1)}, f32[1,1024]{1,0:T(1,128)}, u32[]{:S(2)}) copy-start(f32[1,1024]{1,0:T(1,128)} %get-tuple-element.187) | copy-start | bytes 12292
  540.6 12.2 %copy-start.50 = (f32[512]{0:T(512)S(1)}, f32[512]{0:T(512)}, u32[]{:S(2)}) copy-start(f32[512]{0:T(512)} %broadcast_multiply_fusion) | copy-start | bytes 6148
  563.3 129.3 %copy-start.40 = (f32[48,1024]{1,0:T(8,128)S(1)}, f32[48,1024]{1,0:T(8,128)}, u32[]{:S(2)}) copy-start(f32[48,1024]{1,0:T(8,128)} %get-tuple-element.79) | copy-start | bytes 589828
  700.2 4.2 copy-start.34
  703.6 4.4 copy-start.33
  704.4 4.4 copy-start.32
  (35 other events, 84.8 us)

commit v6 on v5

--- a/solution.py
+++ b/solution.py
@@ -1205,6 +1205,34 @@
 def stacked(rows):
     lines = jnp.concatenate([row.reshape(-1, rows[0].shape[-1]) for row in rows])
     return jnp.pad(lines, ((0, -lines.shape[0] % 8), (0, 0)))
+
+
+def split_small_kernel(early, later, gains, firsts, lasts, hidden, model, others, taps, table):
+    width = early.shape[1]
+    rows = hidden.shape[1] // width
+    gains[0:2, :], gains[2:6, :] = early[0:2, :], later[0:4, :]
+    firsts[0:2, :], firsts[2:3, :] = early[2:4, :], later[4:5, :]
+    lasts[...] = later[5:8, :]
+    for k in range(rows):
+        span = slice(k * width, (k + 1) * width)
+        hidden[0:1, span], hidden[1:2, span] = early[4 + k : 5 + k, :], later[8 + k : 9 + k, :]
+    at, then = 4 + rows, 8 + rows
+    model[...] = early[at : at + 3, :]
+    others[0:1, :], others[1:2, :] = early[at + 3 : at + 4, :], later[then : then + 1, :]
+    taps[...] = later[then + 1 : then + 1 + KERNEL, :]
+    for b in range(BUCKETS):
+        row, lane = at + 4 + b * HEAD // width, b * HEAD % width
+        table[b : b + 1, :] = early[row : row + 1, lane : lane + HEAD]
+
+
+def split_small(early, later, hidden_width):
+    width = early.shape[1]
+    shapes = [(6, width), (3, width), (3, width), (2, hidden_width), (3, width), (2, width), (KERNEL, width), (BUCKETS, HEAD)]
+    return pl.pallas_call(
+        split_small_kernel,
+        out_shape=[jax.ShapeDtypeStruct(shape, jnp.float32) for shape in shapes],
+        name="split_small",
+    )(early, later)
 
 
 def body(
@@ -1341,11 +1369,6 @@
         [up_one_factors, down_one_factors, (normed_attn, projected_grad), (attn_rows, attn_grad)],
         early_small,
     )
-    hidden_rows = up_one_bias.size // model_width
-    after_hidden = 4 + hidden_rows
-    table_at = after_hidden + 4
-    table_sum = early_sum[table_at : table_at + table_rows.shape[0]].reshape(-1)[: table_flat.size]
-    later_hidden = 8 + hidden_rows
     return (
         output,
         input_grad,
@@ -1357,14 +1380,7 @@
         conv_second_sum,
         up_two_sum,
         down_two_sum,
-        jnp.concatenate([early_sum[0:2], later_sum[0:4]]),
-        jnp.concatenate([early_sum[2:4], later_sum[4:5]]),
-        later_sum[5:8],
-        jnp.stack([early_sum[4:after_hidden].reshape(-1), later_sum[8:later_hidden].reshape(-1)]),
-        early_sum[after_hidden : after_hidden + 3],
-        jnp.concatenate([early_sum[after_hidden + 3 : table_at], later_sum[later_hidden : later_hidden + 1]]),
-        later_sum[later_hidden + 1 : later_hidden + 1 + KERNEL],
-        table_sum.reshape(table_grad.shape),
+        *split_small(early_sum, later_sum, up_one_bias.size),
     )
 
 

time: 720 us -> 713 us (level)
    unnamed x128 -> x122, local copies, waits for them, and re-layouts: 20.9 us -> 20.9 us
where the time goes in v6:
time: 713 us; the launch traced here: 704 us
  Pallas kernels  543 us (76%)
  matrix products  87.3 us (12%)
  other arithmetic  36 us (5%)
  local copies, waits for them, and re-layouts  26.7 us (4%)
    pallas_call x1, Pallas kernels, front(): pl.pallas_call(functools.partial(front_kernel, pairs, count, chunks, line...  242 us
    pallas_call x1, Pallas kernels, attend_back_split(): pl.pallas_call(functools.partial(attend_back_split_kernel, pairs, len(fac...  150 us
    pallas_call x1, Pallas kernels, scatter_sums(): pl.pallas_call(functools.partial(scatter_kernel, len(factors), chunks, li...  128 us
    dot_general x8, matrix products, times_transposed(): lax.dot_general(former, latter, (((1,), (1,)), ((), ())), preferred_eleme...  61.7 us
    dot_general x5, matrix products, product(): return jnp.dot(former, latter, preferred_element_type=jnp.float32)  25.7 us
    unnamed x122, local copies, waits for them, and re-layouts  20.9 us
  transfers between devices with their start and end apart: 2, of which 1 were waited for; matrix products, arithmetic and copies ran while one was open for 1% of the time, Pallas kernels for 0%

profile of v6, /device:TPU:0, one launch (start us, length us, event | category | flops | bytes accessed | tf_op | source)
XLA Modules:
  0.0 703.7 jit_solution(11169663122568382450)
XLA Ops:
  1.7 2.2 convert_element_type.124.refs_0_
  11.5 241.9 %front.1 = (bf16[512,1024]{1,0:T(8,128)(2,1)}, bf16[512,4096]{1,0:T(8,128)(2,1)}, bf16[512,4096]{1,0:T(8,128)(2,1)}, f32[512,1024]{1,0:T(8,128)}, bf16[512,1024]...) custom-call(bf16[512,1024]{1,0:T(8,128)(2,1)} %bitcast.121, ...), custom_call_target="tpu_custom_call" | custom-call | tf_op jit(solution)/shard_map/front/pallas_call | solution.py:1029
  253.3 3.9 fusion.62
  260.6 2.4 fusion.65.value_ref.gate_ref
  265.1 4.9 collective-permute-start
  273.5 7.5 %depthwise.1 = f32[1,512,1024]{2,1,0:T(8,128)} custom-call(bf16[1,544,1024]{2,1,0:T(8,128)(2,1)} %pad_maximum_fusion.wide_ref, f32[32,1024]{1,0:T(8,128)} %pad.22.taps_ref), custom_call_target="tpu_custom_call" | custom-call | flops 32505856 | bytes 3145728 | tf_op jit(solution)/shard_map/depthwise/pallas_call | solution.py:1105
  284.6 3.4 fusion.63
  288.8 7.5 %multiply_convert_fusion = (bf16[512,4096]{1,0:T(8,128)(2,1)S(1)}, f32[512,4096]{1,0:T(8,128)}) fusion(f32[4096]{0:T(1024)S(1)} %bitcast.145, bf16[512,1024]{1,0:T(8,128)(2,1)S(1)} %add_convert_fusion.3.refs_1_, bf16[1024,4096]{1,0:T(8,128)(2,1)S(1)} %bitcast.171), kind=kOutput, calls=%fused_computation.15 | convolution fusion | flops 4307550208 | bytes 22036480 | tf_op jit(solution)/shard_map/dot_general | solution.py:34
  296.3 8.5 %fusion.64 = (f32[512]{0:T(512)S(1)}, f32[512,1024]{1,0:T(8,128)S(1)}) fusion(f32[512,1024]{1,0:T(8,128)S(1)} %get-tuple-element.232, f32[1024]{0:T(1024)S(1)} %bitcast.162, bf16[512,4096]{1,0:T(8,128)(2,1)S(1)} %get-tuple-element.233.refs_0_, bf16[4096,1024]{1,0:T(8,128)(2,1)} %bitcast.172), kind=kOutput, calls=%fused_computation.147 | convolution fusion | flops 4297063936 | bytes 16783360 | tf_op jit(solution)/shard_map/dot_general | solution.py:34
  308.3 12.0 %convert_reduce_fusion.1 = (f32[4096]{0:T(1024)S(1)}, bf16[512,4096]{1,0:T(8,128)(2,1)S(1)}) fusion(f32[512,4096]{1,0:T(8,128)} %get-tuple-element.234, f32[4096]{0:T(1024)S(1)} %bitcast.146, bf16[512,1024]{1,0:T(8,128)(2,1)S(1)} %get-tuple-element.199.refs_4_, bf16[4096,1024]{1,0:T(8,128)(2,1)} %bitcast.173), kind=kOutput, calls=%fused_computation.14 | convolution fusion | flops 4322226176 | bytes 22052864 | tf_op jit(solution)/shard_map/dot_general | solution.py:44
  320.4 9.5 %multiply_reduce_fusion.3 = (f32[1024]{0:T(1024)S(1)}, f32[512]{0:T(512)S(1)}, f32[1024]{0:T(1024)S(1)}, f32[512,1024]{1,0:T(8,128)S(1)}) fusion(f32[512,1024]{1,0:T(8,128)S(1)} %get-tuple-element.232, f32[512]{0:T(512)S(1)} %fusion.42, f32[512]{0:T(512)S(1)} %broadcast_multiply_fusion.3, f32[1024]{0:T(1024)S(1)} %bitcast.133, ...), kind=kOutput, calls=%fused_computation.61 | convolution fusion | flops 4299159040 | bytes 16795648 | tf_op jit(solution)/shard_map/dot_general | solution.py:44
  332.8 3.5 multiply_reduce_fusion.4
  340.0 3.4 collective-permute-done.1
  344.5 13.4 %depthwise_back.1 = (bf16[512,1024]{1,0:T(8,128)(2,1)}, bf16[512,1024]{1,0:T(8,128)(2,1)}, f32[32,1024]{1,0:T(8,128)}) custom-call(bf16[1,544,1024]{2,1,0:T(8,128)(2,1)} %pad_maximum_fusion.1.grad_ref, bf16[1,544,1024]{2,1,0:T(8,128)(2,1)} %pad_maximum_fusion.wide_ref, f32[32,1024]{1,0:T(8,128)} %pad.22.taps_ref, f32[512,2048]{1,0:T(8,128)} %copy-done, ...), custom_call_target="tpu_custom_call" | custom-call | flops 65011712 | bytes 8388608 | tf_op jit(solution)/shard_map/depthwise_back/pallas_call | solution.py:1127
  360.2 7.0 multiply_reduce_fusion.5
  368.2 2.4 fusion.53
  373.2 2.3 convolution_convert_fusion.do_ref
  375.5 150.4 %attend_back_split.1 = (bf16[512,3072]{1,0:T(8,128)(2,1)}, f32[4,64,128]{2,1,0:T(8,128)}, f32[256,512]{1,0:T(8,128)}, f32[64,2048]{1,0:T(8,128)}, f32[64,512]{1,...) custom-call(bf16[512,1024]{1,0:T(8,128)(2,1)} %convolution_convert_fusion.do_ref, ...), custom_call_target="tpu_custom_call" | custom-call | tf_op jit(solution)/shard_map/attend_back_split/pallas_call | solution.py:834
  525.9 2.0 convert_reduce_fusion.5
  528.2 7.0 %multiply_reduce_fusion = (f32[1024]{0:T(1024)S(1)}, f32[512]{0:T(512)S(1)}, f32[1024]{0:T(1024)S(1)}, f32[512,1024]{1,0:T(8,128)S(1)}) fusion(f32[512,1024]{1,0:T(8,128)S(1)} %copy-done.3, f32[512]{0:T(512)S(1)} %fusion.44, f32[512]{0:T(512)S(1)} %broadcast_multiply_fusion.1, f32[1024]{0:T(1024)S(1)} %bitcast.147, ...), kind=kOutput, calls=%fused_computation.54 | convolution fusion | flops 3225417216 | bytes 13649920 | tf_op jit(solution)/shard_map/dot_general | solution.py:44
  540.6 11.8 %convert_reduce_fusion = (f32[4096]{0:T(1024)S(1)}, bf16[512,4096]{1,0:T(8,128)(2,1)}) fusion(bf16[512,4096]{1,0:T(8,128)(2,1)S(1)} %copy-done.50, bf16[512,1024]{1,0:T(8,128)(2,1)S(1)} %get-tuple-element.192.refs_5_, bf16[4096,1024]{1,0:T(8,128)(2,1)} %bitcast.167), kind=kOutput, calls=%fused_computation.13 | convolution fusion | flops 4322226176 | bytes 17842176 | tf_op jit(solution)/shard_map/dot_general | solution.py:44
  552.9 8.6 %fusion.48 = (f32[1024]{0:T(1024)S(1)}, f32[512]{0:T(512)S(1)}, f32[512]{0:T(512)S(1)}, f32[512,1024]{1,0:T(8,128)S(1)}) fusion(f32[1024]{0:T(1024)S(1)} %bitcast.126, f32[512]{0:T(512)S(1)} %copy-done.49, bf16[1,512,1024]{2,1,0:T(8,128)(2,1)S(1)} %copy-done.12, bf16[512,4096]{1,0:T(8,128)(2,1)} %get-tuple-element.195.refs_4_, bf16[1024,4096]{1,0:T(8,128)(2,1)} %bitcast.166), kind=kOutput, calls=%fused_computation.135 | convolution fusion | flops 4299159552 | bytes 15742976 | tf_op jit(solution)/shard_map/dot_general | solution.py:44
  563.3 127.7 %scatter_sums.1 = (f32[64,2048]{1,0:T(8,128)}, f32[256,512]{1,0:T(8,128)}, f32[64,1536]{1,0:T(8,128)}, f32[64,512]{1,0:T(8,128)}, f32[24,1024]{1,0:T(8,128)}) custom-call(bf16[512,1024]{1,0:T(8,128)(2,1)} %get-tuple-element.74.refs_0_, bf16[512,4096]{1,0:T(8,128)(2,1)} %get-tuple-element.75.refs_1_, bf16[512,1024]{1,0:T(8,128)(2,1)} %get-tuple-element.76.refs_2_, ...), custom_call_target="tpu_custom_call" | custom-call | tf_op jit(solution)/shard_map/scatter_sums/pallas_call | solution.py:534
  694.2 3.4 fusion.32
  (208 shorter events, 55.7 us)
Async XLA Ops:
  0.7 4.1 copy-start.26
  5.6 4.6 copy-start.45
  5.6 5.2 copy-start.46
  263.0 7.0 copy-start.11
  263.0 7.2 %copy-start.2 = (f32[512,1024]{1,0:T(8,128)S(1)}, f32[512,1024]{1,0:T(8,128)}, u32[]{:S(2)}) copy-start(f32[512,1024]{1,0:T(8,128)} %get-tuple-element.57) | copy-start | bytes 6291460
  265.1 4.9 copy-start.15
  265.1 7.2 %collective-permute-start = (bf16[1,30,1024]{2,1,0:T(8,128)(2,1)S(1)}, bf16[1,30,1024]{2,1,0:T(8,128)(2,1)S(1)}, u32[]{:S(2)}, u32[]{:S(2)}) collective-permute-start(bf16[1,30,1024]{2,1,0:T(8,128)(2,1)S(1)} %slice.94), channel_id=1, source_target_pairs={{0,16},{1,17},{2,18},{3,19},{4,20},{5,21},{6,22},{7,23},{8,24},{9,... | collective-permute-start | bytes 184328 | tf_op jit(solution)/shard_map/ppermute | solution.py:24
  283.2 5.5 slice-start
  284.6 4.2 slice-start.1
  288.7 7.6 %copy-start.19 = (bf16[512,1024]{1,0:T(8,128)(2,1)}, bf16[512,1024]{1,0:T(8,128)(2,1)S(1)}, u32[]{:S(2)}) copy-start(bf16[512,1024]{1,0:T(8,128)(2,1)S(1)} %add_convert_fusion.3.refs_1_) | copy-start | bytes 3145732
  296.3 8.6 %copy-start.22 = (bf16[512,4096]{1,0:T(8,128)(2,1)}, bf16[512,4096]{1,0:T(8,128)(2,1)S(1)}, u32[]{:S(2)}) copy-start(bf16[512,4096]{1,0:T(8,128)(2,1)S(1)} %get-tuple-element.233.refs_0_) | copy-start | bytes 12582916
  308.3 12.1 %copy-start.20 = (bf16[512,1024]{1,0:T(8,128)(2,1)}, bf16[512,1024]{1,0:T(8,128)(2,1)S(1)}, u32[]{:S(2)}) copy-start(bf16[512,1024]{1,0:T(8,128)(2,1)S(1)} %get-tuple-element.199.refs_4_) | copy-start | bytes 3145732
  320.4 9.5 %copy-start.23 = (bf16[512,4096]{1,0:T(8,128)(2,1)}, bf16[512,4096]{1,0:T(8,128)(2,1)S(1)}, u32[]{:S(2)}) copy-start(bf16[512,4096]{1,0:T(8,128)(2,1)S(1)} %get-tuple-element.201.refs_5_) | copy-start | bytes 12582916
  337.2 6.2 collective-permute-start.1
  360.2 7.0 copy-start.14
  360.2 7.0 copy-start.40
  539.3 13.1 %copy-start.24 = (bf16[512,1024]{1,0:T(8,128)(2,1)}, bf16[512,1024]{1,0:T(8,128)(2,1)S(1)}, u32[]{:S(2)}) copy-start(bf16[512,1024]{1,0:T(8,128)(2,1)S(1)} %get-tuple-element.192.refs_5_) | copy-start | bytes 3145732
  540.6 11.8 %copy-start.41 = (f32[4,64,128]{2,1,0:T(8,128)S(1)}, f32[4,64,128]{2,1,0:T(8,128)}, u32[]{:S(2)}) copy-start(f32[4,64,128]{2,1,0:T(8,128)} %get-tuple-element.77) | copy-start | bytes 393220
  540.6 12.2 %copy-start.12 = (bf16[1,512,1024]{2,1,0:T(8,128)(2,1)S(1)}, bf16[1,512,1024]{2,1,0:T(8,128)(2,1)}, u32[]{:S(2)}) copy-start(bf16[1,512,1024]{2,1,0:T(8,128)(2,1)} %param.16) | copy-start | bytes 3145732
  540.6 12.2 %copy-start.48 = (f32[1,1024]{1,0:T(1,128)S(1)}, f32[1,1024]{1,0:T(1,128)}, u32[]{:S(2)}) copy-start(f32[1,1024]{1,0:T(1,128)} %get-tuple-element.215) | copy-start | bytes 12292
  540.6 12.2 %copy-start.49 = (f32[512]{0:T(512)S(1)}, f32[512]{0:T(512)}, u32[]{:S(2)}) copy-start(f32[512]{0:T(512)} %broadcast_multiply_fusion) | copy-start | bytes 6148
  694.2 4.2 copy-start.34
  697.5 4.4 copy-start.33
  698.4 4.4 copy-start.32
  (34 other events, 80.7 us)
